TPU v7x, 512 devices: a whole 4x8x8 slice. The times are simulated.
512 devices in a mesh: segment: 4 (over z_lo, core), expert: 16 (over z_hi, x), fsdp: 8 (over y).
Axes of the slice: x: 4, y: 8, z: 8 (z_hi: 4, z_lo: 2; z = z_hi * 2 + z_lo), core: 2. Of those that a mesh axis runs over, the one named last changes fastest.
Arguments:
- acts: bfloat16 [4, 2, 2048, 1024], P('segment', None, ('expert', 'fsdp')), may hold values from -6 to 6
- out_grad: bfloat16 [2, 2048, 1024], P(None, ('expert', 'fsdp')), may hold values from -6 to 6
- expert_ids: int32 [4, 2, 2048, 2], P('segment', None, ('expert', 'fsdp')), may hold values from 0 to 15, all different within a row; in each aligned block of 16 rows (0 to 15, 16 to 31, ..., all dimensions but the last counted through in order) at most 2 rows name the same one
- gates: bfloat16 [4, 2, 2048, 2], P('segment', None, ('expert', 'fsdp')), may hold values from 0.19921875 to 1
- w_gate: bfloat16 [4, 16, 1024, 2048], P('segment', 'expert', None, 'fsdp'), may hold values from -0.1875 to 0.1875
- w_up: bfloat16 [4, 16, 1024, 2048], P('segment', 'expert', None, 'fsdp'), may hold values from -0.1875 to 0.1875
- w_down: bfloat16 [4, 16, 2048, 1024], P('segment', 'expert', 'fsdp'), may hold values from -0.125 to 0.125
Outputs:
- act_grad: bfloat16 [4, 2, 2048, 1024], P('segment', None, ('expert', 'fsdp'))
- gate_grad: float32 [4, 2, 2048, 2], P('segment', None, ('expert', 'fsdp'))
- grad_w_gate: bfloat16 [4, 16, 1024, 2048], P('segment', 'expert', None, 'fsdp')
- grad_w_up: bfloat16 [4, 16, 1024, 2048], P('segment', 'expert', None, 'fsdp')
- grad_w_down: bfloat16 [4, 16, 2048, 1024], P('segment', 'expert', 'fsdp')
Inputs may be any that keep to these rules, and one draw needn't show every extreme that they name: `expert_ids`: each row names 2 different experts. Within the tokens of one device for one layer and micro-batch (aligned blocks of 16 rows) no expert is named by more than 2 tokens, and in some such block an expert is named by exactly 2.
All inputs are finite; a program needn't handle non-finite values.
Results may differ from a plain program's by a relative error of at most 0.035.
Values may be sent and summed in bfloat16 or wider, within the bound.
No kernel may reach another device: no remote copies, remote signals or barrier semaphores. Data moves between devices by JAX's collectives and lax.ppermute only.
A program may use at most 64 MiB of HBM per device.

v0:
```python
import jax
import jax.numpy as jnp
from jax import lax
from jax.sharding import PartitionSpec as P


def from_behind(value, axis, steps):
    count = lax.axis_size(axis)
    leading, last = (max(0, -steps), min(count, count - steps))
    return lax.ppermute(value, axis, [(source, source + steps) for source in range(leading, last)])


def silu_parts(pre_gate):
    sigmoid = jax.nn.sigmoid(pre_gate)
    return (pre_gate * sigmoid, sigmoid * (1.0 + pre_gate * (1.0 - sigmoid)))


def local(acts, out_grad, expert_ids, gates, w_gate, w_up, w_down):
    segments = lax.axis_size("segment")
    segment_now = lax.axis_index("segment")
    n_expert = lax.axis_size("expert")
    n_fsdp = lax.axis_size("fsdp")
    micro_count = acts.shape[1]
    tok_count = acts.shape[2]
    width = acts.shape[3]
    top_count = expert_ids.shape[3]
    capacity = 5 * top_count * tok_count // (4 * n_expert)
    w_first = w_gate[0, 0]
    w_third = w_up[0, 0]
    w_second = w_down[0, 0]
    hid_local = w_first.shape[1]
    expert_iota = jnp.arange(n_expert, dtype=jnp.int32)
    slot_iota = jnp.arange(capacity, dtype=jnp.int32)
    micro_iota = jnp.arange(micro_count, dtype=jnp.int32)
    contract_rows = (((0,), (0,)), ((), ()))
    contract_cols = (((1,), (1,)), ((), ()))
    grad_first = jnp.zeros((width, hid_local), jnp.float32)
    grad_third = jnp.zeros((width, hid_local), jnp.float32)
    grad_second = jnp.zeros((hid_local, width), jnp.float32)
    act_out = jnp.zeros(acts.shape, jnp.bfloat16)
    gate_out = jnp.zeros(gates.shape, jnp.float32)
    previous = jnp.zeros((tok_count, width), jnp.bfloat16)
    for moment in range(micro_count + segments - 1):
        micro_index = moment - (segments - 1 - segment_now)
        valid = (micro_index >= 0) & (micro_index < micro_count)
        picked = jnp.clip(micro_index, 0, micro_count - 1)
        tokens_now = lax.dynamic_index_in_dim(acts[0], picked, 0, keepdims=False)
        loss_grad = lax.dynamic_index_in_dim(out_grad, picked, 0, keepdims=False)
        ids_now = lax.dynamic_index_in_dim(expert_ids[0], picked, 0, keepdims=False)
        gates_now = lax.dynamic_index_in_dim(gates[0], picked, 0, keepdims=False)
        if moment > 0:
            incoming = from_behind(previous, "segment", -1)
        else:
            incoming = previous
        grad_now = jnp.where(segment_now == segments - 1, loss_grad, incoming)
        table = (ids_now[:, :, None] == expert_iota).astype(jnp.int32)
        counts = jnp.sum(table, axis=1)
        before = jnp.cumsum(counts, axis=0) - counts
        slots = jnp.sum(before[:, None, :] * table, axis=2)
        routing = (
            (ids_now[None, None] == expert_iota[:, None, None, None])
            & (slots[None, None] == slot_iota[None, :, None, None])
        ).astype(jnp.float32)
        placing = jnp.sum(routing, axis=3).astype(jnp.bfloat16)
        token_buf = jnp.einsum(
            "ect,td->ecd", placing, tokens_now, preferred_element_type=jnp.float32
        ).astype(jnp.bfloat16)
        grad_buf = jnp.einsum(
            "ect,td->ecd", placing, grad_now, preferred_element_type=jnp.float32
        ).astype(jnp.bfloat16)
        gate_buf = jnp.einsum("ectk,tk->ec", routing, gates_now.astype(jnp.float32)).astype(
            jnp.bfloat16
        )
        start_state = (
            grad_first,
            grad_third,
            grad_second,
            jnp.zeros((n_fsdp, n_expert, capacity, width), jnp.bfloat16),
            jnp.zeros((n_fsdp, n_expert, capacity), jnp.bfloat16),
        )
        grouped = (
            lax.all_gather(token_buf[None], "fsdp", axis=0, tiled=True),
            lax.all_gather(grad_buf[None], "fsdp", axis=0, tiled=True),
            lax.all_gather(gate_buf[None], "fsdp", axis=0, tiled=True),
        )
        token_rows = lax.all_to_all(grouped[0], "expert", split_axis=1, concat_axis=1, tiled=True)
        grad_rows = lax.all_to_all(grouped[1], "expert", split_axis=1, concat_axis=1, tiled=True)
        gate_rows = lax.all_to_all(grouped[2], "expert", split_axis=1, concat_axis=1, tiled=True)

        def compute(state):
            sum_first, sum_third, sum_second, part_rows, part_gates = state
            flat_tokens = token_rows.reshape(-1, width)
            flat_grads = grad_rows.reshape(-1, width)
            gate_col = gate_rows.reshape(-1).astype(jnp.float32)[:, None]
            pre_gate = jnp.dot(flat_tokens, w_first, preferred_element_type=jnp.float32)
            pre_up = jnp.dot(flat_tokens, w_third, preferred_element_type=jnp.float32)
            activated, slope_term = silu_parts(pre_gate)
            hidden = activated * pre_up
            back_hidden = lax.dot_general(
                flat_grads, w_second, contract_cols, preferred_element_type=jnp.float32
            )
            scaled = back_hidden * gate_col
            grad_gate_pre = (scaled * pre_up * slope_term).astype(jnp.bfloat16)
            grad_up_pre = (scaled * activated).astype(jnp.bfloat16)
            hidden_gated = (hidden * gate_col).astype(jnp.bfloat16)
            sum_first = sum_first + lax.dot_general(
                flat_tokens, grad_gate_pre, contract_rows, preferred_element_type=jnp.float32
            )
            sum_third = sum_third + lax.dot_general(
                flat_tokens, grad_up_pre, contract_rows, preferred_element_type=jnp.float32
            )
            sum_second = sum_second + lax.dot_general(
                hidden_gated, flat_grads, contract_rows, preferred_element_type=jnp.float32
            )
            partial_value = lax.dot_general(
                grad_gate_pre, w_first, contract_cols, preferred_element_type=jnp.float32
            )
            partial_value = partial_value + lax.dot_general(
                grad_up_pre, w_third, contract_cols, preferred_element_type=jnp.float32
            )
            gate_part = jnp.sum(hidden * back_hidden, axis=1)
            part_rows = partial_value.astype(jnp.bfloat16).reshape(token_rows.shape)
            part_gates = gate_part.astype(jnp.bfloat16).reshape(gate_rows.shape)
            return (sum_first, sum_third, sum_second, part_rows, part_gates)

        finished = lax.cond(valid, compute, lambda state: state, start_state)
        grad_first, grad_third, grad_second, part_rows, part_gates = finished
        summed_rows, summed_gates = (
            lax.psum_scatter(part_rows, "fsdp", scatter_dimension=0, tiled=True).astype(
                jnp.float32
            ),
            lax.psum_scatter(part_gates, "fsdp", scatter_dimension=0, tiled=True).astype(
                jnp.float32
            ),
        )
        back_rows, back_gates = (
            lax.all_to_all(
                summed_rows[0].astype(jnp.bfloat16),
                "expert",
                split_axis=0,
                concat_axis=0,
                tiled=True,
            ),
            lax.all_to_all(
                summed_gates[0].astype(jnp.bfloat16),
                "expert",
                split_axis=0,
                concat_axis=0,
                tiled=True,
            ),
        )
        token_back = jnp.einsum(
            "ect,ecd->td", placing, back_rows, preferred_element_type=jnp.float32
        )
        new_grad = (grad_now.astype(jnp.float32) + token_back).astype(jnp.bfloat16)
        gate_new = jnp.einsum("ectk,ec->tk", routing, back_gates.astype(jnp.float32))
        chosen = micro_iota == micro_index
        act_out = jnp.where(chosen[None, :, None, None], new_grad[None, None], act_out)
        gate_out = jnp.where(chosen[None, :, None, None], gate_new[None, None], gate_out)
        previous = new_grad
    return (
        act_out,
        gate_out,
        grad_first.astype(jnp.bfloat16)[None, None],
        grad_third.astype(jnp.bfloat16)[None, None],
        grad_second.astype(jnp.bfloat16)[None, None],
    )


def solution(mesh):
    in_specs = (
        P("segment", None, ("expert", "fsdp"), None),
        P(None, ("expert", "fsdp"), None),
        P("segment", None, ("expert", "fsdp"), None),
        P("segment", None, ("expert", "fsdp"), None),
        P("segment", "expert", None, "fsdp"),
        P("segment", "expert", None, "fsdp"),
        P("segment", "expert", "fsdp", None),
    )
    out_specs = (
        P("segment", None, ("expert", "fsdp"), None),
        P("segment", None, ("expert", "fsdp"), None),
        P("segment", "expert", None, "fsdp"),
        P("segment", "expert", None, "fsdp"),
        P("segment", "expert", "fsdp", None),
    )
    return jax.shard_map(local, mesh=mesh, in_specs=in_specs, out_specs=out_specs, check_vma=False)
```

profile of v0, /device:TPU:24, one launch (start us, length us, event | category | flops | bytes accessed | tf_op | source)
XLA Modules:
  0.0 1035.6 jit_solution(1967986809864867535)
XLA Ops:
  10.0 16.8 %all-gather.15 = bf16[8,16,2]{1,2,0:T(2,128)(2,1)S(1)} all-gather(bf16[1,16,2]{1,2,0:T(2,128)(2,1)S(1)} %convert_bitcast_fusion.7), channel_id=3, replica_groups=mesh['segment'=4,'expert'=16,'fsdp'=8] {'fsdp'}, dimensions={0}, use_global_device_ids=true | all-gather | bytes 576 | tf_op jit(solution)/shard_map/all_gather | solution.py:84
  27.4 11.0 %all-to-all-start.1 = ((bf16[8,16,2]{0,2,1:T(2,128)(2,1)}), bf16[8,16,2]{0,2,1:T(2,128)(2,1)S(1)}, u32[]{:S(2)}, u32[]{:S(2)}) async-start(bf16[8,16,2]{0,2,1:T(2,128)(2,1)} %copy.256), calls=%async_computation.1 | async-start | bytes 16384 | tf_op jit(solution)/shard_map/all_to_all | solution.py:88
  38.6 25.4 %all-gather = bf16[128,2,1024]{2,0,1:T(8,128)(2,1)S(1)} all-gather(bf16[16,2,1024]{2,0,1:T(8,128)(2,1)S(1)} %convolution_convert_fusion.9), channel_id=2, replica_groups=mesh['segment'=4,'expert'=16,'fsdp'=8] {'fsdp'}, dimensions={0}, use_global_device_ids=true | all-gather | bytes 589824 | tf_op jit(solution)/shard_map/all_gather | solution.py:83
  75.3 25.2 %all-gather.2 = bf16[128,2,1024]{2,0,1:T(8,128)(2,1)S(1)} all-gather(bf16[16,2,1024]{2,0,1:T(8,128)(2,1)S(1)} %convolution_convert_fusion.8), channel_id=4, replica_groups=mesh['segment'=4,'expert'=16,'fsdp'=8] {'fsdp'}, dimensions={0}, use_global_device_ids=true | all-gather | bytes 589824 | tf_op jit(solution)/shard_map/all_gather | solution.py:82
  112.8 11.7 %all-to-all-done.2 = bf16[8,16,2,1024]{3,2,0,1:T(2,128)(2,1)S(1)} async-done(((bf16[8,16,2,1024]{3,2,0,1:T(2,128)(2,1)}), bf16[8,16,2,1024]{3,2,0,1:T(2,128)(2,1)S(1)}, u32[]{:S(2)}, u32[]{:S(2)}) %all-to-all-start.2) | async-done | bytes 524320 | tf_op jit(solution)/shard_map/all_to_all | solution.py:86
  129.8 13.8 %all-gather.16 = bf16[8,16,2]{1,2,0:T(2,128)(2,1)S(1)} all-gather(bf16[1,16,2]{1,2,0:T(2,128)(2,1)S(1)} %convert_bitcast_fusion.6), channel_id=6, replica_groups=mesh['segment'=4,'expert'=16,'fsdp'=8] {'fsdp'}, dimensions={0}, use_global_device_ids=true | all-gather | bytes 576 | tf_op jit(solution)/shard_map/all_gather | solution.py:84
  149.5 13.9 %reduce-scatter.11.cloned.1.call-done = bf16[1,16,2,1024]{3,1,2,0:T(8,128)(2,1)} async-done(((bf16[8,16,2,1024]{3,1,2,0:T(8,128)(2,1)}), bf16[1,16,2,1024]{3,1,2,0:T(8,128)(2,1)}) %reduce-scatter.11.cloned.1.call-update) | async-done | bytes 65552 | tf_op jit(solution)/shard_map/reduce_scatter | solution.py:129
  175.5 25.5 %all-gather.5 = bf16[128,2,1024]{2,0,1:T(8,128)(2,1)S(1)} all-gather(bf16[16,2,1024]{2,0,1:T(8,128)(2,1)S(1)} %convolution_convert_fusion.6), channel_id=7, replica_groups=mesh['segment'=4,'expert'=16,'fsdp'=8] {'fsdp'}, dimensions={0}, use_global_device_ids=true | all-gather | bytes 589824 | tf_op jit(solution)/shard_map/all_gather | solution.py:82
  215.9 25.4 %all-gather.3 = bf16[128,2,1024]{2,0,1:T(8,128)(2,1)S(1)} all-gather(bf16[16,2,1024]{2,0,1:T(8,128)(2,1)S(1)} %convolution_convert_fusion.7), channel_id=5, replica_groups=mesh['segment'=4,'expert'=16,'fsdp'=8] {'fsdp'}, dimensions={0}, use_global_device_ids=true | all-gather | bytes 589824 | tf_op jit(solution)/shard_map/all_gather | solution.py:83
  252.5 15.3 %all-to-all-done.4 = bf16[8,16,2,1024]{3,2,0,1:T(2,128)(2,1)} async-done(((bf16[8,16,2,1024]{3,2,0,1:T(2,128)(2,1)}), bf16[8,16,2,1024]{3,2,0,1:T(2,128)(2,1)}, u32[]{:S(2)}, u32[]{:S(2)}) %all-to-all-start.4) | async-done | bytes 524320 | tf_op jit(solution)/shard_map/all_to_all | solution.py:87
  271.8 13.1 %all-gather.17 = bf16[8,16,2]{1,2,0:T(2,128)(2,1)S(1)} all-gather(bf16[1,16,2]{1,2,0:T(2,128)(2,1)S(1)} %convert_bitcast_fusion.5), channel_id=9, replica_groups=mesh['segment'=4,'expert'=16,'fsdp'=8] {'fsdp'}, dimensions={0}, use_global_device_ids=true | all-gather | bytes 576 | tf_op jit(solution)/shard_map/all_gather | solution.py:84
  291.0 36.2 %reduce-scatter.13.cloned.1.call-done = bf16[1,16,2,1024]{3,1,2,0:T(8,128)(2,1)} async-done(((bf16[8,16,2,1024]{3,1,2,0:T(8,128)(2,1)}), bf16[1,16,2,1024]{3,1,2,0:T(8,128)(2,1)}) %reduce-scatter.13.cloned.1.call-update) | async-done | bytes 65552 | tf_op jit(solution)/shard_map/reduce_scatter | solution.py:129
  339.3 25.5 %all-gather.8 = bf16[128,2,1024]{2,0,1:T(8,128)(2,1)S(1)} all-gather(bf16[16,2,1024]{2,0,1:T(8,128)(2,1)S(1)} %convolution_convert_fusion.4), channel_id=10, replica_groups=mesh['segment'=4,'expert'=16,'fsdp'=8] {'fsdp'}, dimensions={0}, use_global_device_ids=true | all-gather | bytes 589824 | tf_op jit(solution)/shard_map/all_gather | solution.py:82
  379.8 25.4 %all-gather.6 = bf16[128,2,1024]{2,0,1:T(8,128)(2,1)S(1)} all-gather(bf16[16,2,1024]{2,0,1:T(8,128)(2,1)S(1)} %convolution_convert_fusion.5), channel_id=8, replica_groups=mesh['segment'=4,'expert'=16,'fsdp'=8] {'fsdp'}, dimensions={0}, use_global_device_ids=true | all-gather | bytes 589824 | tf_op jit(solution)/shard_map/all_gather | solution.py:83
  418.8 12.9 %all-to-all-done.8 = bf16[8,16,2,1024]{3,2,0,1:T(2,128)(2,1)} async-done(((bf16[8,16,2,1024]{3,2,0,1:T(2,128)(2,1)}), bf16[8,16,2,1024]{3,2,0,1:T(2,128)(2,1)}, u32[]{:S(2)}, u32[]{:S(2)}) %all-to-all-start.8) | async-done | bytes 524320 | tf_op jit(solution)/shard_map/all_to_all | solution.py:87
  435.8 13.1 %all-gather.18 = bf16[8,16,2]{1,2,0:T(2,128)(2,1)S(1)} all-gather(bf16[1,16,2]{1,2,0:T(2,128)(2,1)S(1)} %convert_bitcast_fusion.4), channel_id=12, replica_groups=mesh['segment'=4,'expert'=16,'fsdp'=8] {'fsdp'}, dimensions={0}, use_global_device_ids=true | all-gather | bytes 576 | tf_op jit(solution)/shard_map/all_gather | solution.py:84
  455.0 36.1 %reduce-scatter.15.cloned.1.call-done = bf16[1,16,2,1024]{3,1,2,0:T(8,128)(2,1)} async-done(((bf16[8,16,2,1024]{3,1,2,0:T(8,128)(2,1)}), bf16[1,16,2,1024]{3,1,2,0:T(8,128)(2,1)}) %reduce-scatter.15.cloned.1.call-update) | async-done | bytes 65552 | tf_op jit(solution)/shard_map/reduce_scatter | solution.py:129
  503.1 25.5 %all-gather.11 = bf16[128,2,1024]{2,0,1:T(8,128)(2,1)S(1)} all-gather(bf16[16,2,1024]{2,0,1:T(8,128)(2,1)S(1)} %convolution_convert_fusion.2), channel_id=13, replica_groups=mesh['segment'=4,'expert'=16,'fsdp'=8] {'fsdp'}, dimensions={0}, use_global_device_ids=true | all-gather | bytes 589824 | tf_op jit(solution)/shard_map/all_gather | solution.py:82
  543.7 25.3 %all-gather.9 = bf16[128,2,1024]{2,0,1:T(8,128)(2,1)S(1)} all-gather(bf16[16,2,1024]{2,0,1:T(8,128)(2,1)S(1)} %convolution_convert_fusion.3), channel_id=11, replica_groups=mesh['segment'=4,'expert'=16,'fsdp'=8] {'fsdp'}, dimensions={0}, use_global_device_ids=true | all-gather | bytes 589824 | tf_op jit(solution)/shard_map/all_gather | solution.py:83
  580.3 15.3 %all-to-all-done.12 = bf16[8,16,2,1024]{3,2,0,1:T(2,128)(2,1)} async-done(((bf16[8,16,2,1024]{3,2,0,1:T(2,128)(2,1)}), bf16[8,16,2,1024]{3,2,0,1:T(2,128)(2,1)}, u32[]{:S(2)}, u32[]{:S(2)}) %all-to-all-start.12) | async-done | bytes 524320 | tf_op jit(solution)/shard_map/all_to_all | solution.py:87
  595.6 23.9 %conditional.8 = (f32[1024,256]{0,1:T(8,128)S(1)}, f32[1024,256]{0,1:T(8,128)S(1)}, f32[256,1024]{1,0:T(8,128)}, bf16[8,16,2,1024]{3,2,1,0:T(2,128)(2,1)S(1)}, bf16[8,16,2]{2,1,0:T(8,128)(2,1)}) conditional(s32[]{:T(128)} %convert_element_type.418, (f32[1024,256]{0,1:T(8,128)S(1)}, f32[1024,256]{0,1:T(8,128)S(1)}, ...), branch_computations={%region_28.29_spmd, %region_29.31_spmd} | conditional | flops 1076625152 | bytes 30152912 | solution.py:126
  622.7 13.1 %all-gather.19 = bf16[8,16,2]{1,2,0:T(2,128)(2,1)S(1)} all-gather(bf16[1,16,2]{1,2,0:T(2,128)(2,1)S(1)} %convert_bitcast_fusion.3), channel_id=15, replica_groups=mesh['segment'=4,'expert'=16,'fsdp'=8] {'fsdp'}, dimensions={0}, use_global_device_ids=true | all-gather | bytes 576 | tf_op jit(solution)/shard_map/all_gather | solution.py:84
  641.9 13.2 %reduce-scatter.17.cloned.1.call-done = bf16[1,16,2,1024]{3,1,2,0:T(8,128)(2,1)} async-done(((bf16[8,16,2,1024]{3,1,2,0:T(8,128)(2,1)}), bf16[1,16,2,1024]{3,1,2,0:T(8,128)(2,1)}) %reduce-scatter.17.cloned.1.call-update) | async-done | bytes 65552 | tf_op jit(solution)/shard_map/reduce_scatter | solution.py:129
  667.2 25.6 %all-gather.14 = bf16[128,2,1024]{2,0,1:T(8,128)(2,1)S(1)} all-gather(bf16[16,2,1024]{2,0,1:T(8,128)(2,1)S(1)} %convolution_convert_fusion), channel_id=16, replica_groups=mesh['segment'=4,'expert'=16,'fsdp'=8] {'fsdp'}, dimensions={0}, use_global_device_ids=true | all-gather | bytes 589824 | tf_op jit(solution)/shard_map/all_gather | solution.py:82
  705.4 39.8 %reduce-scatter.29.cloned.1.call-done = bf16[1,16,2]{2,1,0:T(8,128)(2,1)} async-done(((bf16[8,16,2]{2,1,0:T(8,128)(2,1)}), bf16[1,16,2]{2,1,0:T(8,128)(2,1)}) %reduce-scatter.29.cloned.1.call-update) | async-done | bytes 80 | tf_op jit(solution)/shard_map/reduce_scatter | solution.py:132
  747.1 27.3 %all-gather.12 = bf16[128,2,1024]{2,0,1:T(8,128)(2,1)} all-gather(bf16[16,2,1024]{2,0,1:T(8,128)(2,1)S(1)} %convolution_convert_fusion.1), channel_id=14, replica_groups=mesh['segment'=4,'expert'=16,'fsdp'=8] {'fsdp'}, dimensions={0}, use_global_device_ids=true | all-gather | bytes 589824 | tf_op jit(solution)/shard_map/all_gather | solution.py:83
  801.7 38.4 %reduce-scatter.27.cloned.1.call-done = bf16[1,16,2]{2,1,0:T(8,128)(2,1)} async-done(((bf16[8,16,2]{2,1,0:T(8,128)(2,1)}), bf16[1,16,2]{2,1,0:T(8,128)(2,1)}) %reduce-scatter.27.cloned.1.call-update) | async-done | bytes 80 | tf_op jit(solution)/shard_map/reduce_scatter | solution.py:132
  841.4 10.1 all-to-all-start.23
  851.5 21.6 %conditional.9 = (f32[1024,256]{0,1:T(8,128)S(1)}, f32[1024,256]{0,1:T(8,128)S(1)}, f32[256,1024]{1,0:T(8,128)}, bf16[8,16,2,1024]{3,2,1,0:T(2,128)(2,1)S(1)}, bf16[8,16,2]{2,1,0:T(8,128)(2,1)}) conditional(s32[]{:T(128)} %convert_element_type.428, (f32[1024,256]{0,1:T(8,128)S(1)}, f32[1024,256]{0,1:T(8,128)S(1)}, ...), branch_computations={%region_36.37_spmd, %region_37.39_spmd} | conditional | flops 1076625152 | bytes 32250092 | solution.py:126
  902.5 19.8 %reduce-scatter.23.cloned.1.call-done = bf16[1,16,2]{2,1,0:T(8,128)(2,1)} async-done(((bf16[8,16,2]{2,1,0:T(8,128)(2,1)}), bf16[1,16,2]{2,1,0:T(8,128)(2,1)}) %reduce-scatter.23.cloned.1.call-update) | async-done | bytes 80 | tf_op jit(solution)/shard_map/reduce_scatter | solution.py:132
  947.6 16.4 %reduce-scatter.21.cloned.1.call-done = bf16[1,16,2]{2,1,0:T(8,128)(2,1)} async-done(((bf16[8,16,2]{2,1,0:T(8,128)(2,1)}), bf16[1,16,2]{2,1,0:T(8,128)(2,1)}) %reduce-scatter.21.cloned.1.call-update) | async-done | bytes 80 | tf_op jit(solution)/shard_map/reduce_scatter | solution.py:132
  986.1 19.7 %reduce-scatter.19.cloned.1.call-done = bf16[1,16,2,1024]{3,1,2,0:T(8,128)(2,1)} async-done(((bf16[8,16,2,1024]{3,1,2,0:T(8,128)(2,1)}), bf16[1,16,2,1024]{3,1,2,0:T(8,128)(2,1)}) %reduce-scatter.19.cloned.1.call-update) | async-done | bytes 65552 | tf_op jit(solution)/shard_map/reduce_scatter | solution.py:129
  (395 shorter events, 388.1 us)
Async XLA Ops:
  27.4 37.9 %all-to-all-start.1 = ((bf16[8,16,2]{0,2,1:T(2,128)(2,1)}), bf16[8,16,2]{0,2,1:T(2,128)(2,1)S(1)}, u32[]{:S(2)}, u32[]{:S(2)}) async-start(bf16[8,16,2]{0,2,1:T(2,128)(2,1)} %copy.256), calls=%async_computation.1 | async-start | bytes 16384 | tf_op jit(solution)/shard_map/all_to_all | solution.py:88
  65.3 36.6 %all-to-all-start = ((bf16[8,16,2,1024]{3,2,0,1:T(2,128)(2,1)}), bf16[8,16,2,1024]{3,2,0,1:T(2,128)(2,1)S(1)}, u32[]{:S(2)}, u32[]{:S(2)}) async-start(bf16[8,16,2,1024]{3,2,0,1:T(2,128)(2,1)} %copy.255), calls=%async_computation | async-start | bytes 1048576 | tf_op jit(solution)/shard_map/all_to_all | solution.py:87
  101.9 22.5 %all-to-all-start.2 = ((bf16[8,16,2,1024]{3,2,0,1:T(2,128)(2,1)}), bf16[8,16,2,1024]{3,2,0,1:T(2,128)(2,1)S(1)}, u32[]{:S(2)}, u32[]{:S(2)}) async-start(bf16[8,16,2,1024]{3,2,0,1:T(2,128)(2,1)} %copy.257), calls=%async_computation.2 | async-start | bytes 1048576 | tf_op jit(solution)/shard_map/all_to_all | solution.py:86
  111.7 51.7 %reduce-scatter.11.cloned.1.call-start = ((), (), s32[]{:S(2)}) async-start(), calls=%async_computation.35 | async-start | bytes 589824 | tf_op jit(solution)/shard_map/reduce_scatter | solution.py:129
  144.3 20.6 %all-to-all-start.5 = ((bf16[8,16,2]{0,2,1:T(2,128)(2,1)}), bf16[8,16,2]{0,2,1:T(2,128)(2,1)S(1)}, u32[]{:S(2)}, u32[]{:S(2)}) async-start(bf16[8,16,2]{0,2,1:T(2,128)(2,1)} %copy.266), calls=%async_computation.6 | async-start | bytes 16384 | tf_op jit(solution)/shard_map/all_to_all | solution.py:88
  165.5 36.8 %all-to-all-start.3 = ((bf16[16,2,1024]{2,1,0:T(2,128)(2,1)}), bf16[16,2,1024]{2,1,0:T(2,128)(2,1)S(1)}, u32[]{:S(2)}, u32[]{:S(2)}) async-start(bf16[16,2,1024]{2,1,0:T(2,128)(2,1)} %copy.262), calls=%async_computation.4 | async-start | bytes 131072 | tf_op jit(solution)/shard_map/all_to_all | solution.py:137
  202.3 40.3 %all-to-all-start.6 = ((bf16[8,16,2,1024]{3,2,0,1:T(2,128)(2,1)}), bf16[8,16,2,1024]{3,2,0,1:T(2,128)(2,1)}, u32[]{:S(2)}, u32[]{:S(2)}) async-start(bf16[8,16,2,1024]{3,2,0,1:T(2,128)(2,1)} %copy.267), calls=%async_computation.7 | async-start | bytes 1048576 | tf_op jit(solution)/shard_map/all_to_all | solution.py:86
  242.6 25.1 %all-to-all-start.4 = ((bf16[8,16,2,1024]{3,2,0,1:T(2,128)(2,1)}), bf16[8,16,2,1024]{3,2,0,1:T(2,128)(2,1)}, u32[]{:S(2)}, u32[]{:S(2)}) async-start(bf16[8,16,2,1024]{3,2,0,1:T(2,128)(2,1)} %copy.265), calls=%async_computation.5 | async-start | bytes 1048576 | tf_op jit(solution)/shard_map/all_to_all | solution.py:87
  252.4 74.8 %reduce-scatter.13.cloned.1.call-start = ((), (), s32[]{:S(2)}) async-start(), calls=%async_computation.36 | async-start | bytes 589824 | tf_op jit(solution)/shard_map/reduce_scatter | solution.py:129
  285.5 43.2 %all-to-all-start.9 = ((bf16[8,16,2]{0,2,1:T(2,128)(2,1)}), bf16[8,16,2]{0,2,1:T(2,128)(2,1)S(1)}, u32[]{:S(2)}, u32[]{:S(2)}) async-start(bf16[8,16,2]{0,2,1:T(2,128)(2,1)} %copy.276), calls=%async_computation.11 | async-start | bytes 16384 | tf_op jit(solution)/shard_map/all_to_all | solution.py:88
  329.3 36.8 %all-to-all-start.7 = ((bf16[16,2,1024]{2,1,0:T(2,128)(2,1)}), bf16[16,2,1024]{2,1,0:T(2,128)(2,1)S(1)}, u32[]{:S(2)}, u32[]{:S(2)}) async-start(bf16[16,2,1024]{2,1,0:T(2,128)(2,1)} %copy.272), calls=%async_computation.9 | async-start | bytes 131072 | tf_op jit(solution)/shard_map/all_to_all | solution.py:137
  366.1 40.4 %all-to-all-start.10 = ((bf16[8,16,2,1024]{3,2,0,1:T(2,128)(2,1)}), bf16[8,16,2,1024]{3,2,0,1:T(2,128)(2,1)}, u32[]{:S(2)}, u32[]{:S(2)}) async-start(bf16[8,16,2,1024]{3,2,0,1:T(2,128)(2,1)} %copy.277), calls=%async_computation.12 | async-start | bytes 1048576 | tf_op jit(solution)/shard_map/all_to_all | solution.py:86
  406.5 25.1 %all-to-all-start.8 = ((bf16[8,16,2,1024]{3,2,0,1:T(2,128)(2,1)}), bf16[8,16,2,1024]{3,2,0,1:T(2,128)(2,1)}, u32[]{:S(2)}, u32[]{:S(2)}) async-start(bf16[8,16,2,1024]{3,2,0,1:T(2,128)(2,1)} %copy.275), calls=%async_computation.10 | async-start | bytes 1048576 | tf_op jit(solution)/shard_map/all_to_all | solution.py:87
  416.3 74.8 %reduce-scatter.15.cloned.1.call-start = ((), (), s32[]{:S(2)}) async-start(), calls=%async_computation.37 | async-start | bytes 589824 | tf_op jit(solution)/shard_map/reduce_scatter | solution.py:129
  449.6 43.1 %all-to-all-start.13 = ((bf16[8,16,2]{0,2,1:T(2,128)(2,1)}), bf16[8,16,2]{0,2,1:T(2,128)(2,1)S(1)}, u32[]{:S(2)}, u32[]{:S(2)}) async-start(bf16[8,16,2]{0,2,1:T(2,128)(2,1)} %copy.286), calls=%async_computation.16 | async-start | bytes 16384 | tf_op jit(solution)/shard_map/all_to_all | solution.py:88
  493.3 36.7 %all-to-all-start.11 = ((bf16[16,2,1024]{2,1,0:T(2,128)(2,1)}), bf16[16,2,1024]{2,1,0:T(2,128)(2,1)S(1)}, u32[]{:S(2)}, u32[]{:S(2)}) async-start(bf16[16,2,1024]{2,1,0:T(2,128)(2,1)} %copy.282), calls=%async_computation.14 | async-start | bytes 131072 | tf_op jit(solution)/shard_map/all_to_all | solution.py:137
  530.0 40.3 %all-to-all-start.14 = ((bf16[8,16,2,1024]{3,2,0,1:T(2,128)(2,1)}), bf16[8,16,2,1024]{3,2,0,1:T(2,128)(2,1)}, u32[]{:S(2)}, u32[]{:S(2)}) async-start(bf16[8,16,2,1024]{3,2,0,1:T(2,128)(2,1)} %copy.287), calls=%async_computation.17 | async-start | bytes 1048576 | tf_op jit(solution)/shard_map/all_to_all | solution.py:86
  570.3 25.3 %all-to-all-start.12 = ((bf16[8,16,2,1024]{3,2,0,1:T(2,128)(2,1)}), bf16[8,16,2,1024]{3,2,0,1:T(2,128)(2,1)}, u32[]{:S(2)}, u32[]{:S(2)}) async-start(bf16[8,16,2,1024]{3,2,0,1:T(2,128)(2,1)} %copy.285), calls=%async_computation.15 | async-start | bytes 1048576 | tf_op jit(solution)/shard_map/all_to_all | solution.py:87
  580.2 74.9 %reduce-scatter.17.cloned.1.call-start = ((), (), s32[]{:S(2)}) async-start(), calls=%async_computation.38 | async-start | bytes 589824 | tf_op jit(solution)/shard_map/reduce_scatter | solution.py:129
  636.4 20.2 %all-to-all-start.17 = ((bf16[8,16,2]{0,2,1:T(2,128)(2,1)}), bf16[8,16,2]{0,2,1:T(2,128)(2,1)S(1)}, u32[]{:S(2)}, u32[]{:S(2)}) async-start(bf16[8,16,2]{0,2,1:T(2,128)(2,1)} %copy.296), calls=%async_computation.21 | async-start | bytes 16384 | tf_op jit(solution)/shard_map/all_to_all | solution.py:88
  657.3 36.8 %all-to-all-start.15 = ((bf16[16,2,1024]{2,1,0:T(2,128)(2,1)}), bf16[16,2,1024]{2,1,0:T(2,128)(2,1)S(1)}, u32[]{:S(2)}, u32[]{:S(2)}) async-start(bf16[16,2,1024]{2,1,0:T(2,128)(2,1)} %copy.292), calls=%async_computation.19 | async-start | bytes 131072 | tf_op jit(solution)/shard_map/all_to_all | solution.py:137
  694.1 80.3 %all-to-all-start.18 = ((bf16[8,16,2,1024]{3,2,0,1:T(2,128)(2,1)}), bf16[8,16,2,1024]{3,2,0,1:T(2,128)(2,1)}, u32[]{:S(2)}, u32[]{:S(2)}) async-start(bf16[8,16,2,1024]{3,2,0,1:T(2,128)(2,1)} %copy.297), calls=%async_computation.22 | async-start | bytes 1048576 | tf_op jit(solution)/shard_map/all_to_all | solution.py:86
  703.9 41.3 %reduce-scatter.29.cloned.1.call-start = ((), (), s32[]{:S(2)}) async-start(), calls=%async_computation.44 | async-start | bytes 36864 | tf_op jit(solution)/shard_map/reduce_scatter | solution.py:132
  704.1 42.4 %collective-permute-start.3 = (bf16[16,1024]{1,0:T(8,128)(2,1)S(1)}, bf16[16,1024]{1,0:T(8,128)(2,1)S(1)}, u32[]{:S(2)}, u32[]{:S(2)}) collective-permute-start(bf16[16,1024]{1,0:T(8,128)(2,1)S(1)} %add_convert_fusion.1), channel_id=1, source_target_pairs={{128,0},{256,128},{384,256},{129,1},{257,129},{385,257},{130,2},{2... | collective-permute-start | bytes 98312 | tf_op jit(solution)/shard_map/ppermute | solution.py:10
  794.2 47.2 %all-to-all-start.16 = ((bf16[8,16,2,1024]{3,2,0,1:T(2,128)(2,1)}), bf16[8,16,2,1024]{3,2,0,1:T(2,128)(2,1)}, u32[]{:S(2)}, u32[]{:S(2)}) async-start(bf16[8,16,2,1024]{3,2,0,1:T(2,128)(2,1)} %copy.295), calls=%async_computation.20 | async-start | bytes 1048576 | tf_op jit(solution)/shard_map/all_to_all | solution.py:87
  798.5 41.6 %reduce-scatter.27.cloned.1.call-start = ((), (), s32[]{:S(2)}) async-start(), calls=%async_computation.43 | async-start | bytes 36864 | tf_op jit(solution)/shard_map/reduce_scatter | solution.py:132
  799.0 82.1 %reduce-scatter.25.cloned.1.call-start = ((), (), s32[]{:S(2)}) async-start(), calls=%async_computation.42 | async-start | bytes 36864 | tf_op jit(solution)/shard_map/reduce_scatter | solution.py:132
  799.8 122.5 %reduce-scatter.23.cloned.1.call-start = ((), (), s32[]{:S(2)}) async-start(), calls=%async_computation.41 | async-start | bytes 36864 | tf_op jit(solution)/shard_map/reduce_scatter | solution.py:132
  841.4 32.6 %all-to-all-start.23 = ((bf16[16,1,2]{2,1,0:T(2,128)(2,1)}), bf16[16,1,2]{2,1,0:T(2,128)(2,1)}, u32[]{:S(2)}, u32[]{:S(2)}) async-start(bf16[16,1,2]{2,1,0:T(2,128)(2,1)} %copy.315), calls=%async_computation.32 | async-start | bytes 16384 | tf_op jit(solution)/shard_map/all_to_all | solution.py:144
  851.5 112.5 %reduce-scatter.21.cloned.1.call-start = ((), (), s32[]{:S(2)}) async-start(), calls=%async_computation.40 | async-start | bytes 36864 | tf_op jit(solution)/shard_map/reduce_scatter | solution.py:132
  892.5 113.3 %reduce-scatter.19.cloned.1.call-start = ((), (), s32[]{:S(2)}) async-start(), calls=%async_computation.39 | async-start | bytes 589824 | tf_op jit(solution)/shard_map/reduce_scatter | solution.py:129
  1007.3 20.0 %all-to-all-start.19 = ((bf16[16,2,1024]{2,1,0:T(2,128)(2,1)}), bf16[16,2,1024]{2,1,0:T(2,128)(2,1)S(1)}, u32[]{:S(2)}, u32[]{:S(2)}) async-start(bf16[16,2,1024]{2,1,0:T(2,128)(2,1)} %copy.302), calls=%async_computation.24 | async-start | bytes 131072 | tf_op jit(solution)/shard_map/all_to_all | solution.py:137
  (92 other events, 938.4 us)
Sparse Core Ops, SparseCore 0:
  127.7 35.5 reduce-scatter.10
  269.8 57.2 reduce-scatter.12
  433.8 57.2 reduce-scatter.14
  620.6 34.4 reduce-scatter.16
  707.2 37.9 reduce-scatter.28
  801.7 38.3 reduce-scatter.26
  842.9 38.2 reduce-scatter.24
  883.9 38.3 reduce-scatter.22
  925.7 38.2 reduce-scatter.20
  966.6 39.0 reduce-scatter.18
where the time goes:
time: 1050 us; the launch traced here: 1040 us
  waiting for transfers between devices  344 us (33%)
  blocking collectives  326 us (31%)
  starting transfers between devices  229 us (22%)
  local copies, waits for them, and re-layouts  89.5 us (9%)
  matrix products  23.3 us (2%)
  between operations  15.6 us (1%)
    all_gather x5, blocking collectives, local(): lax.all_gather(grad_buf[None], 'fsdp', axis=0, tiled=True)  129 us
    all_gather x5, blocking collectives, local(): lax.all_gather(token_buf[None], 'fsdp', axis=0, tiled=True)  127 us
    reduce_scatter x5, waiting for transfers between devices, local(): lax.psum_scatter(part_gates, 'fsdp', scatter_dimension=0, tiled=True)  121 us
    reduce_scatter x5, waiting for transfers between devices, local(): lax.psum_scatter(part_rows, 'fsdp', scatter_dimension=0, tiled=True)  119 us
    all_gather x5, blocking collectives, local(): lax.all_gather(gate_buf[None], 'fsdp', axis=0, tiled=True)  69.7 us
    all_to_all x5, starting transfers between devices, local(): lax.all_to_all(summed_gates[0].astype(jnp.bfloat16), 'expert', split_axis...  50 us
    all_to_all x5, starting transfers between devices, local(): lax.all_to_all(summed_rows[0].astype(jnp.bfloat16), 'expert', split_axis=...  49.6 us
    all_to_all x5, starting transfers between devices, local(): lax.all_to_all(grouped[0], 'expert', split_axis=1, concat_axis=1, tiled=T...  48.8 us
  transfers between devices with their start and end apart: 39, of which 22 were waited for; matrix products, arithmetic and copies ran while one was open for 6% of the time, Pallas kernels for 0%

commit v1 on v0

v1 whole, which is shorter than its diff:
```python
import jax
import jax.numpy as jnp
from jax import lax
from jax.experimental import pallas as pl
from jax.experimental.pallas import tpu as pltpu
from jax.sharding import PartitionSpec as P

BF = jnp.bfloat16
F32 = jnp.float32
NN = (((1,), (0,)), ((), ()))
NT = (((1,), (1,)), ((), ()))
TN = (((0,), (0,)), ((), ()))
LANES = 128
ROUTE = ("expert", "fsdp")


def dot(a, b, dims):
    return lax.dot_general(a, b, dims, preferred_element_type=F32)


def iota(shape, dim):
    return lax.broadcasted_iota(jnp.int32, shape, dim)


def call(body, outs, *args):
    return pl.pallas_call(
        body,
        out_shape=[jax.ShapeDtypeStruct(s, d) for s, d in outs],
        in_specs=[pl.BlockSpec(memory_space=pltpu.VMEM)] * len(args),
        out_specs=[pl.BlockSpec(memory_space=pltpu.VMEM)] * len(outs),
        compiler_params=pltpu.CompilerParams(vmem_limit_bytes=48 * 1024 * 1024),
    )(*args)


def upper(rows, cols):
    return (iota((rows, cols), 0) % 8) >= 4


def place(routing, tokens):
    half = tokens.shape[1] // 2
    spread = dot(routing, tokens, TN)
    rows = spread.shape[0]
    return jnp.where(upper(rows, half), spread[:, half:], spread[:, :half]).astype(BF)


def prep_body(micro, tok, cap, n_expert, n_fsdp, ids_ref, gates_ref, x_ref, send_ref, put_ref, get_ref, getz_ref):
    rows = micro * tok
    ids = ids_ref[...]
    gates = gates_ref[...]
    first, second = ids[:, 0:1], ids[:, 1:2]
    experts = iota((rows, LANES), 1)
    one, two = experts == first, experts == second
    counts = (one | two).astype(BF)
    r0, r1 = iota((rows, rows), 0), iota((rows, rows), 1)
    lower = ((r1 < r0) & (r1 // tok == r0 // tok)).astype(BF)
    before = dot(lower, counts, NN)
    place_of = iota((rows, 1), 0) // tok * cap
    slot_one = jnp.sum(jnp.where(one, before, 0.0), axis=1, keepdims=True).astype(jnp.int32) + place_of
    slot_two = jnp.sum(jnp.where(two, before, 0.0), axis=1, keepdims=True).astype(jnp.int32) + place_of
    cols = 8 * n_expert
    col = iota((rows, cols), 1)
    put_one = ((col // 8 == first) & (col % 4 == slot_one)).astype(F32)
    put_two = ((col // 8 == second) & (col % 4 == slot_two)).astype(F32)
    put = (put_one + put_two).astype(BF)
    put_ref[...] = put
    put_gates = (put_one * gates[:, 0:1] + put_two * gates[:, 1:2]).astype(BF)
    gate_cols = dot(put_gates, jnp.ones((rows, LANES), BF), TN).astype(BF)
    spread = jnp.concatenate([place(put, x_ref[...]), gate_cols], axis=1)
    width = spread.shape[1]
    send_ref[...] = jnp.broadcast_to(spread.reshape(n_expert, 1, 8, width), (n_expert, n_fsdp, 8, width))
    total = 8 * n_expert * n_fsdp
    wide = iota((rows, total), 1)
    target = wide // (8 * n_fsdp)
    row = wide % 4
    low = (wide % 8) < 4
    hit_one = (target == first) & (row == slot_one)
    hit_two = (target == second) & (row == slot_two)
    hit = hit_one | hit_two
    get_ref[:rows] = jnp.where(hit & low, 1.0, 0.0).astype(BF)
    get_ref[rows:] = jnp.where(hit & ~low, 1.0, 0.0).astype(BF)
    getz_ref[:rows] = jnp.where(hit_one & low, 1.0, 0.0).astype(BF)
    getz_ref[rows:] = jnp.where(hit_two & low, 1.0, 0.0).astype(BF)


def place_body(n_expert, n_fsdp, put_ref, g_ref, send_ref):
    spread = place(put_ref[...], g_ref[...])
    width = spread.shape[1]
    send_ref[...] = jnp.broadcast_to(spread.reshape(n_expert, 1, 8, width), (n_expert, n_fsdp, 8, width))


def join(mine, other, mask):
    value = jnp.where(mask, other, mine)
    rows, cols = value.shape
    turned = pltpu.roll(value.reshape(rows // 8, 8, cols), 4, 1).reshape(rows, cols)
    return value + turned


CHUNK = 256


def forward_body(rows_ref, wg_ref, wu_ref, slope_ref, act_ref, hid_ref, hg_ref):
    total = rows_ref.shape[0]
    half = wg_ref.shape[0] // 2

    def step(i, carry):
        at = pl.ds(pl.multiple_of(i * CHUNK, CHUNK), CHUNK)
        x = rows_ref[at, :half]
        c = rows_ref[at, half:].astype(F32)
        c = jnp.concatenate([c] * (wg_ref.shape[1] // LANES), axis=1)
        mask = upper(CHUNK, wg_ref.shape[1])
        a = join(dot(x, wg_ref[:half, :], NN), dot(x, wg_ref[half:, :], NN), mask)
        b = join(dot(x, wu_ref[:half, :], NN), dot(x, wu_ref[half:, :], NN), mask)
        sig = jax.nn.sigmoid(a)
        s = a * sig
        slope_ref[at, :] = c * (b * (sig * (1.0 + a * (1.0 - sig))))
        act_ref[at, :] = c * s
        h = s * b
        hid_ref[at, :] = h
        hg_ref[at, :] = (c * h).astype(BF)
        return carry

    lax.fori_loop(0, total // CHUNK, step, 0)


def back_body(rows_ref, wd_ref, wg_ref, wu_ref, slope_ref, act_ref, hid_ref, out_ref, da_ref, db_ref):
    total = rows_ref.shape[0]
    half = wg_ref.shape[0] // 2

    def step(i, carry):
        at = pl.ds(pl.multiple_of(i * CHUNK, CHUNK), CHUNK)
        g = rows_ref[at, :]
        mask = upper(CHUNK, wd_ref.shape[0])
        q = join(dot(g, wd_ref[:, :half], NT), dot(g, wd_ref[:, half:], NT), mask)
        da = (q * slope_ref[at, :]).astype(BF)
        db = (q * act_ref[at, :]).astype(BF)
        da_ref[at, :] = da
        db_ref[at, :] = db
        low = dot(da, wg_ref[:half, :], NT) + dot(db, wu_ref[:half, :], NT)
        high = dot(da, wg_ref[half:, :], NT) + dot(db, wu_ref[half:, :], NT)
        out_ref[at, :half] = jnp.where(upper(CHUNK, half), high, low).astype(BF)
        z = jnp.sum(q * hid_ref[at, :], axis=1, keepdims=True)
        out_ref[at, half:] = jnp.broadcast_to(z, (CHUNK, LANES)).astype(BF)
        return carry

    lax.fori_loop(0, total // CHUNK, step, 0)


def merge_body(get_ref, getz_ref, back_ref, g_ref, new_ref, gate_ref):
    tokens, width = g_ref.shape
    half = width // 2
    summed = dot(get_ref[...], back_ref[:, :half], NN)
    g = g_ref[...].astype(F32)
    new_ref[:, :half] = (g[:, :half] + summed[:tokens]).astype(BF)
    new_ref[:, half:] = (g[:, half:] + summed[tokens:]).astype(BF)
    gate_ref[...] = dot(getz_ref[...], back_ref[:, half:], NN)


def local(acts, out_grad, expert_ids, gates, w_gate, w_up, w_down):
    segments = lax.axis_size("segment")
    segment = lax.axis_index("segment")
    n_expert = lax.axis_size("expert")
    n_fsdp = lax.axis_size("fsdp")
    _, micro, tok, width = acts.shape
    top = expert_ids.shape[3]
    cap = top * tok // n_expert
    tokens = micro * tok
    half = width // 2
    wide = half + LANES
    wg, wu, wd = w_gate[0, 0], w_up[0, 0], w_down[0, 0]
    hid = wg.shape[1]
    total = 8 * n_expert * n_fsdp
    sources = n_expert * n_fsdp

    def exchange(value):
        cols = value.shape[-1]
        moved = lax.all_to_all(value.reshape(sources, 8, cols), ROUTE, 0, 0, tiled=True)
        return moved.reshape(total, cols)

    send, put, get, getz = call(
        lambda *r: prep_body(micro, tok, cap, n_expert, n_fsdp, *r),
        [((n_expert, n_fsdp, 8, wide), BF), ((tokens, 8 * n_expert), BF), ((2 * tokens, total), BF), ((top * tokens, total), BF)],
        expert_ids.reshape(tokens, top),
        gates.reshape(tokens, top).astype(F32),
        acts.reshape(tokens, width),
    )
    x_rows = exchange(send)
    slope, act, hidden, hg = call(
        forward_body,
        [((total, hid), F32), ((total, hid), F32), ((total, hid), F32), ((total, hid), BF)],
        x_rows, wg, wu,
    )

    def run(grad):
        (send_g,) = call(
            lambda *r: place_body(n_expert, n_fsdp, *r), [((n_expert, n_fsdp, 8, half), BF)], put, grad
        )
        g_rows = exchange(send_g)
        out, da, db = call(
            back_body,
            [((total, wide), BF), ((total, hid), BF), ((total, hid), BF)],
            g_rows, wd, wg, wu, slope, act, hidden,
        )
        back = exchange(out)
        new, gate_new = call(
            merge_body, [((tokens, width), BF), ((top * tokens, LANES), F32)], get, getz, back, grad
        )
        return new, gate_new, g_rows, da, db

    state = (
        jnp.zeros((tokens, width), BF),
        jnp.zeros((top * tokens, LANES), F32),
        jnp.zeros((total, half), BF),
        jnp.zeros((total, hid), BF),
        jnp.zeros((total, hid), BF),
    )
    grad = out_grad.reshape(tokens, width)
    for layer in reversed(range(segments)):
        state = lax.cond(segment == layer, lambda g, s: tuple(run(g)), lambda g, s: s, grad, state)
        if layer > 0:
            grad = lax.ppermute(state[0], "segment", [(layer, layer - 1)])
    new, gate_new, g_rows, da, db = state

    lower = (iota((total, hid), 0) % 8) < 4
    zero = jnp.zeros((), BF)

    def halves(value):
        return jnp.concatenate([jnp.where(lower, value, zero), jnp.where(lower, zero, value)], axis=1)

    def outer(value):
        both = dot(x_rows[:, :half], halves(value), TN)
        return jnp.concatenate([both[:, :hid], both[:, hid:]], axis=0).astype(BF)[None, None]

    grad_gate = outer(da)
    grad_up = outer(db)
    both = dot(halves(hg), g_rows, TN)
    grad_down = jnp.concatenate([both[:hid], both[hid:]], axis=1).astype(BF)[None, None]
    gate_out = gate_new[:, 0].reshape(top, micro, tok).transpose(1, 2, 0)[None]
    return new.reshape(acts.shape), gate_out, grad_gate, grad_up, grad_down


def solution(mesh):
    in_specs = (
        P("segment", None, ("expert", "fsdp"), None),
        P(None, ("expert", "fsdp"), None),
        P("segment", None, ("expert", "fsdp"), None),
        P("segment", None, ("expert", "fsdp"), None),
        P("segment", "expert", None, "fsdp"),
        P("segment", "expert", None, "fsdp"),
        P("segment", "expert", "fsdp", None),
    )
    out_specs = (
        P("segment", None, ("expert", "fsdp"), None),
        P("segment", None, ("expert", "fsdp"), None),
        P("segment", "expert", None, "fsdp"),
        P("segment", "expert", None, "fsdp"),
        P("segment", "expert", "fsdp", None),
    )
    return jax.shard_map(local, mesh=mesh, in_specs=in_specs, out_specs=out_specs, check_vma=False)
```

time: 1050 us -> 358 us (0.34)
  the two profiles are of different devices: /device:TPU:24 before, /device:TPU:8 now
where the time goes in v1:
time: 358 us
  waiting for transfers between devices  242 us (68%)
  blocking collectives  61.4 us (17%)
  starting transfers between devices  23.2 us (6%)
  Pallas kernels  12.1 us (3%)
  local copies, waits for them, and re-layouts  9.01 us (3%)
  other arithmetic  5.4 us (2%)
    ppermute x3, waiting for transfers between devices, local(): grad = lax.ppermute(state[0], 'segment', [(layer, layer - 1)])  204 us
    all_to_all x2, blocking collectives, exchange(): lax.all_to_all(value.reshape(sources, 8, cols), ROUTE, 0, 0, tiled=True)  61.4 us
    all_to_all x1, waiting for transfers between devices, exchange(): lax.all_to_all(value.reshape(sources, 8, cols), ROUTE, 0, 0, tiled=True)  38 us
    all_to_all x1, starting transfers between devices, exchange(): lax.all_to_all(value.reshape(sources, 8, cols), ROUTE, 0, 0, tiled=True)  19.9 us
    pallas_call x5, Pallas kernels, call(): pl.pallas_call(body, out_shape=[jax.ShapeDtypeStruct(s, d) for s, d in ou...  12.1 us
  transfers between devices with their start and end apart: 4, of which 2 were waited for; matrix products, arithmetic and copies ran while one was open for 0% of the time, Pallas kernels for 0%

profile of v1, /device:TPU:8, one launch (start us, length us, event | category | flops | bytes accessed | tf_op | source)
XLA Modules:
  0.0 357.5 jit_solution(16717671421279076480)
XLA Ops:
  0.6 0.8 copy.24
  1.4 0.8 copy.25
  2.2 0.8 copy-done
  3.0 1.7 shard_map.110
  4.7 19.9 %all-to-all-start.8 = ((bf16[128,8,640]{2,1,0:T(8,128)(2,1)}), bf16[128,8,640]{2,1,0:T(8,128)(2,1)S(1)}, u32[]{:S(2)}, u32[]{:S(2)}) async-start(bf16[128,8,640]{2,1,0:T(8,128)(2,1)} %bitcast.25), calls=%async_computation.8 | async-start | bytes 2621440 | tf_op jit(solution)/shard_map/all_to_all | solution.py:176
  24.7 38.0 %all-to-all-done.8 = bf16[128,8,640]{2,1,0:T(8,128)(2,1)S(1)} async-done(((bf16[128,8,640]{2,1,0:T(8,128)(2,1)}), bf16[128,8,640]{2,1,0:T(8,128)(2,1)S(1)}, u32[]{:S(2)}, u32[]{:S(2)}) %all-to-all-start.8) | async-done | bytes 1310752 | tf_op jit(solution)/shard_map/all_to_all | solution.py:176
  62.7 3.4 shard_map.111
  66.1 4.0 %conditional.4 = (bf16[32,1024]{1,0:T(8,128)(2,1)}, f32[64,128]{1,0:T(8,128)}, bf16[1024,512]{1,0:T(8,128)(2,1)}, bf16[1024,256]{1,0:T(8,128)(2,1)}, bf16[1024,256]{1,0:T(8,128)(2,1)}) conditional(s32[]{:T(128)} %convert_element_type.44, () %tuple.40, (bf16[32,128]{1,0:T(8,128)(2,1)S(1)}, bf16[32,1024]{1,0:T(8,128)(2,1)}, ...), branch_computations={%region_0.0_spmd, %region_1.0_spmd} | conditional | bytes 9699452 | solution.py:218
  66.1 1.1 broadcast_in_dim.22
  67.2 0.8 broadcast.16
  68.0 0.8 broadcast.16.clone
  68.8 0.6 broadcast_in_dim.20
  69.4 0.6 broadcast_in_dim.21
  70.0 1.3 collective-permute-start
  71.3 0.7 collective-permute-start.1
  72.0 1.3 collective-permute-start.2
  73.3 0.6 fusion.20
  73.9 204.2 %collective-permute-done.2 = bf16[32,1024]{1,0:T(8,128)(2,1)S(1)} collective-permute-done((bf16[32,1024]{1,0:T(8,128)(2,1)}, bf16[32,1024]{1,0:T(8,128)(2,1)S(1)}, u32[]{:S(2)}, u32[]{:S(2)}) %collective-permute-start.2) | collective-permute-done | bytes 65568 | tf_op jit(solution)/shard_map/ppermute | solution.py:220
  278.1 68.4 %conditional.7 = (f32[64,128]{1,0:T(8,128)}, bf16[1024,512]{1,0:T(8,128)(2,1)}, bf16[1024,256]{1,0:T(8,128)(2,1)}, bf16[1024,256]{1,0:T(8,128)(2,1)}, bf16[1,2,16,1024]{3,2,1,0:T(8,128)(2,1)}) conditional(s32[]{:T(128)} %convert_element_type.41, (f32[64,128]{1,0:T(8,128)}, bf16[1024,512]{1,0:T(8,128)(2,1)}, bf16[1024,256]{1,0:T(8,128)(2,1)}, ...), branch_computations={%region_6.0_spmd, %region_7.0_spmd} | conditional | bytes 9437280 | solution.py:218
  278.4 29.3 %all_to_all.43 = bf16[128,8,512]{2,1,0:T(8,128)(2,1)S(1)} all-to-all(bf16[128,8,512]{2,1,0:T(8,128)(2,1)S(1)} %bitcast.53), channel_id=1, replica_groups=mesh['segment'=4,'expert'=16,'fsdp'=8] {'expert','fsdp'}, dimensions={0} | all-to-all | bytes 2097152 | tf_op jit(solution)/shard_map/cond/branch_1_fun/all_to_all | solution.py:176
  307.7 5.7 %branch_1_fun.22 = (bf16[1024,640]{1,0:T(8,128)(2,1)S(1)}, bf16[1024,256]{1,0:T(8,128)(2,1)}, bf16[1024,256]{1,0:T(8,128)(2,1)}) custom-call(bf16[1024,512]{1,0:T(8,128)(2,1)S(1)} %bitcast.68, bf16[256,1024]{1,0:T(8,128)(2,1)S(1)} %get-tuple-element.170.wd_ref, bf16[1024,256]{1,0:T(8,128)(2,1)S(1)} %get-tuple-element.171.wg_ref, ...), custom_call_target="tpu_custom_call" | custom-call | tf_op jit(solution)/shard_map/cond/branch_1_fun/pallas_call | solution.py:26
  313.4 32.1 %all_to_all.44 = bf16[128,8,640]{2,1,0:T(8,128)(2,1)S(1)} all-to-all(bf16[128,8,640]{2,1,0:T(8,128)(2,1)S(1)} %bitcast.57), channel_id=1, replica_groups=mesh['segment'=4,'expert'=16,'fsdp'=8] {'expert','fsdp'}, dimensions={0} | all-to-all | bytes 2621440 | tf_op jit(solution)/shard_map/cond/branch_1_fun/all_to_all | solution.py:176
  345.5 0.9 branch_1_fun.23
  346.5 3.1 fusion.10
  349.6 0.8 convolution_convert_fusion
  350.5 1.0 copy.23
  351.5 2.0 convolution_convert_fusion.1
  353.5 0.7 convolution_convert_fusion.2
  354.3 0.9 slice_reduce_fusion
  355.3 0.6 copy.29
  355.9 0.8 pad_maximum_fusion.1
  356.7 0.8 pad_maximum_fusion
  (26 shorter events, 0.6 us)
Async XLA Ops:
  2.2 0.8 copy-start
  4.7 58.0 %copy-start.6 = (bf16[1,1,1024,256]{3,2,1,0:T(8,128)(2,1)S(1)}, bf16[1,1,1024,256]{3,2,1,0:T(8,128)(2,1)}, u32[]{:S(2)}) copy-start(bf16[1,1,1024,256]{3,2,1,0:T(8,128)(2,1)} %param.19) | copy-start | bytes 1572868
  4.7 58.0 %copy-start.7 = (bf16[1,1,1024,256]{3,2,1,0:T(8,128)(2,1)S(1)}, bf16[1,1,1024,256]{3,2,1,0:T(8,128)(2,1)}, u32[]{:S(2)}) copy-start(bf16[1,1,1024,256]{3,2,1,0:T(8,128)(2,1)} %param.20) | copy-start | bytes 1572868
  4.7 57.9 %all-to-all-start.8 = ((bf16[128,8,640]{2,1,0:T(8,128)(2,1)}), bf16[128,8,640]{2,1,0:T(8,128)(2,1)S(1)}, u32[]{:S(2)}, u32[]{:S(2)}) async-start(bf16[128,8,640]{2,1,0:T(8,128)(2,1)} %bitcast.25), calls=%async_computation.8 | async-start | bytes 2621440 | tf_op jit(solution)/shard_map/all_to_all | solution.py:176
  24.7 41.4 %copy-start.8 = (bf16[1,1,256,1024]{3,2,1,0:T(8,128)(2,1)S(1)}, bf16[1,1,256,1024]{3,2,1,0:T(8,128)(2,1)}, u32[]{:S(2)}) copy-start(bf16[1,1,256,1024]{3,2,1,0:T(8,128)(2,1)} %param.21) | copy-start | bytes 1572868
  70.0 1.3 collective-permute-start
  71.3 0.7 collective-permute-start.1
  72.0 206.1 %collective-permute-start.2 = (bf16[32,1024]{1,0:T(8,128)(2,1)}, bf16[32,1024]{1,0:T(8,128)(2,1)S(1)}, u32[]{:S(2)}, u32[]{:S(2)}) collective-permute-start(bf16[32,1024]{1,0:T(8,128)(2,1)} %get-tuple-element.304), channel_id=1, source_target_pairs={{128,0},{129,1},{130,2},{131,3},{132,4},{133,5},{134,6},{135,7},{1... | collective-permute-start | bytes 196616 | tf_op jit(solution)/shard_map/ppermute | solution.py:220
  307.7 5.7 %copy-start.4 = (bf16[128,8,512]{2,1,0:T(8,128)(2,1)}, bf16[128,8,512]{2,1,0:T(8,128)(2,1)S(1)}, u32[]{:S(2)}) copy-start(bf16[128,8,512]{2,1,0:T(8,128)(2,1)S(1)} %all_to_all.43) | copy-start | bytes 3145732 | tf_op jit(solution)/shard_map/cond
  313.4 32.1 %copy-start.12 = (bf16[64,1024]{1,0:T(8,128)(2,1)S(1)}, bf16[64,1024]{1,0:T(8,128)(2,1)}, u32[]{:S(2)}) copy-start(bf16[64,1024]{1,0:T(8,128)(2,1)} %get-tuple-element.167.getz_ref) | copy-start | bytes 393220 | tf_op jit(solution)/shard_map/cond
  346.5 3.1 copy-start.5
  351.5 2.0 copy-start.13

commit v2 on v1

v2 whole, which is shorter than its diff:
```python
import jax
import jax.numpy as jnp
from jax import lax
from jax.experimental import pallas as pl
from jax.experimental.pallas import tpu as pltpu
from jax.sharding import PartitionSpec as P

BF = jnp.bfloat16
F32 = jnp.float32
NN = (((1,), (0,)), ((), ()))
NT = (((1,), (1,)), ((), ()))
TN = (((0,), (0,)), ((), ()))
LANES = 128
CHUNK = 256
ROUTE = ("expert", "fsdp")


def dot(a, b, dims):
    return lax.dot_general(a, b, dims, preferred_element_type=F32)


def iota(shape, dim):
    return lax.broadcasted_iota(jnp.int32, shape, dim)


def call(body, outs, *args, cost=None):
    return pl.pallas_call(
        body,
        out_shape=[jax.ShapeDtypeStruct(s, d) for s, d in outs],
        in_specs=[pl.BlockSpec(memory_space=pltpu.VMEM)] * len(args),
        out_specs=[pl.BlockSpec(memory_space=pltpu.VMEM)] * len(outs),
        compiler_params=pltpu.CompilerParams(vmem_limit_bytes=48 * 1024 * 1024),
        cost_estimate=cost,
    )(*args)


def call_rows(body, outs, streamed, whole):
    total = streamed[0].shape[0]
    by_rows = lambda shape: pl.BlockSpec((CHUNK, shape[1]), lambda i: (i, 0))
    return pl.pallas_call(
        body,
        grid=(total // CHUNK,),
        out_shape=[jax.ShapeDtypeStruct(s, d) for s, d in outs],
        in_specs=[by_rows(v.shape) for v in streamed] + [pl.BlockSpec(memory_space=pltpu.VMEM)] * len(whole),
        out_specs=[by_rows(s) for s, _ in outs],
        compiler_params=pltpu.CompilerParams(vmem_limit_bytes=48 * 1024 * 1024),
    )(*streamed, *whole)


def upper(rows, cols):
    return (iota((rows, cols), 0) % 8) >= 4


def place(routing, tokens):
    half = tokens.shape[1] // 2
    spread = dot(routing, tokens, TN)
    rows = spread.shape[0]
    return jnp.where(upper(rows, half), spread[:, half:], spread[:, :half]).astype(BF)


def prep_body(micro, tok, cap, n_expert, n_fsdp, ids_ref, gates_ref, x_ref, spread_ref, put_ref, get_ref, getz_ref):
    rows = micro * tok
    ids = jnp.concatenate([ids_ref[0, m] for m in range(micro)], axis=0)
    gates = jnp.concatenate([gates_ref[0, m].astype(F32) for m in range(micro)], axis=0)
    first, second = ids[:, 0:1], ids[:, 1:2]
    experts = iota((rows, LANES), 1)
    one, two = experts == first, experts == second
    counts = (one | two).astype(BF)
    r0, r1 = iota((rows, rows), 0), iota((rows, rows), 1)
    lower = ((r1 < r0) & (r1 // tok == r0 // tok)).astype(BF)
    before = dot(lower, counts, NN)
    place_of = iota((rows, 1), 0) // tok * cap
    slot_one = jnp.sum(jnp.where(one, before, 0.0), axis=1, keepdims=True).astype(jnp.int32) + place_of
    slot_two = jnp.sum(jnp.where(two, before, 0.0), axis=1, keepdims=True).astype(jnp.int32) + place_of
    cols = 8 * n_expert
    col = iota((rows, cols), 1)
    put_one = ((col // 8 == first) & (col % 4 == slot_one)).astype(F32)
    put_two = ((col // 8 == second) & (col % 4 == slot_two)).astype(F32)
    put = (put_one + put_two).astype(BF)
    put_ref[...] = put
    put_gates = (put_one * gates[:, 0:1] + put_two * gates[:, 1:2]).astype(BF)
    half = x_ref.shape[1] // 2
    spread_ref[:, :half] = place(put, x_ref[...])
    spread_ref[:, half:] = dot(put_gates, jnp.ones((rows, LANES), BF), TN).astype(BF)
    total = 8 * n_expert * n_fsdp
    wide = iota((rows, total), 1)
    target = wide // (8 * n_fsdp)
    row = wide % 4
    low = (wide % 8) < 4
    hit_one = (target == first) & (row == slot_one)
    hit_two = (target == second) & (row == slot_two)
    hit = hit_one | hit_two
    get_ref[:rows] = jnp.where(hit & low, 1.0, 0.0).astype(BF)
    get_ref[rows:] = jnp.where(hit & ~low, 1.0, 0.0).astype(BF)
    getz_ref[:rows] = jnp.where(hit_one & low, 1.0, 0.0).astype(BF)
    getz_ref[rows:] = jnp.where(hit_two & low, 1.0, 0.0).astype(BF)


def fan(send_ref, value, at):
    n_expert, n_fsdp = send_ref.shape[:2]
    width = value.shape[1]
    send_ref[:, :, :, at : at + width] = jnp.broadcast_to(
        value.reshape(n_expert, 1, 8, width), (n_expert, n_fsdp, 8, width)
    )


def place_body(put_ref, g_ref, send_ref):
    fan(send_ref, place(put_ref[...], g_ref[...]), 0)


def fan_body(spread_ref, send_ref):
    fan(send_ref, spread_ref[...], 0)


def place_both_body(spread_ref, put_ref, g_ref, send_ref):
    fan(send_ref, spread_ref[...], 0)
    fan(send_ref, place(put_ref[...], g_ref[...]), spread_ref.shape[1])


def join(mine, other, mask):
    value = jnp.where(mask, other, mine)
    rows, cols = value.shape
    turned = pltpu.roll(value.reshape(rows // 8, 8, cols), 4, 1).reshape(rows, cols)
    return value + turned


def forward(x, c, wg_ref, wu_ref):
    half, hid = wg_ref.shape[0] // 2, wg_ref.shape[1]
    c = jnp.concatenate([c.astype(F32)] * (hid // LANES), axis=1)
    mask = upper(x.shape[0], hid)
    a = join(dot(x, wg_ref[:half, :], NN), dot(x, wg_ref[half:, :], NN), mask)
    b = join(dot(x, wu_ref[:half, :], NN), dot(x, wu_ref[half:, :], NN), mask)
    sig = jax.nn.sigmoid(a)
    s = a * sig
    h = s * b
    return c * (b * (sig * (1.0 + a * (1.0 - sig)))), c * s, h, (c * h).astype(BF)


def backward(g, slope, act, hidden, wd_ref, wg_ref, wu_ref):
    half, hid = wg_ref.shape[0] // 2, wg_ref.shape[1]
    rows = g.shape[0]
    q = join(dot(g, wd_ref[:, :half], NT), dot(g, wd_ref[:, half:], NT), upper(rows, hid))
    da = (q * slope).astype(BF)
    db = (q * act).astype(BF)
    low = dot(da, wg_ref[:half, :], NT) + dot(db, wu_ref[:half, :], NT)
    high = dot(da, wg_ref[half:, :], NT) + dot(db, wu_ref[half:, :], NT)
    out = jnp.where(upper(rows, half), high, low).astype(BF)
    z = jnp.sum(q * hidden, axis=1, keepdims=True)
    return da, db, out, jnp.broadcast_to(z, (rows, LANES)).astype(BF)


def forward_body(rows_ref, wg_ref, wu_ref, slope_ref, act_ref, hid_ref, hg_ref, x_ref):
    half = wg_ref.shape[0] // 2
    x = rows_ref[:, :half]
    x_ref[...] = x
    slope, act, hidden, hg_ref[...] = forward(x, rows_ref[:, half:], wg_ref, wu_ref)
    slope_ref[...] = slope.astype(BF)
    act_ref[...] = act.astype(BF)
    hid_ref[...] = hidden.astype(BF)


def back_body(rows_ref, slope_ref, act_ref, hid_ref, wd_ref, wg_ref, wu_ref, out_ref, da_ref, db_ref, *z_ref):
    half = wg_ref.shape[0] // 2
    da_ref[...], db_ref[...], out, z = backward(
        rows_ref[...],
        slope_ref[...].astype(F32),
        act_ref[...].astype(F32),
        hid_ref[...].astype(F32),
        wd_ref,
        wg_ref,
        wu_ref,
    )
    out_ref[:, :half] = out
    if z_ref:
        z_ref[0][...] = z
    else:
        out_ref[:, half:] = z


def both_body(rows_ref, wd_ref, wg_ref, wu_ref, out_ref, da_ref, db_ref, z_ref, hg_ref, x_ref, g_ref):
    half = wg_ref.shape[0] // 2
    x = rows_ref[:, :half]
    g = rows_ref[:, half + LANES :]
    x_ref[...] = x
    g_ref[...] = g
    slope, act, hidden, hg_ref[...] = forward(x, rows_ref[:, half : half + LANES], wg_ref, wu_ref)
    da_ref[...], db_ref[...], out_ref[...], z_ref[...] = backward(g, slope, act, hidden, wd_ref, wg_ref, wu_ref)


def merge_body(get_ref, back_ref, g_ref, new_ref):
    tokens, width = g_ref.shape
    half = width // 2
    summed = dot(get_ref[...], back_ref[:, :half], NN)
    g = g_ref[...].astype(F32)
    new_ref[:, :half] = (g[:, :half] + summed[:tokens]).astype(BF)
    new_ref[:, half:] = (g[:, half:] + summed[tokens:]).astype(BF)


def gate_body(getz_ref, z_ref, gate_ref):
    _, micro, tok, top = gate_ref.shape
    value = dot(getz_ref[...], z_ref[:, z_ref.shape[1] - LANES :], NN)
    for m in range(micro):
        parts = [value[(k * micro + m) * tok : (k * micro + m + 1) * tok, 0:1] for k in range(top)]
        gate_ref[0, m] = jnp.concatenate(parts, axis=1)


def outer_body(x_ref, g_ref, da_ref, db_ref, hg_ref, gate_ref, up_ref, down_ref):
    total, half = x_ref.shape
    hid = da_ref.shape[1]
    mask = upper(total, hid)
    x = x_ref[...]
    for k in range(2):
        at = slice(k * half, (k + 1) * half)
        keep = mask if k else ~mask
        only = lambda ref: jnp.where(keep, ref[...].astype(F32), 0.0).astype(BF)
        gate_ref[0, 0, at, :] = dot(x, only(da_ref), TN).astype(BF)
        up_ref[0, 0, at, :] = dot(x, only(db_ref), TN).astype(BF)
        down_ref[0, 0, :, at] = dot(only(hg_ref), g_ref[...], TN).astype(BF)


def local(acts, out_grad, expert_ids, gates, w_gate, w_up, w_down):
    segments = lax.axis_size("segment")
    segment = lax.axis_index("segment")
    n_expert = lax.axis_size("expert")
    n_fsdp = lax.axis_size("fsdp")
    _, micro, tok, width = acts.shape
    top = expert_ids.shape[3]
    cap = top * tok // n_expert
    tokens = micro * tok
    half = width // 2
    wide = half + LANES
    wg, wu, wd = w_gate[0, 0], w_up[0, 0], w_down[0, 0]
    hid = wg.shape[1]
    total = 8 * n_expert * n_fsdp
    sources = n_expert * n_fsdp
    last = segments - 1

    def exchange(value):
        cols = value.shape[-1]
        moved = lax.all_to_all(value.reshape(sources, 8, cols), ROUTE, 0, 0, tiled=True)
        return moved.reshape(total, cols)

    def rows_of(*cols):
        return [((total, c), BF) for c in cols]

    spread, put, get, getz = call(
        lambda *r: prep_body(micro, tok, cap, n_expert, n_fsdp, *r),
        [((8 * n_expert, wide), BF), ((tokens, 8 * n_expert), BF), ((2 * tokens, total), BF), ((top * tokens, total), BF)],
        expert_ids,
        gates,
        acts.reshape(tokens, width),
    )
    loss_grad = out_grad.reshape(tokens, width)

    def merge(back, grad):
        return call(merge_body, [((tokens, width), BF)], get, back, grad)[0]

    def gate_of(value):
        return call(gate_body, [((1, micro, tok, top), F32)], getz, value)[0]

    def outer(x_rows, g_rows, da, db, hg):
        cost = pl.CostEstimate(flops=12 * total * width * hid, bytes_accessed=12 * total * half, transcendentals=0)
        shapes = [(w_gate.shape, BF), (w_up.shape, BF), (w_down.shape, BF)]
        return tuple(call(outer_body, shapes, x_rows, g_rows, da, db, hg, cost=cost))

    def first():
        (send,) = call(
            place_both_body, [((n_expert, n_fsdp, 8, wide + half), BF)], spread, put, loss_grad
        )
        rows = exchange(send)
        out, da, db, z, hg, x_rows, g_rows = call_rows(
            both_body, rows_of(half, hid, hid, LANES, hid, half, half), [rows], [wd, wg, wu]
        )
        new = merge(exchange(out), loss_grad)
        unused = jnp.zeros((total, hid), BF)
        return (new, z, g_rows, da, db), (x_rows, unused, unused, unused, hg)

    def gather_rows():
        (send,) = call(fan_body, [((n_expert, n_fsdp, 8, wide), BF)], spread)
        early = lax.cond(segment == last - 1, exchange, lambda v: v.reshape(total, wide), send)
        token = 1.0 + 0.0 * early[0, :8].astype(F32)
        go = sum(lax.ppermute(token, "segment", [(last - 1, k)]) for k in range(last - 1))
        rows = lax.cond(
            go[0] > 0.5, lambda v, e: exchange(v), lambda v, e: e, send, early
        )
        slope, act, hidden, hg, x_rows = call_rows(
            forward_body, rows_of(hid, hid, hid, hid, half), [rows], [wg, wu]
        )
        state = (
            jnp.zeros((tokens, width), BF),
            jnp.zeros((total, LANES), BF),
            jnp.zeros((total, half), BF),
            jnp.zeros((total, hid), BF),
            jnp.zeros((total, hid), BF),
        )
        return state, (x_rows, slope, act, hidden, hg)

    state, saved = lax.cond(segment == last, first, gather_rows)
    x_rows, slope, act, hidden, hg = saved

    def dispatch(grad):
        (send,) = call(place_body, [((n_expert, n_fsdp, 8, half), BF)], put, grad)
        return exchange(send)

    def middle(grad, state):
        g_rows = dispatch(grad)
        out, da, db, z = call_rows(
            back_body, rows_of(half, hid, hid, LANES), [g_rows, slope, act, hidden], [wd, wg, wu]
        )
        new = merge(exchange(out), grad)
        return new, z, g_rows, da, db

    def final(grad, state):
        g_rows = dispatch(grad)
        out, da, db = call_rows(
            back_body, rows_of(wide, hid, hid), [g_rows, slope, act, hidden], [wd, wg, wu]
        )
        back = exchange(out)
        grads = outer(x_rows, g_rows, da, db, hg)
        return (merge(back, grad), gate_of(back)) + grads

    def finish(grad, state):
        new, z, g_rows, da, db = state
        return (new, gate_of(exchange(z))) + outer(x_rows, g_rows, da, db, hg)

    def step_down(layer, new):
        return lax.ppermute(new, "segment", [(layer, layer - 1)])

    grad = step_down(last, state[0])
    for layer in range(last - 1, 0, -1):
        state = lax.cond(segment == layer, middle, lambda g, s: s, grad, state)
        grad = step_down(layer, state[0])
    new, gate, grad_gate, grad_up, grad_down = lax.cond(segment == 0, final, finish, grad, state)
    return new.reshape(acts.shape), gate, grad_gate, grad_up, grad_down


def solution(mesh):
    in_specs = (
        P("segment", None, ("expert", "fsdp"), None),
        P(None, ("expert", "fsdp"), None),
        P("segment", None, ("expert", "fsdp"), None),
        P("segment", None, ("expert", "fsdp"), None),
        P("segment", "expert", None, "fsdp"),
        P("segment", "expert", None, "fsdp"),
        P("segment", "expert", "fsdp", None),
    )
    out_specs = (
        P("segment", None, ("expert", "fsdp"), None),
        P("segment", None, ("expert", "fsdp"), None),
        P("segment", "expert", None, "fsdp"),
        P("segment", "expert", None, "fsdp"),
        P("segment", "expert", "fsdp", None),
    )
    return jax.shard_map(local, mesh=mesh, in_specs=in_specs, out_specs=out_specs, check_vma=False)
```

time: 358 us -> 319 us (0.89)
  waiting for transfers between devices: 242 us -> 205 us
  blocking collectives: 61.4 us -> 76.1 us
  starting transfers between devices: 23.2 us -> 11.6 us
  other arithmetic: 5.4 us -> 0.01 us
  Pallas kernels: 12.1 us -> 16.3 us
    ppermute x3 -> x5, waiting for transfers between devices: 204 us -> 184 us  [the longest x3 122 us: step_down(): return lax.ppermute(new, 'segment', [(layer, layer - 1)])]
    all_to_all x1, waiting for transfers between devices: 38 us -> 21.2 us  [exchange(): lax.all_to_all(value.reshape(sources, 8, cols), ROUTE, 0, 0, tiled=True)]
    all_to_all x2, blocking collectives: 61.4 us -> 76.1 us  [exchange(): lax.all_to_all(value.reshape(sources, 8, cols), ROUTE, 0, 0, tiled=True)]
    all_to_all x1, starting transfers between devices: 19.9 us -> 6.95 us  [exchange(): lax.all_to_all(value.reshape(sources, 8, cols), ROUTE, 0, 0, tiled=True)]
    pallas_call x0 -> x2, Pallas kernels: none -> 8.86 us  [call_rows(): pl.pallas_call(body, grid=(total // CHUNK,), out_shape=[jax.ShapeDtypeStr...]
    pallas_call x5 -> x6, Pallas kernels: 12.1 us -> 7.45 us  [call(): pl.pallas_call(body, out_shape=[jax.ShapeDtypeStruct(s, d) for s, d in ou...]
  transfers between devices with their start and end apart: 4 -> 6, of which waited for: 2 -> 3; matrix products, arithmetic and copies ran while one was open for 0% -> 0% of each run, Pallas kernels for 0% -> 1%
where the time goes in v2:
time: 319 us; the launch traced here: 318 us
  waiting for transfers between devices  205 us (64%)
  blocking collectives  76.1 us (24%)
  Pallas kernels  16.3 us (5%)
  starting transfers between devices  11.6 us (4%)
  local copies, waits for them, and re-layouts  8.28 us (3%)
    ppermute x3, waiting for transfers between devices, step_down(): return lax.ppermute(new, 'segment', [(layer, layer - 1)])  122 us
    all_to_all x2, blocking collectives, exchange(): lax.all_to_all(value.reshape(sources, 8, cols), ROUTE, 0, 0, tiled=True)  76.1 us
    ppermute x2, waiting for transfers between devices, gather_rows(): lax.ppermute(token, 'segment', [(last - 1, k)])  61.5 us
    all_to_all x1, waiting for transfers between devices, exchange(): lax.all_to_all(value.reshape(sources, 8, cols), ROUTE, 0, 0, tiled=True)  21.2 us
    pallas_call x2, Pallas kernels, call_rows(): pl.pallas_call(body, grid=(total // CHUNK,), out_shape=[jax.ShapeDtypeStr...  8.86 us
    pallas_call x6, Pallas kernels, call(): pl.pallas_call(body, out_shape=[jax.ShapeDtypeStruct(s, d) for s, d in ou...  7.45 us
    all_to_all x1, starting transfers between devices, exchange(): lax.all_to_all(value.reshape(sources, 8, cols), ROUTE, 0, 0, tiled=True)  6.95 us
  transfers between devices with their start and end apart: 6, of which 3 were waited for; matrix products, arithmetic and copies ran while one was open for 0% of the time, Pallas kernels for 1%

profile of v2, /device:TPU:8, one launch (start us, length us, event | category | flops | bytes accessed | tf_op | source)
XLA Modules:
  0.0 318.5 jit_solution(10107125231149073108)
XLA Ops:
  0.6 0.8 copy.13.r_0_
  1.4 0.8 copy.14.r_1_
  2.2 0.8 copy-done.1
  3.0 1.0 shard_map.111
  4.0 117.6 %conditional.6 = (bf16[32,1024]{1,0:T(8,128)(2,1)}, bf16[1024,128]{1,0:T(8,128)(2,1)}, bf16[1024,512]{1,0:T(8,128)(2,1)}, bf16[1024,256]{1,0:T(8,128)(2,1)S(1)},...) conditional(s32[]{:T(128)} %convert_element_type.28, ...), branch_computations={%region_0.0_spmd, %region_5.0_spmd} | conditional | flops 36 | bytes 17105594 | solution.py:298
  4.3 1.3 collective-permute-start
  5.6 0.7 collective-permute-start.1
  6.3 61.5 %collective-permute-done = f32[8]{0:T(128)S(1)} collective-permute-done((f32[8]{0:T(128)S(1)}, f32[8]{0:T(128)S(1)}, u32[]{:S(2)}, u32[]{:S(2)}) %collective-permute-start) | collective-permute-done | bytes 64 | tf_op jit(solution)/shard_map/cond/branch_0_fun/ppermute | solution.py:282
  67.8 45.9 %conditional.1 = (bf16[1024,640]{1,0:T(8,128)(2,1)}) conditional(s32[]{:T(128)} %bitcast.6, bf16[1024,640]{1,0:T(8,128)(2,1)} %copy-done.18, bf16[16,8,8,640]{3,2,1,0:T(8,128)(2,1)S(1)} %branch_0_fun.4), branch_computations={%region_3.0_spmd, %region_4.0_spmd} | conditional | bytes 2621448 | solution.py:283
  67.8 45.9 %all_to_all.45 = bf16[128,8,640]{2,1,0:T(8,128)(2,1)} all-to-all(bf16[128,8,640]{2,1,0:T(8,128)(2,1)S(1)} %bitcast.53), channel_id=1, replica_groups=mesh['segment'=4,'expert'=16,'fsdp'=8] {'expert','fsdp'}, dimensions={0} | all-to-all | bytes 2621440 | tf_op jit(solution)/shard_map/cond/branch_0_fun/cond/branch_1_fun/all_to_all | solution.py:240
  113.7 4.5 %branch_0_fun.5 = (bf16[1024,256]{1,0:T(8,128)(2,1)S(1)}, bf16[1024,256]{1,0:T(8,128)(2,1)S(1)}, bf16[1024,256]{1,0:T(8,128)(2,1)}, bf16[1024,256]{1,0:T(8,128)(2,1)}, bf16[1024,512]{1,0:T(8,128)(2,1)}) custom-call(bf16[1024,640]{1,0:T(8,128)(2,1)} %get-tuple-element.321.rows_ref, bf16[1024,256]{1,0:T(8,128)(2,1)S(1)} %copy-done.2, ...), custom_call_target="tpu_custom_call" | custom-call | tf_op jit(solution)/shard_map/cond/branch_0_fun/pallas_call | solution.py:40
  118.3 1.1 broadcast.20
  119.4 0.9 broadcast.21.clone
  120.2 0.7 broadcast.19
  121.0 0.6 broadcast.18
  121.6 0.7 collective-permute-start.2
  122.3 0.2 conditional.7
  122.5 0.7 collective-permute-start.3
  123.2 1.4 collective-permute-start.4
  124.7 122.0 %collective-permute-done.4 = bf16[32,1024]{1,0:T(8,128)(2,1)S(1)} collective-permute-done((bf16[32,1024]{1,0:T(8,128)(2,1)}, bf16[32,1024]{1,0:T(8,128)(2,1)S(1)}, u32[]{:S(2)}, u32[]{:S(2)}) %collective-permute-start.4) | collective-permute-done | bytes 65568 | tf_op jit(solution)/shard_map/ppermute | solution.py:327
  246.7 71.2 %conditional.9 = (bf16[32,1024]{1,0:T(8,128)(2,1)}, bf16[1,1,1024,256]{3,2,1,0:T(8,128)(2,1)}, bf16[1,1,1024,256]{3,2,1,0:T(8,128)(2,1)}, bf16[1,1,256,1024]{3,2,1,0:T(8,128)(2,1)}, f32[1,2,16,2]{2,3,1,0:T(2,128)S(1)}) conditional(s32[]{:T(128)} %convert_element_type.25, (bf16[1024,128]{1,0:T(8,128)(2,1)}, bf16[64,1024]{1,0:T(8,128)(2,1)S(1)}, ...), branch_computations={%region_10.0_spmd, %region_11.0_spmd} | conditional | flops 3221225472 | bytes 29360964 | solution.py:333
  246.7 0.6 copy-done.22
  247.4 0.3 branch_1_fun.23
  247.7 30.2 %all_to_all.52 = bf16[128,8,512]{2,1,0:T(8,128)(2,1)S(1)} all-to-all(bf16[128,8,512]{2,1,0:T(8,128)(2,1)S(1)} %bitcast.42), channel_id=1, replica_groups=mesh['segment'=4,'expert'=16,'fsdp'=8] {'expert','fsdp'}, dimensions={0} | all-to-all | bytes 2097152 | tf_op jit(solution)/shard_map/cond/branch_1_fun/all_to_all | solution.py:240
  277.9 4.3 %branch_1_fun.24 = (bf16[1024,640]{1,0:T(8,128)(2,1)S(1)}, bf16[1024,256]{1,0:T(8,128)(2,1)S(1)}, bf16[1024,256]{1,0:T(8,128)(2,1)S(1)}) custom-call(bf16[1024,512]{1,0:T(8,128)(2,1)S(1)} %bitcast.43, bf16[1024,256]{1,0:T(8,128)(2,1)} %copy-done.19, bf16[1024,256]{1,0:T(8,128)(2,1)} %copy-done.20, bf16[1024,256]{1,0:T(8,128)(2,1)} %get-tuple-element.194.hid_ref, ...), custom_call_target="tpu_custom_call" | custom-call | tf_op jit(solution)/shard_map/cond/branch_1_fun/pallas_call | solution.py:40
  282.3 1.1 copy-done
  283.4 7.0 %all-to-all-start.10 = ((bf16[128,8,640]{2,1,0:T(8,128)(2,1)}), bf16[128,8,640]{2,1,0:T(8,128)(2,1)S(1)}, u32[]{:S(2)}, u32[]{:S(2)}) async-start(bf16[128,8,640]{2,1,0:T(8,128)(2,1)} %bitcast.45), calls=%async_computation.10 | async-start | bytes 2621440 | tf_op jit(solution)/shard_map/cond/branch_1_fun/all_to_all | solution.py:240
  290.3 4.1 %branch_1_fun.27 = (bf16[1,1,1024,256]{3,2,1,0:T(8,128)(2,1)}, bf16[1,1,1024,256]{3,2,1,0:T(8,128)(2,1)}, bf16[1,1,256,1024]{3,2,1,0:T(8,128)(2,1)}) custom-call(bf16[1024,512]{1,0:T(8,128)(2,1)} %get-tuple-element.200.x_ref, bf16[1024,512]{1,0:T(8,128)(2,1)S(1)} %bitcast.44, bf16[1024,256]{1,0:T(8,128)(2,1)S(1)} %get-tuple-element.201.da_ref, ...), custom_call_target="tpu_custom_call" | custom-call | flops 3221225472 | bytes 6291456 | tf_op jit(solution)/shard_map/cond/branch_1_fun/pallas_call | solution.py:27
  294.4 21.2 %all-to-all-done.10 = bf16[128,8,640]{2,1,0:T(8,128)(2,1)S(1)} async-done(((bf16[128,8,640]{2,1,0:T(8,128)(2,1)}), bf16[128,8,640]{2,1,0:T(8,128)(2,1)S(1)}, u32[]{:S(2)}, u32[]{:S(2)}) %all-to-all-start.10) | async-done | bytes 1310752 | tf_op jit(solution)/shard_map/cond/branch_1_fun/all_to_all | solution.py:240
  315.6 1.8 branch_1_fun.25
  317.4 0.2 branch_1_fun.26
  317.9 0.6 copy-done.26
  (37 shorter events, 0.6 us)
Async XLA Ops:
  2.2 0.8 copy-start.1
  4.3 63.5 %copy-start.18 = (bf16[1024,640]{1,0:T(8,128)(2,1)}, bf16[1024,640]{1,0:T(8,128)(2,1)S(1)}, u32[]{:S(2)}) copy-start(bf16[1024,640]{1,0:T(8,128)(2,1)S(1)} %get-tuple-element.320) | copy-start | bytes 3932164 | tf_op jit(solution)/shard_map/cond
  4.3 63.4 %collective-permute-start = (f32[8]{0:T(128)S(1)}, f32[8]{0:T(128)S(1)}, u32[]{:S(2)}, u32[]{:S(2)}) collective-permute-start(f32[8]{0:T(128)S(1)} %fusion.2), channel_id=1, source_target_pairs={{256,0},{257,1},{258,2},{259,3},{260,4},{261,5},{262,6},{263,7},{2... | collective-permute-start | bytes 104 | tf_op jit(solution)/shard_map/cond/branch_0_fun/ppermute | solution.py:282
  5.6 62.1 %collective-permute-start.1 = (f32[8]{0:T(128)S(1)}, f32[8]{0:T(128)S(1)}, u32[]{:S(2)}, u32[]{:S(2)}) collective-permute-start(f32[8]{0:T(128)S(1)} %fusion.2), channel_id=1, source_target_pairs={{256,128},{257,129},{258,130},{259,131},{260,132},{261,133},{262,1... | collective-permute-start | bytes 104 | tf_op jit(solution)/shard_map/cond/branch_0_fun/ppermute | solution.py:282
  67.8 46.0 %copy-start.2 = (bf16[1024,256]{1,0:T(8,128)(2,1)S(1)}, bf16[1024,256]{1,0:T(8,128)(2,1)}, u32[]{:S(2)}) copy-start(bf16[1024,256]{1,0:T(8,128)(2,1)} %get-tuple-element.131.wg_ref) | copy-start | bytes 1572868 | tf_op jit(solution)/shard_map/cond
  67.8 45.9 %copy-start.7 = (bf16[1024,256]{1,0:T(8,128)(2,1)S(1)}, bf16[1024,256]{1,0:T(8,128)(2,1)}, u32[]{:S(2)}) copy-start(bf16[1024,256]{1,0:T(8,128)(2,1)} %get-tuple-element.132.wu_ref) | copy-start | bytes 1572868 | tf_op jit(solution)/shard_map/cond
  121.6 0.7 collective-permute-start.2
  122.5 0.7 collective-permute-start.3
  123.2 123.5 %copy-start.21 = (bf16[64,1024]{1,0:T(8,128)(2,1)S(1)}, bf16[64,1024]{1,0:T(8,128)(2,1)}, u32[]{:S(2)}) copy-start(bf16[64,1024]{1,0:T(8,128)(2,1)} %get-tuple-element.250) | copy-start | bytes 393220
  123.2 123.5 %collective-permute-start.4 = (bf16[32,1024]{1,0:T(8,128)(2,1)}, bf16[32,1024]{1,0:T(8,128)(2,1)S(1)}, u32[]{:S(2)}, u32[]{:S(2)}) collective-permute-start(bf16[32,1024]{1,0:T(8,128)(2,1)} %get-tuple-element.256), channel_id=1, source_target_pairs={{128,0},{129,1},{130,2},{131,3},{132,4},{133,5},{134,6},{135,7},{1... | collective-permute-start | bytes 196616 | tf_op jit(solution)/shard_map/ppermute | solution.py:327
  246.7 0.7 copy-start.22
  246.7 0.7 copy-start.25
  246.7 31.2 %copy-start.19 = (bf16[1024,256]{1,0:T(8,128)(2,1)}, bf16[1024,256]{1,0:T(8,128)(2,1)S(1)}, u32[]{:S(2)}) copy-start(bf16[1024,256]{1,0:T(8,128)(2,1)S(1)} %get-tuple-element.192.slope_ref) | copy-start | bytes 1572868 | tf_op jit(solution)/shard_map/cond
  246.7 31.2 %copy-start.20 = (bf16[1024,256]{1,0:T(8,128)(2,1)}, bf16[1024,256]{1,0:T(8,128)(2,1)S(1)}, u32[]{:S(2)}) copy-start(bf16[1024,256]{1,0:T(8,128)(2,1)S(1)} %get-tuple-element.193.act_ref) | copy-start | bytes 1572868 | tf_op jit(solution)/shard_map/cond
  247.7 30.2 %copy-start.6 = (bf16[1024,256]{1,0:T(8,128)(2,1)S(1)}, bf16[1024,256]{1,0:T(8,128)(2,1)}, u32[]{:S(2)}) copy-start(bf16[1024,256]{1,0:T(8,128)(2,1)} %get-tuple-element.196.wg_ref) | copy-start | bytes 1572868 | tf_op jit(solution)/shard_map/cond
  247.7 30.2 %copy-start.11 = (bf16[1024,256]{1,0:T(8,128)(2,1)S(1)}, bf16[1024,256]{1,0:T(8,128)(2,1)}, u32[]{:S(2)}) copy-start(bf16[1024,256]{1,0:T(8,128)(2,1)} %get-tuple-element.197.wu_ref) | copy-start | bytes 1572868 | tf_op jit(solution)/shard_map/cond
  247.7 30.2 %copy-start.17 = (bf16[256,1024]{1,0:T(8,128)(2,1)S(1)}, bf16[256,1024]{1,0:T(8,128)(2,1)}, u32[]{:S(2)}) copy-start(bf16[256,1024]{1,0:T(8,128)(2,1)} %get-tuple-element.195.wd_ref) | copy-start | bytes 1572868 | tf_op jit(solution)/shard_map/cond
  282.3 1.1 copy-start
  283.4 32.2 %all-to-all-start.10 = ((bf16[128,8,640]{2,1,0:T(8,128)(2,1)}), bf16[128,8,640]{2,1,0:T(8,128)(2,1)S(1)}, u32[]{:S(2)}, u32[]{:S(2)}) async-start(bf16[128,8,640]{2,1,0:T(8,128)(2,1)} %bitcast.45), calls=%async_computation.10 | async-start | bytes 2621440 | tf_op jit(solution)/shard_map/cond/branch_1_fun/all_to_all | solution.py:240
  294.4 23.0 %copy-start.23 = (bf16[64,1024]{1,0:T(8,128)(2,1)S(1)}, bf16[64,1024]{1,0:T(8,128)(2,1)}, u32[]{:S(2)}) copy-start(bf16[64,1024]{1,0:T(8,128)(2,1)} %copy-done.22) | copy-start | bytes 393220 | tf_op jit(solution)/shard_map/cond
  317.9 0.6 copy-start.26

commit v3 on v2

--- a/solution.py
+++ b/solution.py
@@ -11,7 +11,7 @@
 NT = (((1,), (1,)), ((), ()))
 TN = (((0,), (0,)), ((), ()))
 LANES = 128
-CHUNK = 256
+CHUNK = 512
 ROUTE = ("expert", "fsdp")
 
 
@@ -204,6 +204,11 @@
         gate_ref[0, m] = jnp.concatenate(parts, axis=1)
 
 
+def merge_gate_body(get_ref, getz_ref, back_ref, g_ref, new_ref, gate_ref):
+    merge_body(get_ref, back_ref, g_ref, new_ref)
+    gate_body(getz_ref, back_ref, gate_ref)
+
+
 def outer_body(x_ref, g_ref, da_ref, db_ref, hg_ref, gate_ref, up_ref, down_ref):
     total, half = x_ref.shape
     hid = da_ref.shape[1]
@@ -275,13 +280,17 @@
         unused = jnp.zeros((total, hid), BF)
         return (new, z, g_rows, da, db), (x_rows, unused, unused, unused, hg)
 
+    def spread_out(value):
+        return exchange(call(fan_body, [((n_expert, n_fsdp, 8, wide), BF)], value)[0])
+
     def gather_rows():
-        (send,) = call(fan_body, [((n_expert, n_fsdp, 8, wide), BF)], spread)
-        early = lax.cond(segment == last - 1, exchange, lambda v: v.reshape(total, wide), send)
-        token = 1.0 + 0.0 * early[0, :8].astype(F32)
-        go = sum(lax.ppermute(token, "segment", [(last - 1, k)]) for k in range(last - 1))
+        lent = lax.ppermute(spread, "segment", [(last - 1, 0)])
+        helped = lax.cond(segment == 0, spread_out, lambda v: jnp.zeros((total, wide), BF), lent)
+        token = 1.0 + 0.0 * helped[0, :8].astype(F32)
+        go = lax.ppermute(token, "segment", [(0, 1)])
+        handed = lax.ppermute(helped, "segment", [(0, last - 1)])
         rows = lax.cond(
-            go[0] > 0.5, lambda v, e: exchange(v), lambda v, e: e, send, early
+            (segment == 0) | (go[0] > 0.5), lambda v, e: spread_out(v), lambda v, e: e, spread, handed
         )
         slope, act, hidden, hg, x_rows = call_rows(
             forward_body, rows_of(hid, hid, hid, hid, half), [rows], [wg, wu]
@@ -317,7 +326,12 @@
         )
         back = exchange(out)
         grads = outer(x_rows, g_rows, da, db, hg)
-        return (merge(back, grad), gate_of(back)) + grads
+        new, gate = call(
+            merge_gate_body,
+            [((tokens, width), BF), ((1, micro, tok, top), F32)],
+            get, getz, back, grad,
+        )
+        return (new, gate) + grads
 
     def finish(grad, state):
         new, z, g_rows, da, db = state

time: 319 us -> 299 us (0.937)
  waiting for transfers between devices: 205 us -> 153 us
  blocking collectives: 76.1 us -> 107 us
    all_to_all x2 -> x3, blocking collectives: 76.1 us -> 107 us  [exchange(): lax.all_to_all(value.reshape(sources, 8, cols), ROUTE, 0, 0, tiled=True)]
    ppermute x2 -> x3, waiting for transfers between devices: 61.5 us -> 32.8 us  [the longest x1 26.1 us: gather_rows(): handed = lax.ppermute(helped, 'segment', [(0, last - 1)])]
    ppermute x3, waiting for transfers between devices: 122 us -> 99.2 us  [step_down(): return lax.ppermute(new, 'segment', [(layer, layer - 1)])]
  transfers between devices with their start and end apart: 6 -> 7, of which waited for: 3 -> 5; matrix products, arithmetic and copies ran while one was open for 0% -> 0% of each run, Pallas kernels for 1% -> 1%
where the time goes in v3:
time: 299 us
  waiting for transfers between devices  153 us (51%)
  blocking collectives  107 us (36%)
  Pallas kernels  14 us (5%)
  starting transfers between devices  13.9 us (5%)
  local copies, waits for them, and re-layouts  8.91 us (3%)
    all_to_all x3, blocking collectives, exchange(): lax.all_to_all(value.reshape(sources, 8, cols), ROUTE, 0, 0, tiled=True)  107 us
    ppermute x3, waiting for transfers between devices, step_down(): return lax.ppermute(new, 'segment', [(layer, layer - 1)])  99.2 us
    ppermute x1, waiting for transfers between devices, gather_rows(): handed = lax.ppermute(helped, 'segment', [(0, last - 1)])  26.1 us
    all_to_all x1, waiting for transfers between devices, exchange(): lax.all_to_all(value.reshape(sources, 8, cols), ROUTE, 0, 0, tiled=True)  21.2 us
    pallas_call x6, Pallas kernels, call(): pl.pallas_call(body, out_shape=[jax.ShapeDtypeStruct(s, d) for s, d in ou...  7.39 us
    all_to_all x1, starting transfers between devices, exchange(): lax.all_to_all(value.reshape(sources, 8, cols), ROUTE, 0, 0, tiled=True)  7.05 us
    pallas_call x2, Pallas kernels, call_rows(): pl.pallas_call(body, grid=(total // CHUNK,), out_shape=[jax.ShapeDtypeStr...  6.65 us
  transfers between devices with their start and end apart: 7, of which 5 were waited for; matrix products, arithmetic and copies ran while one was open for 0% of the time, Pallas kernels for 1%

profile of v3, /device:TPU:8, one launch (start us, length us, event | category | flops | bytes accessed | tf_op | source)
XLA Modules:
  0.0 298.6 jit_solution(13057104917289289231)
XLA Ops:
  0.6 0.8 copy.13.r_0_
  1.4 0.8 copy.14.r_1_
  2.2 0.8 copy-done.1
  3.0 1.0 shard_map.111
  4.0 122.1 %conditional.6 = (bf16[32,1024]{1,0:T(8,128)(2,1)S(1)}, bf16[1024,128]{1,0:T(8,128)(2,1)}, bf16[1024,512]{1,0:T(8,128)(2,1)}, bf16[1024,256]{1,0:T(8,128)(2,1)S(...) conditional(s32[]{:T(128)} %convert_element_type.30, ...), branch_computations={%region_0.0_spmd, %region_5.0_spmd} | conditional | flops 29 | bytes 23003724 | solution.py:307
  4.0 1.3 collective-permute-start
  5.3 5.9 %collective-permute-done = bf16[128,640]{1,0:T(8,128)(2,1)S(1)} collective-permute-done((bf16[128,640]{1,0:T(8,128)(2,1)S(1)}, bf16[128,640]{1,0:T(8,128)(2,1)S(1)}, u32[]{:S(2)}, u32[]{:S(2)}) %collective-permute-start) | collective-permute-done | bytes 163872 | tf_op jit(solution)/shard_map/cond/branch_0_fun/ppermute | solution.py:287
  11.2 45.7 %conditional = (bf16[1024,640]{1,0:T(8,128)(2,1)}, f32[8]{0:T(128)S(1)}) conditional(s32[]{:T(128)} %convert_element_type.21, () %tuple.37, bf16[128,640]{1,0:T(8,128)(2,1)S(1)} %collective-permute-done), branch_computations={%region_1.0_spmd, %region_2.0_spmd} | conditional | flops 8 | bytes 2621504 | solution.py:288
  11.3 45.0 %all_to_all.44 = bf16[128,8,640]{2,1,0:T(8,128)(2,1)} all-to-all(bf16[128,8,640]{2,1,0:T(8,128)(2,1)S(1)} %bitcast.39), channel_id=1, replica_groups=mesh['segment'=4,'expert'=16,'fsdp'=8] {'expert','fsdp'}, dimensions={0} | all-to-all | bytes 2621440 | tf_op jit(solution)/shard_map/cond/branch_0_fun/cond/branch_1_fun/all_to_all | solution.py:245
  57.0 1.4 collective-permute-start.2
  58.3 1.3 collective-permute-start.1
  59.6 0.8 collective-permute-done.1
  60.5 26.1 %collective-permute-done.2 = bf16[1024,640]{1,0:T(8,128)(2,1)S(1)} collective-permute-done((bf16[1024,640]{1,0:T(8,128)(2,1)}, bf16[1024,640]{1,0:T(8,128)(2,1)S(1)}, u32[]{:S(2)}, u32[]{:S(2)}) %collective-permute-start.2) | collective-permute-done | bytes 1310752 | tf_op jit(solution)/shard_map/cond/branch_0_fun/ppermute | solution.py:291
  86.6 32.2 %conditional.1 = (bf16[1024,640]{1,0:T(8,128)(2,1)S(1)}) conditional(s32[]{:T(128)} %convert_element_type.22, bf16[1024,640]{1,0:T(8,128)(2,1)S(1)} %collective-permute-done.2, bf16[128,640]{1,0:T(8,128)(2,1)S(1)} %get-tuple-element.128), branch_computations={%region_3.0_spmd, %region_4.0_spmd} | conditional | bytes 2621448 | solution.py:292
  86.7 32.1 %all_to_all.45 = bf16[128,8,640]{2,1,0:T(8,128)(2,1)S(1)} all-to-all(bf16[128,8,640]{2,1,0:T(8,128)(2,1)S(1)} %bitcast.38), channel_id=1, replica_groups=mesh['segment'=4,'expert'=16,'fsdp'=8] {'expert','fsdp'}, dimensions={0} | all-to-all | bytes 2621440 | tf_op jit(solution)/shard_map/cond/branch_0_fun/cond/branch_1_fun/all_to_all | solution.py:245
  118.8 1.1 copy-done.22
  119.9 3.5 %branch_0_fun.3 = (bf16[1024,256]{1,0:T(8,128)(2,1)S(1)}, bf16[1024,256]{1,0:T(8,128)(2,1)S(1)}, bf16[1024,256]{1,0:T(8,128)(2,1)S(1)}, bf16[1024,256]{1,0:T(8,128)(2,1)}, bf16[1024,512]{1,0:T(8,128)(2,1)}) custom-call(bf16[1024,640]{1,0:T(8,128)(2,1)} %copy-done.22, bf16[1024,256]{1,0:T(8,128)(2,1)S(1)} %copy-done.2, bf16[1024,256]{1,0:T(8,128)(2,1)S(1)} %copy-done.7), custom_call_target="tpu_custom_call" | custom-call | tf_op jit(solution)/shard_map/cond/branch_0_fun/pallas_call | solution.py:40
  123.4 1.1 broadcast.24
  124.5 0.8 broadcast.25.clone
  125.3 0.7 broadcast.23
  126.1 0.8 collective-permute-start.3
  127.7 1.4 collective-permute-start.5
  129.1 99.2 %collective-permute-done.5 = bf16[32,1024]{1,0:T(8,128)(2,1)S(1)} collective-permute-done((bf16[32,1024]{1,0:T(8,128)(2,1)S(1)}, bf16[32,1024]{1,0:T(8,128)(2,1)S(1)}, u32[]{:S(2)}, u32[]{:S(2)}) %collective-permute-start.5) | collective-permute-done | bytes 65568 | tf_op jit(solution)/shard_map/ppermute | solution.py:341
  228.3 69.7 %conditional.9 = (bf16[32,1024]{1,0:T(8,128)(2,1)}, bf16[1,1,1024,256]{3,2,1,0:T(8,128)(2,1)}, bf16[1,1,1024,256]{3,2,1,0:T(8,128)(2,1)}, bf16[1,1,256,1024]{3,2,1,0:T(8,128)(2,1)}, f32[1,2,16,2]{2,3,1,0:T(2,128)S(1)}) conditional(s32[]{:T(128)} %convert_element_type.27, (bf16[1024,128]{1,0:T(8,128)(2,1)}, bf16[64,1024]{1,0:T(8,128)(2,1)S(1)}, ...), branch_computations={%region_10.0_spmd, %region_11.0_spmd} | conditional | flops 3221225472 | bytes 33031008 | solution.py:347
  228.3 0.7 copy-done.18
  229.6 29.8 %all_to_all.52 = bf16[128,8,512]{2,1,0:T(8,128)(2,1)S(1)} all-to-all(bf16[128,8,512]{2,1,0:T(8,128)(2,1)S(1)} %bitcast.45), channel_id=1, replica_groups=mesh['segment'=4,'expert'=16,'fsdp'=8] {'expert','fsdp'}, dimensions={0} | all-to-all | bytes 2097152 | tf_op jit(solution)/shard_map/cond/branch_1_fun/all_to_all | solution.py:245
  259.5 3.2 %branch_1_fun.27 = (bf16[1024,640]{1,0:T(8,128)(2,1)S(1)}, bf16[1024,256]{1,0:T(8,128)(2,1)S(1)}, bf16[1024,256]{1,0:T(8,128)(2,1)S(1)}) custom-call(bf16[1024,512]{1,0:T(8,128)(2,1)S(1)} %bitcast.46, bf16[1024,256]{1,0:T(8,128)(2,1)S(1)} %copy-done.19, bf16[1024,256]{1,0:T(8,128)(2,1)} %copy-done.20, bf16[1024,256]{1,0:T(8,128)(2,1)} %copy-done.21, ...), custom_call_target="tpu_custom_call" | custom-call | tf_op jit(solution)/shard_map/cond/branch_1_fun/pallas_call | solution.py:40
  262.7 1.1 copy-done
  263.8 7.0 %all-to-all-start.9 = ((bf16[128,8,640]{2,1,0:T(8,128)(2,1)}), bf16[128,8,640]{2,1,0:T(8,128)(2,1)S(1)}, u32[]{:S(2)}, u32[]{:S(2)}) async-start(bf16[128,8,640]{2,1,0:T(8,128)(2,1)} %bitcast.48), calls=%async_computation.9 | async-start | bytes 2621440 | tf_op jit(solution)/shard_map/cond/branch_1_fun/all_to_all | solution.py:245
  270.8 4.1 %branch_1_fun.29 = (bf16[1,1,1024,256]{3,2,1,0:T(8,128)(2,1)}, bf16[1,1,1024,256]{3,2,1,0:T(8,128)(2,1)}, bf16[1,1,256,1024]{3,2,1,0:T(8,128)(2,1)}) custom-call(bf16[1024,512]{1,0:T(8,128)(2,1)} %get-tuple-element.202.x_ref, bf16[1024,512]{1,0:T(8,128)(2,1)S(1)} %bitcast.47, bf16[1024,256]{1,0:T(8,128)(2,1)S(1)} %get-tuple-element.203.da_ref, ...), custom_call_target="tpu_custom_call" | custom-call | flops 3221225472 | bytes 6291456 | tf_op jit(solution)/shard_map/cond/branch_1_fun/pallas_call | solution.py:27
  274.9 21.2 %all-to-all-done.9 = bf16[128,8,640]{2,1,0:T(8,128)(2,1)S(1)} async-done(((bf16[128,8,640]{2,1,0:T(8,128)(2,1)}), bf16[128,8,640]{2,1,0:T(8,128)(2,1)S(1)}, u32[]{:S(2)}, u32[]{:S(2)}) %all-to-all-start.9) | async-done | bytes 1310752 | tf_op jit(solution)/shard_map/cond/branch_1_fun/all_to_all | solution.py:245
  296.1 1.8 branch_1_fun.28
  (43 shorter events, 2.8 us)
Async XLA Ops:
  2.2 0.8 copy-start.1
  4.0 7.2 %collective-permute-start = (bf16[128,640]{1,0:T(8,128)(2,1)S(1)}, bf16[128,640]{1,0:T(8,128)(2,1)S(1)}, u32[]{:S(2)}, u32[]{:S(2)}) collective-permute-start(bf16[128,640]{1,0:T(8,128)(2,1)S(1)} %get-tuple-element.128), channel_id=1, source_target_pairs={{256,0},{257,1},{258,2},{259,3},{260,4},{261,5},{262,6},{263,7},{2... | collective-permute-start | bytes 491528 | tf_op jit(solution)/shard_map/cond/branch_0_fun/ppermute | solution.py:287
  57.0 29.6 %collective-permute-start.2 = (bf16[1024,640]{1,0:T(8,128)(2,1)}, bf16[1024,640]{1,0:T(8,128)(2,1)S(1)}, u32[]{:S(2)}, u32[]{:S(2)}) collective-permute-start(bf16[1024,640]{1,0:T(8,128)(2,1)} %get-tuple-element.130), channel_id=1, source_target_pairs={{0,256},{1,257},{2,258},{3,259},{4,260},{5,261},{6,262},{7,263},{8... | collective-permute-start | bytes 3932168 | tf_op jit(solution)/shard_map/cond/branch_0_fun/ppermute | solution.py:291
  58.3 2.1 collective-permute-start.1
  60.5 59.4 %copy-start.2 = (bf16[1024,256]{1,0:T(8,128)(2,1)S(1)}, bf16[1024,256]{1,0:T(8,128)(2,1)}, u32[]{:S(2)}) copy-start(bf16[1024,256]{1,0:T(8,128)(2,1)} %get-tuple-element.131.wg_ref) | copy-start | bytes 1572868 | tf_op jit(solution)/shard_map/cond
  60.5 59.4 %copy-start.7 = (bf16[1024,256]{1,0:T(8,128)(2,1)S(1)}, bf16[1024,256]{1,0:T(8,128)(2,1)}, u32[]{:S(2)}) copy-start(bf16[1024,256]{1,0:T(8,128)(2,1)} %get-tuple-element.132.wu_ref) | copy-start | bytes 1572868 | tf_op jit(solution)/shard_map/cond
  118.8 1.1 copy-start.22
  126.1 0.8 collective-permute-start.3
  126.9 0.7 collective-permute-start.4
  127.6 100.7 %copy-start.23 = (bf16[64,1024]{1,0:T(8,128)(2,1)S(1)}, bf16[64,1024]{1,0:T(8,128)(2,1)}, u32[]{:S(2)}) copy-start(bf16[64,1024]{1,0:T(8,128)(2,1)} %get-tuple-element.252) | copy-start | bytes 393220
  127.7 100.6 %copy-start.27 = (bf16[32,1024]{1,0:T(8,128)(2,1)}, bf16[32,1024]{1,0:T(8,128)(2,1)S(1)}, u32[]{:S(2)}) copy-start(bf16[32,1024]{1,0:T(8,128)(2,1)S(1)} %get-tuple-element.258) | copy-start | bytes 196612
  127.7 100.6 %collective-permute-start.5 = (bf16[32,1024]{1,0:T(8,128)(2,1)S(1)}, bf16[32,1024]{1,0:T(8,128)(2,1)S(1)}, u32[]{:S(2)}, u32[]{:S(2)}) collective-permute-start(bf16[32,1024]{1,0:T(8,128)(2,1)S(1)} %get-tuple-element.258), channel_id=1, source_target_pairs={{128,0},{129,1},{130,2},{131,3},{132,4},{133,5},{134,6},{135,7},{1... | collective-permute-start | bytes 196616 | tf_op jit(solution)/shard_map/ppermute | solution.py:341
  228.3 0.8 copy-start.18
  228.3 1.0 copy-start.20
  228.3 31.1 %copy-start.21 = (bf16[1024,256]{1,0:T(8,128)(2,1)}, bf16[1024,256]{1,0:T(8,128)(2,1)S(1)}, u32[]{:S(2)}) copy-start(bf16[1024,256]{1,0:T(8,128)(2,1)S(1)} %get-tuple-element.195.hid_ref) | copy-start | bytes 1572868 | tf_op jit(solution)/shard_map/cond
  228.3 31.1 %copy-start.24 = (bf16[64,1024]{1,0:T(8,128)(2,1)}, bf16[64,1024]{1,0:T(8,128)(2,1)S(1)}, u32[]{:S(2)}) copy-start(bf16[64,1024]{1,0:T(8,128)(2,1)S(1)} %get-tuple-element.190.getz_ref) | copy-start | bytes 393220 | tf_op jit(solution)/shard_map/cond
  228.3 31.1 %copy-start.26 = (bf16[32,1024]{1,0:T(8,128)(2,1)}, bf16[32,1024]{1,0:T(8,128)(2,1)S(1)}, u32[]{:S(2)}) copy-start(bf16[32,1024]{1,0:T(8,128)(2,1)S(1)} %get-tuple-element.192.g_ref) | copy-start | bytes 196612 | tf_op jit(solution)/shard_map/cond
  229.6 29.9 %copy-start.6 = (bf16[1024,256]{1,0:T(8,128)(2,1)S(1)}, bf16[1024,256]{1,0:T(8,128)(2,1)}, u32[]{:S(2)}) copy-start(bf16[1024,256]{1,0:T(8,128)(2,1)} %get-tuple-element.197.wg_ref) | copy-start | bytes 1572868 | tf_op jit(solution)/shard_map/cond
  229.6 29.9 %copy-start.11 = (bf16[1024,256]{1,0:T(8,128)(2,1)S(1)}, bf16[1024,256]{1,0:T(8,128)(2,1)}, u32[]{:S(2)}) copy-start(bf16[1024,256]{1,0:T(8,128)(2,1)} %get-tuple-element.198.wu_ref) | copy-start | bytes 1572868 | tf_op jit(solution)/shard_map/cond
  229.6 29.9 %copy-start.17 = (bf16[256,1024]{1,0:T(8,128)(2,1)S(1)}, bf16[256,1024]{1,0:T(8,128)(2,1)}, u32[]{:S(2)}) copy-start(bf16[256,1024]{1,0:T(8,128)(2,1)} %get-tuple-element.196.wd_ref) | copy-start | bytes 1572868 | tf_op jit(solution)/shard_map/cond
  229.6 29.9 %copy-start.19 = (bf16[1024,256]{1,0:T(8,128)(2,1)S(1)}, bf16[1024,256]{1,0:T(8,128)(2,1)}, u32[]{:S(2)}) copy-start(bf16[1024,256]{1,0:T(8,128)(2,1)} %copy-done.18) | copy-start | bytes 1572868 | tf_op jit(solution)/shard_map/cond
  262.7 1.1 copy-start
  263.8 32.3 %all-to-all-start.9 = ((bf16[128,8,640]{2,1,0:T(8,128)(2,1)}), bf16[128,8,640]{2,1,0:T(8,128)(2,1)S(1)}, u32[]{:S(2)}, u32[]{:S(2)}) async-start(bf16[128,8,640]{2,1,0:T(8,128)(2,1)} %bitcast.48), calls=%async_computation.9 | async-start | bytes 2621440 | tf_op jit(solution)/shard_map/cond/branch_1_fun/all_to_all | solution.py:245
  298.0 0.6 copy-start.28

commit v4 on v3

--- a/solution.py
+++ b/solution.py
@@ -12,6 +12,7 @@
 TN = (((0,), (0,)), ((), ()))
 LANES = 128
 CHUNK = 512
+SMALL = 128
 ROUTE = ("expert", "fsdp")
 
 
@@ -34,12 +35,12 @@
     )(*args)
 
 
-def call_rows(body, outs, streamed, whole):
+def call_rows(body, outs, streamed, whole, chunk=CHUNK):
     total = streamed[0].shape[0]
-    by_rows = lambda shape: pl.BlockSpec((CHUNK, shape[1]), lambda i: (i, 0))
+    by_rows = lambda shape: pl.BlockSpec((chunk, shape[1]), lambda i: (i, 0))
     return pl.pallas_call(
         body,
-        grid=(total // CHUNK,),
+        grid=(total // chunk,),
         out_shape=[jax.ShapeDtypeStruct(s, d) for s, d in outs],
         in_specs=[by_rows(v.shape) for v in streamed] + [pl.BlockSpec(memory_space=pltpu.VMEM)] * len(whole),
         out_specs=[by_rows(s) for s, _ in outs],
@@ -58,7 +59,7 @@
     return jnp.where(upper(rows, half), spread[:, half:], spread[:, :half]).astype(BF)
 
 
-def prep_body(micro, tok, cap, n_expert, n_fsdp, ids_ref, gates_ref, x_ref, spread_ref, put_ref, get_ref, getz_ref):
+def prep_body(micro, tok, cap, n_expert, n_fsdp, ids_ref, gates_ref, x_ref, spread_ref, put_ref, get_ref, getz_ref, near_ref, nearz_ref):
     rows = micro * tok
     ids = jnp.concatenate([ids_ref[0, m] for m in range(micro)], axis=0)
     gates = jnp.concatenate([gates_ref[0, m].astype(F32) for m in range(micro)], axis=0)
@@ -78,6 +79,11 @@
     put_two = ((col // 8 == second) & (col % 4 == slot_two)).astype(F32)
     put = (put_one + put_two).astype(BF)
     put_ref[...] = put
+    under = (col % 8) < 4
+    near_ref[:rows] = jnp.where(under, put_one + put_two, 0.0).astype(BF)
+    near_ref[rows:] = jnp.where(under, 0.0, put_one + put_two).astype(BF)
+    nearz_ref[:rows] = jnp.where(under, put_one, 0.0).astype(BF)
+    nearz_ref[rows:] = jnp.where(under, put_two, 0.0).astype(BF)
     put_gates = (put_one * gates[:, 0:1] + put_two * gates[:, 1:2]).astype(BF)
     half = x_ref.shape[1] // 2
     spread_ref[:, :half] = place(put, x_ref[...])
@@ -177,6 +183,15 @@
         out_ref[:, half:] = z
 
 
+def grad_body(rows_ref, slope_ref, act_ref, wd_ref, da_ref, db_ref):
+    half = wd_ref.shape[1] // 2
+    g = rows_ref[...]
+    mask = upper(g.shape[0], wd_ref.shape[0])
+    q = join(dot(g, wd_ref[:, :half], NT), dot(g, wd_ref[:, half:], NT), mask)
+    da_ref[...] = (q * slope_ref[...].astype(F32)).astype(BF)
+    db_ref[...] = (q * act_ref[...].astype(F32)).astype(BF)
+
+
 def both_body(rows_ref, wd_ref, wg_ref, wu_ref, out_ref, da_ref, db_ref, z_ref, hg_ref, x_ref, g_ref):
     half = wg_ref.shape[0] // 2
     x = rows_ref[:, :half]
@@ -185,6 +200,48 @@
     g_ref[...] = g
     slope, act, hidden, hg_ref[...] = forward(x, rows_ref[:, half : half + LANES], wg_ref, wu_ref)
     da_ref[...], db_ref[...], out_ref[...], z_ref[...] = backward(g, slope, act, hidden, wd_ref, wg_ref, wu_ref)
+
+
+def nothing_body(*refs):
+    pass
+
+
+def near_place_body(put_ref, g_ref, send_ref):
+    send_ref[...] = place(put_ref[...], g_ref[...])
+
+
+def near_forward_body(rows_ref, w_ref, slope_ref, act_ref, hid_ref):
+    half = w_ref.shape[2] // 2
+    slope, act, hidden, _ = forward(rows_ref[:, :half], rows_ref[:, half:], w_ref.at[0, 0], w_ref.at[0, 1])
+    slope_ref[0] = slope.astype(BF)
+    act_ref[0] = act.astype(BF)
+    hid_ref[0] = hidden.astype(BF)
+
+
+def near_back_body(g_ref, slope_ref, act_ref, hid_ref, w_ref, out_ref, low_ref, high_ref, z_ref):
+    half, hid = w_ref.shape[2] // 2, w_ref.shape[3]
+    rows = g_ref.shape[0]
+    block = pl.program_id(0)
+
+    @pl.when(block == 0)
+    def _():
+        low_ref[...] = jnp.zeros_like(low_ref)
+        high_ref[...] = jnp.zeros_like(high_ref)
+        z_ref[...] = jnp.zeros_like(z_ref)
+
+    g = g_ref[...]
+    q = join(dot(g, w_ref[0, 2, :half, :], NN), dot(g, w_ref[0, 2, half:, :], NN), upper(rows, hid))
+    da = (q * slope_ref[0].astype(F32)).astype(BF)
+    db = (q * act_ref[0].astype(F32)).astype(BF)
+    low_ref[...] += dot(da, w_ref[0, 0, :half, :], NT) + dot(db, w_ref[0, 1, :half, :], NT)
+    high_ref[...] += dot(da, w_ref[0, 0, half:, :], NT) + dot(db, w_ref[0, 1, half:, :], NT)
+    z = jnp.sum(q * hid_ref[0].astype(F32), axis=1, keepdims=True)
+    z_ref[...] += jnp.broadcast_to(z, z_ref.shape)
+
+    @pl.when(block == pl.num_programs(0) - 1)
+    def _():
+        out_ref[:, :half] = jnp.where(upper(rows, half), high_ref[...], low_ref[...]).astype(BF)
+        out_ref[:, half:] = z_ref[...].astype(BF)
 
 
 def merge_body(get_ref, back_ref, g_ref, new_ref):
@@ -245,12 +302,48 @@
         moved = lax.all_to_all(value.reshape(sources, 8, cols), ROUTE, 0, 0, tiled=True)
         return moved.reshape(total, cols)
 
+    def unfilled(*shapes):
+        return pl.pallas_call(
+            nothing_body,
+            out_shape=[jax.ShapeDtypeStruct(s, d) for s, d in shapes],
+            out_specs=[pl.BlockSpec(memory_space=pl.ANY)] * len(shapes),
+        )()
+
+    def by_block(body, outs, args, whole, scratch=()):
+        one = lambda v: pl.BlockSpec((1,) + v[1:], lambda i: (i,) + (0,) * (len(v) - 1))
+        stay = lambda v: pl.BlockSpec(v, lambda i: (0,) * len(v))
+        return pl.pallas_call(
+            body,
+            grid=(n_fsdp,),
+            out_shape=[jax.ShapeDtypeStruct(v, d) for v, d in outs],
+            in_specs=[stay(v.shape) for v in whole] + [one(v.shape) for v in args],
+            out_specs=[one(v) if len(v) > 2 else stay(v) for v, _ in outs],
+            scratch_shapes=[pltpu.VMEM(v, F32) for v in scratch],
+            compiler_params=pltpu.CompilerParams(vmem_limit_bytes=48 * 1024 * 1024),
+        )(*whole, *args)
+
+    def shift(value, steps):
+        pairs = [(k, (k + steps) % n_fsdp) for k in range(n_fsdp)]
+        return lax.ppermute(value, "fsdp", pairs)
+
+    def ring(own):
+        ahead, behind = [own], [own]
+        for step in range(n_fsdp // 2):
+            ahead.append(shift(ahead[-1], 1))
+            if step < n_fsdp // 2 - 1:
+                behind.append(shift(behind[-1], -1))
+        return ahead + behind[:0:-1]
+
+    def near(value):
+        return value.reshape(n_expert, n_fsdp, 8, value.shape[-1])
+
     def rows_of(*cols):
         return [((total, c), BF) for c in cols]
 
-    spread, put, get, getz = call(
+    spread, put, get, getz, near_get, near_getz = call(
         lambda *r: prep_body(micro, tok, cap, n_expert, n_fsdp, *r),
-        [((8 * n_expert, wide), BF), ((tokens, 8 * n_expert), BF), ((2 * tokens, total), BF), ((top * tokens, total), BF)],
+        [((8 * n_expert, wide), BF), ((tokens, 8 * n_expert), BF), ((2 * tokens, total), BF), ((top * tokens, total), BF)]
+        + [((2 * tokens, 8 * n_expert), BF), ((top * tokens, 8 * n_expert), BF)],
         expert_ids,
         gates,
         acts.reshape(tokens, width),
@@ -268,6 +361,9 @@
         shapes = [(w_gate.shape, BF), (w_up.shape, BF), (w_down.shape, BF)]
         return tuple(call(outer_body, shapes, x_rows, g_rows, da, db, hg, cost=cost))
 
+    fsdp_now = lax.axis_index("fsdp")
+    near_rows = 8 * n_expert
+    blocks = (3, width, hid)
     def first():
         (send,) = call(
             place_both_body, [((n_expert, n_fsdp, 8, wide + half), BF)], spread, put, loss_grad
@@ -277,8 +373,10 @@
             both_body, rows_of(half, hid, hid, LANES, hid, half, half), [rows], [wd, wg, wu]
         )
         new = merge(exchange(out), loss_grad)
-        unused = jnp.zeros((total, hid), BF)
-        return (new, z, g_rows, da, db), (x_rows, unused, unused, unused, hg)
+        unused = unfilled(
+            ((total, hid), BF), ((total, hid), BF), ((total, hid), BF), ((near_rows, wide), BF), *[(blocks, BF)] * n_fsdp
+        )
+        return (new, z, g_rows, da, db), (x_rows, *unused[:3], hg), unused[3], tuple(unused[4:])
 
     def spread_out(value):
         return exchange(call(fan_body, [((n_expert, n_fsdp, 8, wide), BF)], value)[0])
@@ -289,27 +387,70 @@
         token = 1.0 + 0.0 * helped[0, :8].astype(F32)
         go = lax.ppermute(token, "segment", [(0, 1)])
         handed = lax.ppermute(helped, "segment", [(0, last - 1)])
+        pieces = lax.cond(
+            segment == 1,
+            lambda: tuple(ring(jnp.stack([wg, wu, wd.T]))),
+            lambda: tuple(unfilled(*[(blocks, BF)] * n_fsdp)),
+        )
+        far = pieces[n_fsdp // 2][0, 0, 0].astype(F32)
         rows = lax.cond(
-            (segment == 0) | (go[0] > 0.5), lambda v, e: spread_out(v), lambda v, e: e, spread, handed
+            (segment == 0) | ((go[0] > 0.5) & (jnp.abs(far) < 1e30)), lambda v, e: spread_out(v), lambda v, e: e, spread, handed
         )
         slope, act, hidden, hg, x_rows = call_rows(
-            forward_body, rows_of(hid, hid, hid, hid, half), [rows], [wg, wu]
-        )
-        state = (
-            jnp.zeros((tokens, width), BF),
-            jnp.zeros((total, LANES), BF),
-            jnp.zeros((total, half), BF),
-            jnp.zeros((total, hid), BF),
-            jnp.zeros((total, hid), BF),
-        )
-        return state, (x_rows, slope, act, hidden, hg)
-
-    state, saved = lax.cond(segment == last, first, gather_rows)
+            forward_body, rows_of(hid, hid, hid, hid, half), [rows], [wg, wu], SMALL
+        )
+        plane = lax.dynamic_index_in_dim(near(rows), fsdp_now, 1, keepdims=False).reshape(near_rows, wide)
+        state = unfilled(
+            ((tokens, width), BF), ((total, LANES), BF), ((total, half), BF), ((total, hid), BF), ((total, hid), BF)
+        )
+        return tuple(state), (x_rows, slope, act, hidden, hg), plane, pieces
+
+    state, saved, plane, pieces = lax.cond(segment == last, first, gather_rows)
     x_rows, slope, act, hidden, hg = saved
 
     def dispatch(grad):
         (send,) = call(place_body, [((n_expert, n_fsdp, 8, half), BF)], put, grad)
         return exchange(send)
+
+    near_shape = ((n_fsdp, near_rows, hid), BF)
+
+    def near_forward(plane, pieces):
+        whole = jnp.stack(pieces)
+        return (whole, *by_block(near_forward_body, [near_shape] * 3, [whole], [plane]))
+
+    whole, near_slope, near_act, near_hid = lax.cond(
+        segment == 1,
+        near_forward,
+        lambda *_: tuple(unfilled(((n_fsdp,) + blocks, BF), near_shape, near_shape, near_shape)),
+        plane,
+        pieces,
+    )
+
+    def exchange_near(value):
+        cols = value.shape[-1]
+        moved = lax.all_to_all(value.reshape(n_expert, 8, cols), "expert", 0, 0, tiled=True)
+        return moved.reshape(near_rows, cols)
+
+    gate_shape = ((1, micro, tok, top), F32)
+
+    def relay(grad, new):
+        (send,) = call(near_place_body, [((near_rows, half), BF)], put, grad)
+        g_near = exchange_near(send)
+        (out,) = by_block(
+            near_back_body,
+            [((near_rows, wide), BF)],
+            [near_slope, near_act, near_hid, whole],
+            [g_near],
+            [(near_rows, half), (near_rows, half), (near_rows, LANES)],
+        )
+        back = exchange_near(out)
+        new, gate = call(
+            merge_gate_body, [((tokens, width), BF), gate_shape], near_get, near_getz, back, grad
+        )
+        return new, g_near, gate
+
+    def relay_not(grad, new):
+        return (new, *unfilled(((near_rows, half), BF), gate_shape))
 
     def middle(grad, state):
         g_rows = dispatch(grad)
@@ -319,7 +460,7 @@
         new = merge(exchange(out), grad)
         return new, z, g_rows, da, db
 
-    def final(grad, state):
+    def final(grad, state, done):
         g_rows = dispatch(grad)
         out, da, db = call_rows(
             back_body, rows_of(wide, hid, hid), [g_rows, slope, act, hidden], [wd, wg, wu]
@@ -327,24 +468,42 @@
         back = exchange(out)
         grads = outer(x_rows, g_rows, da, db, hg)
         new, gate = call(
-            merge_gate_body,
-            [((tokens, width), BF), ((1, micro, tok, top), F32)],
-            get, getz, back, grad,
+            merge_gate_body, [((tokens, width), BF), gate_shape], get, getz, back, grad
         )
         return (new, gate) + grads
 
-    def finish(grad, state):
-        new, z, g_rows, da, db = state
-        return (new, gate_of(exchange(z))) + outer(x_rows, g_rows, da, db, hg)
+    def collect(state, done):
+        new, g_near, gate, _ = done
+        g_all = jnp.zeros((n_expert, n_fsdp, 8, half), BF)
+        for k, piece in enumerate(ring(g_near)):
+            at = (0, (fsdp_now - k) % n_fsdp, 0, 0)
+            g_all = lax.dynamic_update_slice(g_all, piece.reshape(n_expert, 1, 8, half), at)
+        g_rows = g_all.reshape(total, half)
+        da, db = call_rows(grad_body, rows_of(hid, hid), [g_rows, slope, act], [wd], SMALL)
+        return gate, g_rows, da, db
+
+    def settle(state, done):
+        _, z, g_rows, da, db = state
+        z = z + (0.0 * done[3][0]).astype(BF)
+        return gate_of(exchange(z)), g_rows, da, db
+
+    def finish(grad, state, done):
+        gate, g_rows, da, db = lax.cond(segment == 1, collect, settle, state, done)
+        return (done[0], gate) + outer(x_rows, g_rows, da, db, hg)
 
     def step_down(layer, new):
         return lax.ppermute(new, "segment", [(layer, layer - 1)])
 
     grad = step_down(last, state[0])
-    for layer in range(last - 1, 0, -1):
+    for layer in range(last - 1, 1, -1):
         state = lax.cond(segment == layer, middle, lambda g, s: s, grad, state)
         grad = step_down(layer, state[0])
-    new, gate, grad_gate, grad_up, grad_down = lax.cond(segment == 0, final, finish, grad, state)
+    new, g_near, gate = lax.cond(segment == 1, relay, relay_not, grad, state[0])
+    grad = step_down(1, new)
+    hold = lax.ppermute(1.0 + 0.0 * new[0, :8].astype(F32), "segment", [(1, last)])
+    new, gate, grad_gate, grad_up, grad_down = lax.cond(
+        segment == 0, final, finish, grad, state, (new, g_near, gate, hold)
+    )
     return new.reshape(acts.shape), gate, grad_gate, grad_up, grad_down
 
 

time: 299 us -> 314 us (1.050)
  waiting for transfers between devices: 153 us -> 78.9 us
  starting transfers between devices: 13.9 us -> 60.1 us
  blocking collectives: 107 us -> 145 us
    ppermute x3, waiting for transfers between devices: 99.2 us -> 51.1 us  [step_down(): return lax.ppermute(new, 'segment', [(layer, layer - 1)])]
    ppermute x1, starting transfers between devices: 1.29 us -> 45.3 us  [gather_rows(): go = lax.ppermute(token, 'segment', [(0, 1)])]
    all_to_all x3, blocking collectives: 107 us -> 145 us  [exchange(): lax.all_to_all(value.reshape(sources, 8, cols), ROUTE, 0, 0, tiled=True)]
    ppermute x1, waiting for transfers between devices: 26.1 us -> 0.01 us  [gather_rows(): handed = lax.ppermute(helped, 'segment', [(0, last - 1)])]
    pallas_call x2 -> x6, Pallas kernels: 6.65 us -> 9.74 us  [the longest x2 9.74 us: call_rows(): pl.pallas_call(body, grid=(total // chunk,), out_shape=[jax.ShapeDtypeStr...]
  transfers between devices with their start and end apart: 7 -> 8, of which waited for: 5 -> 4; matrix products, arithmetic and copies ran while one was open for 0% -> 1% of each run, Pallas kernels for 1% -> 1%
where the time goes in v4:
time: 314 us; the launch traced here: 312 us
  blocking collectives  145 us (46%)
  waiting for transfers between devices  78.9 us (25%)
  starting transfers between devices  60.1 us (19%)
  Pallas kernels  17.1 us (5%)
  local copies, waits for them, and re-layouts  7.98 us (3%)
    all_to_all x3, blocking collectives, exchange(): lax.all_to_all(value.reshape(sources, 8, cols), ROUTE, 0, 0, tiled=True)  145 us
    ppermute x3, waiting for transfers between devices, step_down(): return lax.ppermute(new, 'segment', [(layer, layer - 1)])  51.1 us
    ppermute x1, starting transfers between devices, gather_rows(): go = lax.ppermute(token, 'segment', [(0, 1)])  45.3 us
    all_to_all x1, waiting for transfers between devices, exchange(): lax.all_to_all(value.reshape(sources, 8, cols), ROUTE, 0, 0, tiled=True)  21.2 us
    pallas_call x2, Pallas kernels, call_rows(): pl.pallas_call(body, grid=(total // chunk,), out_shape=[jax.ShapeDtypeStr...  9.74 us
    all_to_all x1, starting transfers between devices, exchange(): lax.all_to_all(value.reshape(sources, 8, cols), ROUTE, 0, 0, tiled=True)  7.73 us
    pallas_call x6, Pallas kernels, call(): pl.pallas_call(body, out_shape=[jax.ShapeDtypeStruct(s, d) for s, d in ou...  7.39 us
  transfers between devices with their start and end apart: 8, of which 4 were waited for; matrix products, arithmetic and copies ran while one was open for 1% of the time, Pallas kernels for 1%

profile of v4, /device:TPU:8, one launch (start us, length us, event | category | flops | bytes accessed | tf_op | source)
XLA Modules:
  0.0 312.2 jit_solution(10849921838039393073)
XLA Ops:
  0.6 0.8 copy.23.r_0_
  1.4 0.8 copy.24.r_1_
  2.2 0.8 copy-done.1
  3.0 1.0 shard_map.111
  4.0 180.0 %conditional.9 = (bf16[32,1024]{1,0:T(8,128)(2,1)}, bf16[1024,128]{1,0:T(8,128)(2,1)}, bf16[1024,512]{1,0:T(8,128)(2,1)}, bf16[1024,256]{1,0:T(8,128)(2,1)}, bf1...) conditional(s32[]{:T(128)} %convert_element_type.57, ...), branch_computations={%region_0.7_spmd, %region_7.8_spmd} | conditional | flops 1572901 | bytes 68617288 | solution.py:408
  4.0 1.3 collective-permute-start.7
  5.3 5.9 %collective-permute-done.7 = bf16[128,640]{1,0:T(8,128)(2,1)S(1)} collective-permute-done((bf16[128,640]{1,0:T(8,128)(2,1)S(1)}, bf16[128,640]{1,0:T(8,128)(2,1)S(1)}, u32[]{:S(2)}, u32[]{:S(2)}) %collective-permute-start.7) | collective-permute-done | bytes 163872 | tf_op jit(solution)/shard_map/cond/branch_0_fun/ppermute | solution.py:385
  11.2 51.2 %conditional = (bf16[1024,640]{1,0:T(8,128)(2,1)}, f32[8]{0:T(128)S(1)}) conditional(s32[]{:T(128)} %convert_element_type.42, () %tuple.69, bf16[128,640]{1,0:T(8,128)(2,1)S(1)} %collective-permute-done.7), branch_computations={%region_1.0_spmd, %region_2.0_spmd} | conditional | flops 8 | bytes 2621504 | solution.py:386
  11.3 50.4 %all_to_all.44 = bf16[128,8,640]{2,1,0:T(8,128)(2,1)} all-to-all(bf16[128,8,640]{2,1,0:T(8,128)(2,1)S(1)} %bitcast.103), channel_id=1, replica_groups=mesh['segment'=4,'expert'=16,'fsdp'=8] {'expert','fsdp'}, dimensions={0} | all-to-all | bytes 2621440 | tf_op jit(solution)/shard_map/cond/branch_0_fun/cond/branch_1_fun/all_to_all | solution.py:302
  61.8 0.7 fusion
  62.4 2.4 collective-permute-start.9
  64.8 1.2 slice.20
  66.7 45.3 %collective-permute-start.8 = (f32[8]{0:T(128)S(1)}, f32[8]{0:T(128)S(1)}, u32[]{:S(2)}, u32[]{:S(2)}) collective-permute-start(f32[8]{0:T(128)S(1)} %multiply_add_fusion), channel_id=1, source_target_pairs={{0,128},{1,129},{2,130},{3,131},{4,132},{5,133},{6,134},{7,135},{8... | collective-permute-start | bytes 104 | tf_op jit(solution)/shard_map/cond/branch_0_fun/ppermute | solution.py:388
  112.0 0.8 collective-permute-done.8
  112.9 64.7 %conditional.2 = (bf16[1024,640]{1,0:T(8,128)(2,1)}, bf16[16,8,8,640]{3,2,1,0:T(8,128)(2,1)S(1)}) conditional(s32[]{:T(128)} %convert_element_type.45, bf16[1024,640]{1,0:T(8,128)(2,1)} %collective-permute-done.9, bf16[128,640]{1,0:T(8,128)(2,1)S(1)} %get-tuple-element.237), branch_computations={%region_5.0_spmd, %region_6.0_spmd} | conditional | bytes 5242896 | solution.py:396
  113.0 63.2 %all_to_all.45 = bf16[128,8,640]{2,1,0:T(8,128)(2,1)} all-to-all(bf16[128,8,640]{2,1,0:T(8,128)(2,1)S(1)} %bitcast.102), channel_id=1, replica_groups=mesh['segment'=4,'expert'=16,'fsdp'=8] {'expert','fsdp'}, dimensions={0} | all-to-all | bytes 2621440 | tf_op jit(solution)/shard_map/cond/branch_0_fun/cond/branch_1_fun/all_to_all | solution.py:302
  176.3 1.3 copy.67
  177.6 6.5 %branch_0_fun.9 = (bf16[1024,256]{1,0:T(8,128)(2,1)S(1)}, bf16[1024,256]{1,0:T(8,128)(2,1)}, bf16[1024,256]{1,0:T(8,128)(2,1)}, bf16[1024,256]{1,0:T(8,128)(2,1)}, bf16[1024,512]{1,0:T(8,128)(2,1)}) custom-call(bf16[1024,640]{1,0:T(8,128)(2,1)} %get-tuple-element.244.rows_ref, bf16[1024,256]{1,0:T(8,128)(2,1)S(1)} %copy-done.10, bf16[1024,256]{1,0:T(8,128)(2,1)S(1)} %copy-done.13), custom_call_target="tpu_custom_call" | custom-call | tf_op jit(solution)/shard_map/cond/branch_0_fun/pallas_call | solution.py:41
  184.0 0.7 collective-permute-start.17
  184.7 0.9 conditional.10
  184.7 0.8 copy.119
  186.4 1.4 collective-permute-start.20
  187.8 0.7 add_bitcast_fusion.1
  189.2 51.1 %collective-permute-done.20 = bf16[32,1024]{1,0:T(8,128)(2,1)S(1)} collective-permute-done((bf16[32,1024]{1,0:T(8,128)(2,1)}, bf16[32,1024]{1,0:T(8,128)(2,1)S(1)}, u32[]{:S(2)}, u32[]{:S(2)}) %collective-permute-start.20) | collective-permute-done | bytes 65568 | tf_op jit(solution)/shard_map/ppermute | solution.py:495
  240.2 71.4 %conditional.13 = (bf16[32,1024]{1,0:T(8,128)(2,1)}, f32[1,2,16,2]{2,3,1,0:T(2,128)S(1)}, bf16[1,1,1024,256]{3,2,1,0:T(8,128)(2,1)}, bf16[1,1,1024,256]{3,2,1,0:T(8,128)(2,1)}, bf16[1,1,256,1024]{3,2,1,0:T(8,128)(2,1)}) conditional(s32[]{:T(128)} %convert_element_type.54, (s32[]{:T(128)}, f32[8]{0:T(128)S(1)}, bf16[1024,128]{1,0:T(8,128)(2,1)}, ...), branch_computations={%region_14.17_spmd, %region_17.18_spmd} | conditional | flops 3221356544 | bytes 26739468 | solution.py:504
  241.3 31.1 %all_to_all.52 = bf16[128,8,512]{2,1,0:T(8,128)(2,1)S(1)} all-to-all(bf16[128,8,512]{2,1,0:T(8,128)(2,1)S(1)} %bitcast.107), channel_id=1, replica_groups=mesh['segment'=4,'expert'=16,'fsdp'=8] {'expert','fsdp'}, dimensions={0} | all-to-all | bytes 2097152 | tf_op jit(solution)/shard_map/cond/branch_1_fun/all_to_all | solution.py:302
  272.4 3.3 %branch_1_fun.33 = (bf16[1024,640]{1,0:T(8,128)(2,1)S(1)}, bf16[1024,256]{1,0:T(8,128)(2,1)S(1)}, bf16[1024,256]{1,0:T(8,128)(2,1)S(1)}) custom-call(bf16[1024,512]{1,0:T(8,128)(2,1)S(1)} %bitcast.108, bf16[1024,256]{1,0:T(8,128)(2,1)} %copy-done.17, bf16[1024,256]{1,0:T(8,128)(2,1)} %get-tuple-element.371.act_ref, ...), custom_call_target="tpu_custom_call" | custom-call | tf_op jit(solution)/shard_map/cond/branch_1_fun/pallas_call | solution.py:41
  275.7 1.1 copy-done
  276.7 7.7 %all-to-all-start.8 = ((bf16[128,8,640]{2,1,0:T(8,128)(2,1)}), bf16[128,8,640]{2,1,0:T(8,128)(2,1)S(1)}, u32[]{:S(2)}, u32[]{:S(2)}) async-start(bf16[128,8,640]{2,1,0:T(8,128)(2,1)} %bitcast.110), calls=%async_computation.8 | async-start | bytes 2621440 | tf_op jit(solution)/shard_map/cond/branch_1_fun/all_to_all | solution.py:302
  284.5 4.1 %branch_1_fun.35 = (bf16[1,1,1024,256]{3,2,1,0:T(8,128)(2,1)}, bf16[1,1,1024,256]{3,2,1,0:T(8,128)(2,1)}, bf16[1,1,256,1024]{3,2,1,0:T(8,128)(2,1)}) custom-call(bf16[1024,512]{1,0:T(8,128)(2,1)} %get-tuple-element.379.x_ref, bf16[1024,512]{1,0:T(8,128)(2,1)S(1)} %bitcast.109, bf16[1024,256]{1,0:T(8,128)(2,1)S(1)} %get-tuple-element.380.da_ref, ...), custom_call_target="tpu_custom_call" | custom-call | flops 3221225472 | bytes 6291456 | tf_op jit(solution)/shard_map/cond/branch_1_fun/pallas_call | solution.py:28
  288.5 21.2 %all-to-all-done.8 = bf16[128,8,640]{2,1,0:T(8,128)(2,1)S(1)} async-done(((bf16[128,8,640]{2,1,0:T(8,128)(2,1)}), bf16[128,8,640]{2,1,0:T(8,128)(2,1)S(1)}, u32[]{:S(2)}, u32[]{:S(2)}) %all-to-all-start.8) | async-done | bytes 1310752 | tf_op jit(solution)/shard_map/cond/branch_1_fun/all_to_all | solution.py:302
  309.7 1.8 branch_1_fun.34
  (49 shorter events, 3.1 us)
Async XLA Ops:
  2.2 0.8 copy-start.1
  4.0 7.2 %collective-permute-start.7 = (bf16[128,640]{1,0:T(8,128)(2,1)S(1)}, bf16[128,640]{1,0:T(8,128)(2,1)S(1)}, u32[]{:S(2)}, u32[]{:S(2)}) collective-permute-start(bf16[128,640]{1,0:T(8,128)(2,1)S(1)} %get-tuple-element.237), channel_id=1, source_target_pairs={{256,0},{257,1},{258,2},{259,3},{260,4},{261,5},{262,6},{263,7},{2... | collective-permute-start | bytes 491528 | tf_op jit(solution)/shard_map/cond/branch_0_fun/ppermute | solution.py:385
  5.3 59.5 %copy-start.4 = (bf16[256,1024]{1,0:T(8,128)(2,1)S(1)}, bf16[256,1024]{1,0:T(8,128)(2,1)}, u32[]{:S(2)}) copy-start(bf16[256,1024]{1,0:T(8,128)(2,1)} %get-tuple-element.492) | copy-start | bytes 1572868 | tf_op jit(solution)/shard_map/cond
  5.3 59.5 %copy-start.10 = (bf16[1024,256]{1,0:T(8,128)(2,1)S(1)}, bf16[1024,256]{1,0:T(8,128)(2,1)}, u32[]{:S(2)}) copy-start(bf16[1024,256]{1,0:T(8,128)(2,1)} %get-tuple-element.245.wg_ref) | copy-start | bytes 1572868 | tf_op jit(solution)/shard_map/cond
  5.3 59.5 %copy-start.13 = (bf16[1024,256]{1,0:T(8,128)(2,1)S(1)}, bf16[1024,256]{1,0:T(8,128)(2,1)}, u32[]{:S(2)}) copy-start(bf16[1024,256]{1,0:T(8,128)(2,1)} %get-tuple-element.246.wu_ref) | copy-start | bytes 1572868 | tf_op jit(solution)/shard_map/cond
  62.4 50.5 %collective-permute-start.9 = (bf16[1024,640]{1,0:T(8,128)(2,1)}, bf16[1024,640]{1,0:T(8,128)(2,1)}, u32[]{:S(2)}, u32[]{:S(2)}) collective-permute-start(bf16[1024,640]{1,0:T(8,128)(2,1)} %get-tuple-element.243), channel_id=1, source_target_pairs={{0,256},{1,257},{2,258},{3,259},{4,260},{5,261},{6,262},{7,263},{8... | collective-permute-start | bytes 3932168 | tf_op jit(solution)/shard_map/cond/branch_0_fun/ppermute | solution.py:389
  66.7 46.2 %collective-permute-start.8 = (f32[8]{0:T(128)S(1)}, f32[8]{0:T(128)S(1)}, u32[]{:S(2)}, u32[]{:S(2)}) collective-permute-start(f32[8]{0:T(128)S(1)} %multiply_add_fusion), channel_id=1, source_target_pairs={{0,128},{1,129},{2,130},{3,131},{4,132},{5,133},{6,134},{7,135},{8... | collective-permute-start | bytes 104 | tf_op jit(solution)/shard_map/cond/branch_0_fun/ppermute | solution.py:388
  184.0 0.7 collective-permute-start.17
  185.6 0.7 copy-start.22
  185.6 0.7 collective-permute-start.18
  186.3 53.9 %copy-start.3 = (bf16[1,1,256,1024]{3,2,1,0:T(8,128)(2,1)S(1)}, bf16[1,1,256,1024]{3,2,1,0:T(8,128)(2,1)}, u32[]{:S(2)}) copy-start(bf16[1,1,256,1024]{3,2,1,0:T(8,128)(2,1)} %param.31) | copy-start | bytes 1572868
  186.3 53.9 %copy-start.9 = (bf16[1,1,1024,256]{3,2,1,0:T(8,128)(2,1)S(1)}, bf16[1,1,1024,256]{3,2,1,0:T(8,128)(2,1)}, u32[]{:S(2)}) copy-start(bf16[1,1,1024,256]{3,2,1,0:T(8,128)(2,1)} %param.29) | copy-start | bytes 1572868
  186.3 53.9 %copy-start.18 = (bf16[64,1024]{1,0:T(8,128)(2,1)S(1)}, bf16[64,1024]{1,0:T(8,128)(2,1)}, u32[]{:S(2)}) copy-start(bf16[64,1024]{1,0:T(8,128)(2,1)} %get-tuple-element.464) | copy-start | bytes 393220
  186.4 53.9 %collective-permute-start.20 = (bf16[32,1024]{1,0:T(8,128)(2,1)}, bf16[32,1024]{1,0:T(8,128)(2,1)S(1)}, u32[]{:S(2)}, u32[]{:S(2)}) collective-permute-start(bf16[32,1024]{1,0:T(8,128)(2,1)} %get-tuple-element.462), channel_id=1, source_target_pairs={{128,0},{129,1},{130,2},{131,3},{132,4},{133,5},{134,6},{135,7},{1... | collective-permute-start | bytes 196616 | tf_op jit(solution)/shard_map/ppermute | solution.py:495
  188.5 0.7 collective-permute-start.19
  240.5 0.8 copy-start.7
  240.5 31.9 %copy-start.17 = (bf16[1024,256]{1,0:T(8,128)(2,1)}, bf16[1024,256]{1,0:T(8,128)(2,1)S(1)}, u32[]{:S(2)}) copy-start(bf16[1024,256]{1,0:T(8,128)(2,1)S(1)} %get-tuple-element.370.slope_ref) | copy-start | bytes 1572868 | tf_op jit(solution)/shard_map/cond
  240.5 31.9 %copy-start.19 = (bf16[64,1024]{1,0:T(8,128)(2,1)}, bf16[64,1024]{1,0:T(8,128)(2,1)S(1)}, u32[]{:S(2)}) copy-start(bf16[64,1024]{1,0:T(8,128)(2,1)S(1)} %get-tuple-element.367.getz_ref) | copy-start | bytes 393220 | tf_op jit(solution)/shard_map/cond
  240.5 31.8 %copy-start.21 = (bf16[32,1024]{1,0:T(8,128)(2,1)}, bf16[32,1024]{1,0:T(8,128)(2,1)S(1)}, u32[]{:S(2)}) copy-start(bf16[32,1024]{1,0:T(8,128)(2,1)S(1)} %get-tuple-element.369.g_ref) | copy-start | bytes 196612 | tf_op jit(solution)/shard_map/cond
  240.5 31.8 %copy-start.16 = (bf16[1024,256]{1,0:T(8,128)(2,1)S(1)}, bf16[1024,256]{1,0:T(8,128)(2,1)}, u32[]{:S(2)}) copy-start(bf16[1024,256]{1,0:T(8,128)(2,1)} %get-tuple-element.375.wu_ref) | copy-start | bytes 1572868 | tf_op jit(solution)/shard_map/cond
  241.3 31.1 %copy-start.8 = (bf16[256,1024]{1,0:T(8,128)(2,1)S(1)}, bf16[256,1024]{1,0:T(8,128)(2,1)}, u32[]{:S(2)}) copy-start(bf16[256,1024]{1,0:T(8,128)(2,1)} %copy-done.7) | copy-start | bytes 1572868 | tf_op jit(solution)/shard_map/cond
  275.7 1.1 copy-start
  276.7 33.0 %all-to-all-start.8 = ((bf16[128,8,640]{2,1,0:T(8,128)(2,1)}), bf16[128,8,640]{2,1,0:T(8,128)(2,1)S(1)}, u32[]{:S(2)}, u32[]{:S(2)}) async-start(bf16[128,8,640]{2,1,0:T(8,128)(2,1)} %bitcast.110), calls=%async_computation.8 | async-start | bytes 2621440 | tf_op jit(solution)/shard_map/cond/branch_1_fun/all_to_all | solution.py:302
  311.7 0.6 copy-start.23

commit v5 on v4

--- a/solution.py
+++ b/solution.py
@@ -211,15 +211,21 @@
 
 
 def near_forward_body(rows_ref, w_ref, slope_ref, act_ref, hid_ref):
-    half = w_ref.shape[2] // 2
-    slope, act, hidden, _ = forward(rows_ref[:, :half], rows_ref[:, half:], w_ref.at[0, 0], w_ref.at[0, 1])
-    slope_ref[0] = slope.astype(BF)
-    act_ref[0] = act.astype(BF)
-    hid_ref[0] = hidden.astype(BF)
+    half = w_ref.shape[3] // 2
+    x, c = rows_ref[:, :half], rows_ref[:, half:]
+    c = jnp.concatenate([c.astype(F32)] * (w_ref.shape[2] // LANES), axis=1)
+    mask = upper(*c.shape)
+    a = join(dot(x, w_ref[0, 0, :, :half], NT), dot(x, w_ref[0, 0, :, half:], NT), mask)
+    b = join(dot(x, w_ref[0, 1, :, :half], NT), dot(x, w_ref[0, 1, :, half:], NT), mask)
+    sig = jax.nn.sigmoid(a)
+    s = a * sig
+    slope_ref[0] = (c * (b * (sig * (1.0 + a * (1.0 - sig))))).astype(BF)
+    act_ref[0] = (c * s).astype(BF)
+    hid_ref[0] = (s * b).astype(BF)
 
 
 def near_back_body(g_ref, slope_ref, act_ref, hid_ref, w_ref, out_ref, low_ref, high_ref, z_ref):
-    half, hid = w_ref.shape[2] // 2, w_ref.shape[3]
+    half, hid = w_ref.shape[3] // 2, w_ref.shape[2]
     rows = g_ref.shape[0]
     block = pl.program_id(0)
 
@@ -230,11 +236,11 @@
         z_ref[...] = jnp.zeros_like(z_ref)
 
     g = g_ref[...]
-    q = join(dot(g, w_ref[0, 2, :half, :], NN), dot(g, w_ref[0, 2, half:, :], NN), upper(rows, hid))
+    q = join(dot(g, w_ref[0, 2, :, :half], NT), dot(g, w_ref[0, 2, :, half:], NT), upper(rows, hid))
     da = (q * slope_ref[0].astype(F32)).astype(BF)
     db = (q * act_ref[0].astype(F32)).astype(BF)
-    low_ref[...] += dot(da, w_ref[0, 0, :half, :], NT) + dot(db, w_ref[0, 1, :half, :], NT)
-    high_ref[...] += dot(da, w_ref[0, 0, half:, :], NT) + dot(db, w_ref[0, 1, half:, :], NT)
+    low_ref[...] += dot(da, w_ref[0, 0, :, :half], NN) + dot(db, w_ref[0, 1, :, :half], NN)
+    high_ref[...] += dot(da, w_ref[0, 0, :, half:], NN) + dot(db, w_ref[0, 1, :, half:], NN)
     z = jnp.sum(q * hid_ref[0].astype(F32), axis=1, keepdims=True)
     z_ref[...] += jnp.broadcast_to(z, z_ref.shape)
 
@@ -334,6 +340,19 @@
                 behind.append(shift(behind[-1], -1))
         return ahead + behind[:0:-1]
 
+    def ring_whole(own):
+        whole = unfilled(((n_fsdp,) + own.shape, BF))[0]
+        whole = lax.dynamic_update_slice(whole, own[None], (0, 0, 0, 0))
+        ahead, behind, count = own, own, 1
+        for step in range(n_fsdp // 2):
+            ahead = shift(ahead, 1)
+            behind = shift(behind, -1) if step < n_fsdp // 2 - 1 else None
+            for value in (behind, ahead):
+                if value is not None:
+                    whole = lax.dynamic_update_slice(whole, value[None], (count, 0, 0, 0))
+                    count += 1
+        return whole
+
     def near(value):
         return value.reshape(n_expert, n_fsdp, 8, value.shape[-1])
 
@@ -363,7 +382,7 @@
 
     fsdp_now = lax.axis_index("fsdp")
     near_rows = 8 * n_expert
-    blocks = (3, width, hid)
+    blocks = (3, hid, width)
     def first():
         (send,) = call(
             place_both_body, [((n_expert, n_fsdp, 8, wide + half), BF)], spread, put, loss_grad
@@ -374,38 +393,41 @@
         )
         new = merge(exchange(out), loss_grad)
         unused = unfilled(
-            ((total, hid), BF), ((total, hid), BF), ((total, hid), BF), ((near_rows, wide), BF), *[(blocks, BF)] * n_fsdp
-        )
-        return (new, z, g_rows, da, db), (x_rows, *unused[:3], hg), unused[3], tuple(unused[4:])
+            ((total, hid), BF), ((total, hid), BF), ((total, hid), BF), ((near_rows, wide), BF), ((n_fsdp,) + blocks, BF)
+        )
+        return (new, z, g_rows, da, db), (x_rows, *unused[:3], hg), unused[3], unused[4]
 
     def spread_out(value):
         return exchange(call(fan_body, [((n_expert, n_fsdp, 8, wide), BF)], value)[0])
 
     def gather_rows():
         lent = lax.ppermute(spread, "segment", [(last - 1, 0)])
-        helped = lax.cond(segment == 0, spread_out, lambda v: jnp.zeros((total, wide), BF), lent)
-        token = 1.0 + 0.0 * helped[0, :8].astype(F32)
-        go = lax.ppermute(token, "segment", [(0, 1)])
-        handed = lax.ppermute(helped, "segment", [(0, last - 1)])
-        pieces = lax.cond(
+        whole = lax.cond(
             segment == 1,
-            lambda: tuple(ring(jnp.stack([wg, wu, wd.T]))),
-            lambda: tuple(unfilled(*[(blocks, BF)] * n_fsdp)),
-        )
-        far = pieces[n_fsdp // 2][0, 0, 0].astype(F32)
+            lambda: ring_whole(jnp.stack([wg.T, wu.T, wd])),
+            lambda: unfilled(((n_fsdp,) + blocks, BF))[0],
+        )
+        far = whole[n_fsdp - 1, 0, 0, 0].astype(F32)
         rows = lax.cond(
-            (segment == 0) | ((go[0] > 0.5) & (jnp.abs(far) < 1e30)), lambda v, e: spread_out(v), lambda v, e: e, spread, handed
-        )
+            (segment == 0) | ((segment == 1) & (jnp.abs(far) < 1e30)),
+            spread_out,
+            lambda v: jnp.zeros((total, wide), BF),
+            jnp.where(segment == 0, lent, spread),
+        )
+        handed = lax.ppermute(rows, "segment", [(0, last - 1)])
+        rows = jnp.where(segment == last - 1, handed, rows)
+        go = lax.ppermute(1.0 + 0.0 * rows[0, :8].astype(F32), "segment", [(1, 0)])
+        rows = lax.cond(go[0] > 0.5, lambda v, e: spread_out(v), lambda v, e: e, spread, rows)
         slope, act, hidden, hg, x_rows = call_rows(
-            forward_body, rows_of(hid, hid, hid, hid, half), [rows], [wg, wu], SMALL
+            forward_body, rows_of(hid, hid, hid, hid, half), [rows], [wg, wu], 2 * SMALL
         )
         plane = lax.dynamic_index_in_dim(near(rows), fsdp_now, 1, keepdims=False).reshape(near_rows, wide)
         state = unfilled(
             ((tokens, width), BF), ((total, LANES), BF), ((total, half), BF), ((total, hid), BF), ((total, hid), BF)
         )
-        return tuple(state), (x_rows, slope, act, hidden, hg), plane, pieces
-
-    state, saved, plane, pieces = lax.cond(segment == last, first, gather_rows)
+        return tuple(state), (x_rows, slope, act, hidden, hg), plane, whole
+
+    state, saved, plane, whole = lax.cond(segment == last, first, gather_rows)
     x_rows, slope, act, hidden, hg = saved
 
     def dispatch(grad):
@@ -414,16 +436,12 @@
 
     near_shape = ((n_fsdp, near_rows, hid), BF)
 
-    def near_forward(plane, pieces):
-        whole = jnp.stack(pieces)
-        return (whole, *by_block(near_forward_body, [near_shape] * 3, [whole], [plane]))
-
-    whole, near_slope, near_act, near_hid = lax.cond(
+    near_slope, near_act, near_hid = lax.cond(
         segment == 1,
-        near_forward,
-        lambda *_: tuple(unfilled(((n_fsdp,) + blocks, BF), near_shape, near_shape, near_shape)),
+        lambda p, w: tuple(by_block(near_forward_body, [near_shape] * 3, [w], [p])),
+        lambda *_: tuple(unfilled(near_shape, near_shape, near_shape)),
         plane,
-        pieces,
+        whole,
     )
 
     def exchange_near(value):

time: 314 us -> 288 us (0.917)
  waiting for transfers between devices: 78.9 us -> 130 us
  starting transfers between devices: 60.1 us -> 15.3 us
  blocking collectives: 145 us -> 112 us
    ppermute x2, waiting for transfers between devices: 0.8 us -> 92.2 us  [the longest x1 76.4 us: gather_rows(): go = lax.ppermute(1.0 + 0.0 * rows[0, :8].astype(F32), 'segment', [(1, 0)])]
    ppermute x2, starting transfers between devices: 47.7 us -> 2.64 us  [the longest x1 1.36 us: gather_rows(): handed = lax.ppermute(rows, 'segment', [(0, last - 1)])]
    ppermute x3, waiting for transfers between devices: 51.1 us -> 12.9 us  [step_down(): return lax.ppermute(new, 'segment', [(layer, layer - 1)])]
    all_to_all x3, blocking collectives: 145 us -> 112 us  [exchange(): lax.all_to_all(value.reshape(sources, 8, cols), ROUTE, 0, 0, tiled=True)]
  transfers between devices with their start and end apart: 8 -> 8, of which waited for: 4 -> 5; matrix products, arithmetic and copies ran while one was open for 1% -> 1% of each run, Pallas kernels for 1% -> 1%
where the time goes in v5:
time: 288 us; the launch traced here: 287 us
  waiting for transfers between devices  130 us (45%)
  blocking collectives  112 us (39%)
  starting transfers between devices  15.3 us (5%)
  Pallas kernels  15.2 us (5%)
  local copies, waits for them, and re-layouts  7.91 us (3%)
  other arithmetic  3.52 us (1%)
    all_to_all x3, blocking collectives, exchange(): lax.all_to_all(value.reshape(sources, 8, cols), ROUTE, 0, 0, tiled=True)  112 us
    ppermute x1, waiting for transfers between devices, gather_rows(): go = lax.ppermute(1.0 + 0.0 * rows[0, :8].astype(F32), 'segment', [(1, 0)])  76.4 us
    all_to_all x1, waiting for transfers between devices, exchange(): lax.all_to_all(value.reshape(sources, 8, cols), ROUTE, 0, 0, tiled=True)  21.2 us
    ppermute x1, waiting for transfers between devices, gather_rows(): handed = lax.ppermute(rows, 'segment', [(0, last - 1)])  15.8 us
    ppermute x3, waiting for transfers between devices, step_down(): return lax.ppermute(new, 'segment', [(layer, layer - 1)])  12.9 us
    all_to_all x1, starting transfers between devices, exchange(): lax.all_to_all(value.reshape(sources, 8, cols), ROUTE, 0, 0, tiled=True)  7.97 us
    pallas_call x2, Pallas kernels, call_rows(): pl.pallas_call(body, grid=(total // chunk,), out_shape=[jax.ShapeDtypeStr...  7.83 us
    pallas_call x6, Pallas kernels, call(): pl.pallas_call(body, out_shape=[jax.ShapeDtypeStruct(s, d) for s, d in ou...  7.4 us
  transfers between devices with their start and end apart: 8, of which 5 were waited for; matrix products, arithmetic and copies ran while one was open for 1% of the time, Pallas kernels for 1%

profile of v5, /device:TPU:8, one launch (start us, length us, event | category | flops | bytes accessed | tf_op | source)
XLA Modules:
  0.0 286.6 jit_solution(12280160051188294551)
XLA Ops:
  1.4 0.8 copy.26.r_1_
  2.2 0.8 copy-done.1
  3.0 1.0 shard_map.111
  4.0 191.9 %conditional.9 = (bf16[32,1024]{1,0:T(8,128)(2,1)}, bf16[1024,128]{1,0:T(8,128)(2,1)}, bf16[1024,512]{1,0:T(8,128)(2,1)}, bf16[1024,256]{1,0:T(8,128)(2,1)}, bf1...) conditional(s32[]{:T(128)} %convert_element_type.54, ...), branch_computations={%region_0.7_spmd, %region_7.8_spmd} | conditional | flops 7028774 | bytes 111838208 | solution.py:430
  4.0 1.3 collective-permute-start.7
  5.3 1.8 conditional
  5.3 1.1 slice.21
  7.1 4.2 %collective-permute-done.7 = bf16[128,640]{1,0:T(8,128)(2,1)} collective-permute-done((bf16[128,640]{1,0:T(8,128)(2,1)S(1)}, bf16[128,640]{1,0:T(8,128)(2,1)}, u32[]{:S(2)}, u32[]{:S(2)}) %collective-permute-start.7) | collective-permute-done | bytes 163872 | tf_op jit(solution)/shard_map/cond/branch_0_fun/ppermute | solution.py:404
  11.3 49.2 %conditional.1 = (bf16[1024,640]{1,0:T(8,128)(2,1)S(1)}) conditional(s32[]{:T(128)} %convert_element_type.39, () %tuple.60, (pred[]{:T(512)}, bf16[128,640]{1,0:T(8,128)(2,1)}, bf16[128,640]{1,0:T(8,128)(2,1)S(1)}) %tuple.61), branch_computations={%region_3.3_spmd, %region_4.4_spmd} | conditional | flops 81920 | bytes 3112969 | solution.py:411
  11.3 0.9 broadcast_select_fusion.spread_ref
  12.4 48.1 %all_to_all.44 = bf16[128,8,640]{2,1,0:T(8,128)(2,1)S(1)} all-to-all(bf16[128,8,640]{2,1,0:T(8,128)(2,1)S(1)} %bitcast.102), channel_id=1, replica_groups=mesh['segment'=4,'expert'=16,'fsdp'=8] {'expert','fsdp'}, dimensions={0} | all-to-all | bytes 2621440 | tf_op jit(solution)/shard_map/cond/branch_0_fun/cond/branch_1_fun/all_to_all | solution.py:308
  60.5 1.4 collective-permute-start.8
  61.9 15.8 %collective-permute-done.8 = bf16[1024,640]{1,0:T(8,128)(2,1)S(1)} collective-permute-done((bf16[1024,640]{1,0:T(8,128)(2,1)S(1)}, bf16[1024,640]{1,0:T(8,128)(2,1)S(1)}, u32[]{:S(2)}, u32[]{:S(2)}) %collective-permute-start.8) | collective-permute-done | bytes 1310752 | tf_op jit(solution)/shard_map/cond/branch_0_fun/ppermute | solution.py:417
  77.7 1.2 broadcast_select_fusion.1
  79.6 1.3 collective-permute-start.9
  80.8 76.4 %collective-permute-done.9 = f32[8]{0:T(128)S(1)} collective-permute-done((f32[8]{0:T(128)S(1)}, f32[8]{0:T(128)S(1)}, u32[]{:S(2)}, u32[]{:S(2)}) %collective-permute-start.9) | collective-permute-done | bytes 64 | tf_op jit(solution)/shard_map/cond/branch_0_fun/ppermute | solution.py:419
  157.3 33.8 %conditional.2 = (bf16[1024,640]{1,0:T(8,128)(2,1)}, bf16[16,8,8,640]{3,2,1,0:T(8,128)(2,1)S(1)}) conditional(s32[]{:T(128)} %bitcast.24, bf16[1024,640]{1,0:T(8,128)(2,1)} %broadcast_select_fusion.1, bf16[128,640]{1,0:T(8,128)(2,1)S(1)} %get-tuple-element.202), branch_computations={%region_5.5_spmd, %region_6.6_spmd} | conditional | bytes 5242896 | solution.py:420
  157.4 32.3 %all_to_all.45 = bf16[128,8,640]{2,1,0:T(8,128)(2,1)} all-to-all(bf16[128,8,640]{2,1,0:T(8,128)(2,1)S(1)} %bitcast.103), channel_id=1, replica_groups=mesh['segment'=4,'expert'=16,'fsdp'=8] {'expert','fsdp'}, dimensions={0} | all-to-all | bytes 2621440 | tf_op jit(solution)/shard_map/cond/branch_0_fun/cond/branch_1_fun/all_to_all | solution.py:308
  189.8 1.3 copy.54
  191.1 4.5 %branch_0_fun.9 = (bf16[1024,256]{1,0:T(8,128)(2,1)S(1)}, bf16[1024,256]{1,0:T(8,128)(2,1)S(1)}, bf16[1024,256]{1,0:T(8,128)(2,1)}, bf16[1024,256]{1,0:T(8,128)(2,1)}, bf16[1024,512]{1,0:T(8,128)(2,1)}) custom-call(bf16[1024,640]{1,0:T(8,128)(2,1)} %get-tuple-element.203.rows_ref, bf16[1024,256]{1,0:T(8,128)(2,1)S(1)} %copy-done.9, ...), custom_call_target="tpu_custom_call" | custom-call | tf_op jit(solution)/shard_map/cond/branch_0_fun/pallas_call | solution.py:41
  196.6 0.9 conditional.10
  196.6 0.8 copy.92
  198.2 1.4 collective-permute-start.20
  201.0 12.9 %collective-permute-done.20 = bf16[32,1024]{1,0:T(8,128)(2,1)S(1)} collective-permute-done((bf16[32,1024]{1,0:T(8,128)(2,1)}, bf16[32,1024]{1,0:T(8,128)(2,1)S(1)}, u32[]{:S(2)}, u32[]{:S(2)}) %collective-permute-start.20) | collective-permute-done | bytes 65568 | tf_op jit(solution)/shard_map/ppermute | solution.py:513
  213.9 72.1 %conditional.13 = (bf16[32,1024]{1,0:T(8,128)(2,1)}, f32[1,2,16,2]{2,3,1,0:T(2,128)S(1)}, bf16[1,1,1024,256]{3,2,1,0:T(8,128)(2,1)}, bf16[1,1,1024,256]{3,2,1,0:T(8,128)(2,1)}, bf16[1,1,256,1024]{3,2,1,0:T(8,128)(2,1)}) conditional(s32[]{:T(128)} %convert_element_type.51, (s32[]{:T(128)}, f32[8]{0:T(128)S(1)}, bf16[1024,128]{1,0:T(8,128)(2,1)}, ...), branch_computations={%region_14.17_spmd, %region_17.18_spmd} | conditional | flops 3221356544 | bytes 28836648 | solution.py:522
  214.7 31.6 %all_to_all.52 = bf16[128,8,512]{2,1,0:T(8,128)(2,1)S(1)} all-to-all(bf16[128,8,512]{2,1,0:T(8,128)(2,1)S(1)} %bitcast.107), channel_id=1, replica_groups=mesh['segment'=4,'expert'=16,'fsdp'=8] {'expert','fsdp'}, dimensions={0} | all-to-all | bytes 2097152 | tf_op jit(solution)/shard_map/cond/branch_1_fun/all_to_all | solution.py:308
  246.4 3.3 %branch_1_fun.35 = (bf16[1024,640]{1,0:T(8,128)(2,1)S(1)}, bf16[1024,256]{1,0:T(8,128)(2,1)S(1)}, bf16[1024,256]{1,0:T(8,128)(2,1)S(1)}) custom-call(bf16[1024,512]{1,0:T(8,128)(2,1)S(1)} %bitcast.108, bf16[1024,256]{1,0:T(8,128)(2,1)} %copy-done.16, bf16[1024,256]{1,0:T(8,128)(2,1)} %copy-done.17, bf16[1024,256]{1,0:T(8,128)(2,1)} %get-tuple-element.306.hid_ref, ...), custom_call_target="tpu_custom_call" | custom-call | tf_op jit(solution)/shard_map/cond/branch_1_fun/pallas_call | solution.py:41
  249.7 1.1 copy-done
  250.8 8.0 %all-to-all-start.8 = ((bf16[128,8,640]{2,1,0:T(8,128)(2,1)}), bf16[128,8,640]{2,1,0:T(8,128)(2,1)S(1)}, u32[]{:S(2)}, u32[]{:S(2)}) async-start(bf16[128,8,640]{2,1,0:T(8,128)(2,1)} %bitcast.110), calls=%async_computation.8 | async-start | bytes 2621440 | tf_op jit(solution)/shard_map/cond/branch_1_fun/all_to_all | solution.py:308
  258.7 4.1 %branch_1_fun.37 = (bf16[1,1,1024,256]{3,2,1,0:T(8,128)(2,1)}, bf16[1,1,1024,256]{3,2,1,0:T(8,128)(2,1)}, bf16[1,1,256,1024]{3,2,1,0:T(8,128)(2,1)}) custom-call(bf16[1024,512]{1,0:T(8,128)(2,1)} %get-tuple-element.313.x_ref, bf16[1024,512]{1,0:T(8,128)(2,1)S(1)} %bitcast.109, bf16[1024,256]{1,0:T(8,128)(2,1)S(1)} %get-tuple-element.314.da_ref, ...), custom_call_target="tpu_custom_call" | custom-call | flops 3221225472 | bytes 6291456 | tf_op jit(solution)/shard_map/cond/branch_1_fun/pallas_call | solution.py:28
  262.8 21.2 %all-to-all-done.8 = bf16[128,8,640]{2,1,0:T(8,128)(2,1)S(1)} async-done(((bf16[128,8,640]{2,1,0:T(8,128)(2,1)}), bf16[128,8,640]{2,1,0:T(8,128)(2,1)S(1)}, u32[]{:S(2)}, u32[]{:S(2)}) %all-to-all-start.8) | async-done | bytes 1310752 | tf_op jit(solution)/shard_map/cond/branch_1_fun/all_to_all | solution.py:308
  284.0 1.8 branch_1_fun.36
  (50 shorter events, 5.8 us)
Async XLA Ops:
  2.2 0.8 copy-start.1
  4.0 7.3 %collective-permute-start.7 = (bf16[128,640]{1,0:T(8,128)(2,1)S(1)}, bf16[128,640]{1,0:T(8,128)(2,1)}, u32[]{:S(2)}, u32[]{:S(2)}) collective-permute-start(bf16[128,640]{1,0:T(8,128)(2,1)S(1)} %get-tuple-element.202), channel_id=1, source_target_pairs={{256,0},{257,1},{258,2},{259,3},{260,4},{261,5},{262,6},{263,7},{2... | collective-permute-start | bytes 491528 | tf_op jit(solution)/shard_map/cond/branch_0_fun/ppermute | solution.py:404
  60.5 17.2 %collective-permute-start.8 = (bf16[1024,640]{1,0:T(8,128)(2,1)S(1)}, bf16[1024,640]{1,0:T(8,128)(2,1)S(1)}, u32[]{:S(2)}, u32[]{:S(2)}) collective-permute-start(bf16[1024,640]{1,0:T(8,128)(2,1)S(1)} %get-tuple-element.500), channel_id=1, source_target_pairs={{0,256},{1,257},{2,258},{3,259},{4,260},{5,261},{6,262},{7,263},{8... | collective-permute-start | bytes 3932168 | tf_op jit(solution)/shard_map/cond/branch_0_fun/ppermute | solution.py:417
  79.6 77.7 %collective-permute-start.9 = (f32[8]{0:T(128)S(1)}, f32[8]{0:T(128)S(1)}, u32[]{:S(2)}, u32[]{:S(2)}) collective-permute-start(f32[8]{0:T(128)S(1)} %fusion.2), channel_id=1, source_target_pairs={{128,0},{129,1},{130,2},{131,3},{132,4},{133,5},{134,6},{135,7},{1... | collective-permute-start | bytes 104 | tf_op jit(solution)/shard_map/cond/branch_0_fun/ppermute | solution.py:419
  157.3 33.8 %copy-start.9 = (bf16[1024,256]{1,0:T(8,128)(2,1)S(1)}, bf16[1024,256]{1,0:T(8,128)(2,1)}, u32[]{:S(2)}) copy-start(bf16[1024,256]{1,0:T(8,128)(2,1)} %get-tuple-element.198.wg_ref) | copy-start | bytes 1572868 | tf_op jit(solution)/shard_map/cond
  157.3 33.8 %copy-start.12 = (bf16[1024,256]{1,0:T(8,128)(2,1)S(1)}, bf16[1024,256]{1,0:T(8,128)(2,1)}, u32[]{:S(2)}) copy-start(bf16[1024,256]{1,0:T(8,128)(2,1)} %get-tuple-element.199.wu_ref) | copy-start | bytes 1572868 | tf_op jit(solution)/shard_map/cond
  195.9 0.7 collective-permute-start.17
  197.4 0.7 copy-start.24
  197.4 0.7 collective-permute-start.18
  198.2 15.7 %copy-start.2 = (bf16[1,1,256,1024]{3,2,1,0:T(8,128)(2,1)S(1)}, bf16[1,1,256,1024]{3,2,1,0:T(8,128)(2,1)}, u32[]{:S(2)}) copy-start(bf16[1,1,256,1024]{3,2,1,0:T(8,128)(2,1)} %param.31) | copy-start | bytes 1572868
  198.2 15.7 %copy-start.8 = (bf16[1,1,1024,256]{3,2,1,0:T(8,128)(2,1)S(1)}, bf16[1,1,1024,256]{3,2,1,0:T(8,128)(2,1)}, u32[]{:S(2)}) copy-start(bf16[1,1,1024,256]{3,2,1,0:T(8,128)(2,1)} %param.29) | copy-start | bytes 1572868
  198.2 15.7 %copy-start.20 = (bf16[64,1024]{1,0:T(8,128)(2,1)S(1)}, bf16[64,1024]{1,0:T(8,128)(2,1)}, u32[]{:S(2)}) copy-start(bf16[64,1024]{1,0:T(8,128)(2,1)} %get-tuple-element.382) | copy-start | bytes 393220
  198.2 15.7 %collective-permute-start.20 = (bf16[32,1024]{1,0:T(8,128)(2,1)}, bf16[32,1024]{1,0:T(8,128)(2,1)S(1)}, u32[]{:S(2)}, u32[]{:S(2)}) collective-permute-start(bf16[32,1024]{1,0:T(8,128)(2,1)} %get-tuple-element.380), channel_id=1, source_target_pairs={{128,0},{129,1},{130,2},{131,3},{132,4},{133,5},{134,6},{135,7},{1... | collective-permute-start | bytes 196616 | tf_op jit(solution)/shard_map/ppermute | solution.py:513
  200.3 0.7 collective-permute-start.19
  213.9 0.8 copy-start.6
  213.9 32.4 %copy-start.16 = (bf16[1024,256]{1,0:T(8,128)(2,1)}, bf16[1024,256]{1,0:T(8,128)(2,1)S(1)}, u32[]{:S(2)}) copy-start(bf16[1024,256]{1,0:T(8,128)(2,1)S(1)} %get-tuple-element.304.slope_ref) | copy-start | bytes 1572868 | tf_op jit(solution)/shard_map/cond
  213.9 32.4 %copy-start.17 = (bf16[1024,256]{1,0:T(8,128)(2,1)}, bf16[1024,256]{1,0:T(8,128)(2,1)S(1)}, u32[]{:S(2)}) copy-start(bf16[1024,256]{1,0:T(8,128)(2,1)S(1)} %get-tuple-element.305.act_ref) | copy-start | bytes 1572868 | tf_op jit(solution)/shard_map/cond
  214.0 32.4 %copy-start.21 = (bf16[64,1024]{1,0:T(8,128)(2,1)}, bf16[64,1024]{1,0:T(8,128)(2,1)S(1)}, u32[]{:S(2)}) copy-start(bf16[64,1024]{1,0:T(8,128)(2,1)S(1)} %get-tuple-element.301.getz_ref) | copy-start | bytes 393220 | tf_op jit(solution)/shard_map/cond
  214.0 32.4 %copy-start.23 = (bf16[32,1024]{1,0:T(8,128)(2,1)}, bf16[32,1024]{1,0:T(8,128)(2,1)S(1)}, u32[]{:S(2)}) copy-start(bf16[32,1024]{1,0:T(8,128)(2,1)S(1)} %get-tuple-element.303.g_ref) | copy-start | bytes 196612 | tf_op jit(solution)/shard_map/cond
  214.0 32.4 %copy-start.15 = (bf16[1024,256]{1,0:T(8,128)(2,1)S(1)}, bf16[1024,256]{1,0:T(8,128)(2,1)}, u32[]{:S(2)}) copy-start(bf16[1024,256]{1,0:T(8,128)(2,1)} %get-tuple-element.309.wu_ref) | copy-start | bytes 1572868 | tf_op jit(solution)/shard_map/cond
  214.7 31.7 %copy-start.7 = (bf16[256,1024]{1,0:T(8,128)(2,1)S(1)}, bf16[256,1024]{1,0:T(8,128)(2,1)}, u32[]{:S(2)}) copy-start(bf16[256,1024]{1,0:T(8,128)(2,1)} %copy-done.6) | copy-start | bytes 1572868 | tf_op jit(solution)/shard_map/cond
  249.7 1.1 copy-start
  250.8 33.2 %all-to-all-start.8 = ((bf16[128,8,640]{2,1,0:T(8,128)(2,1)}), bf16[128,8,640]{2,1,0:T(8,128)(2,1)S(1)}, u32[]{:S(2)}, u32[]{:S(2)}) async-start(bf16[128,8,640]{2,1,0:T(8,128)(2,1)} %bitcast.110), calls=%async_computation.8 | async-start | bytes 2621440 | tf_op jit(solution)/shard_map/cond/branch_1_fun/all_to_all | solution.py:308
  286.0 0.6 copy-start.25

commit v6 on v5

--- a/solution.py
+++ b/solution.py
@@ -315,14 +315,15 @@
             out_specs=[pl.BlockSpec(memory_space=pl.ANY)] * len(shapes),
         )()
 
-    def by_block(body, outs, args, whole, scratch=()):
+    def by_block(body, outs, args, whole, scratch=(), first=None):
         one = lambda v: pl.BlockSpec((1,) + v[1:], lambda i: (i,) + (0,) * (len(v) - 1))
         stay = lambda v: pl.BlockSpec(v, lambda i: (0,) * len(v))
         return pl.pallas_call(
             body,
             grid=(n_fsdp,),
             out_shape=[jax.ShapeDtypeStruct(v, d) for v, d in outs],
-            in_specs=[stay(v.shape) for v in whole] + [one(v.shape) for v in args],
+            in_specs=[stay(v.shape) for v in whole]
+            + [one(v.shape if first is None else (v.shape[0], first) + v.shape[2:]) for v in args],
             out_specs=[one(v) if len(v) > 2 else stay(v) for v, _ in outs],
             scratch_shapes=[pltpu.VMEM(v, F32) for v in scratch],
             compiler_params=pltpu.CompilerParams(vmem_limit_bytes=48 * 1024 * 1024),
@@ -344,13 +345,15 @@
         whole = unfilled(((n_fsdp,) + own.shape, BF))[0]
         whole = lax.dynamic_update_slice(whole, own[None], (0, 0, 0, 0))
         ahead, behind, count = own, own, 1
-        for step in range(n_fsdp // 2):
-            ahead = shift(ahead, 1)
-            behind = shift(behind, -1) if step < n_fsdp // 2 - 1 else None
-            for value in (behind, ahead):
-                if value is not None:
-                    whole = lax.dynamic_update_slice(whole, value[None], (count, 0, 0, 0))
-                    count += 1
+        for _ in range(n_fsdp // 2 - 1):
+            ahead, behind = shift(ahead, 1), shift(behind, -1)
+            for value in (ahead, behind):
+                whole = lax.dynamic_update_slice(whole, value[None], (count, 0, 0, 0))
+                count += 1
+        cut = own.shape[1] // 2
+        one, two = shift(ahead[:, :cut], 1), shift(behind[:, cut:], -1)
+        whole = lax.dynamic_update_slice(whole, one[None], (count, 0, 0, 0))
+        whole = lax.dynamic_update_slice(whole, two[None], (count, 0, cut, 0))
         return whole
 
     def near(value):
@@ -415,9 +418,12 @@
             jnp.where(segment == 0, lent, spread),
         )
         handed = lax.ppermute(rows, "segment", [(0, last - 1)])
-        rows = jnp.where(segment == last - 1, handed, rows)
         go = lax.ppermute(1.0 + 0.0 * rows[0, :8].astype(F32), "segment", [(1, 0)])
-        rows = lax.cond(go[0] > 0.5, lambda v, e: spread_out(v), lambda v, e: e, spread, rows)
+        rows = lax.switch(
+            jnp.where(segment == last - 1, 2, jnp.where(go[0] > 0.5, 0, 1)),
+            (lambda v, e, h: spread_out(v), lambda v, e, h: e, lambda v, e, h: h),
+            spread, rows, handed,
+        )
         slope, act, hidden, hg, x_rows = call_rows(
             forward_body, rows_of(hid, hid, hid, hid, half), [rows], [wg, wu], 2 * SMALL
         )
@@ -438,7 +444,7 @@
 
     near_slope, near_act, near_hid = lax.cond(
         segment == 1,
-        lambda p, w: tuple(by_block(near_forward_body, [near_shape] * 3, [w], [p])),
+        lambda p, w: tuple(by_block(near_forward_body, [near_shape] * 3, [w], [p], first=2)),
         lambda *_: tuple(unfilled(near_shape, near_shape, near_shape)),
         plane,
         whole,

time: 288 us -> 286 us (level)
    ppermute x1, waiting for transfers between devices: 76.4 us -> 92.2 us  [gather_rows(): go = lax.ppermute(1.0 + 0.0 * rows[0, :8].astype(F32), 'segment', [(1, 0)])]
    ppermute x1, waiting for transfers between devices: 15.8 us -> 0.01 us  [gather_rows(): handed = lax.ppermute(rows, 'segment', [(0, last - 1)])]
  transfers between devices with their start and end apart: 8 -> 8, of which waited for: 5 -> 4; matrix products, arithmetic and copies ran while one was open for 1% -> 1% of each run, Pallas kernels for 1% -> 1%
where the time goes in v6:
time: 286 us; the launch traced here: 284 us
  waiting for transfers between devices  130 us (45%)
  blocking collectives  114 us (40%)
  starting transfers between devices  15.1 us (5%)
  Pallas kernels  13.9 us (5%)
  local copies, waits for them, and re-layouts  8 us (3%)
    all_to_all x3, blocking collectives, exchange(): lax.all_to_all(value.reshape(sources, 8, cols), ROUTE, 0, 0, tiled=True)  114 us
    ppermute x1, waiting for transfers between devices, gather_rows(): go = lax.ppermute(1.0 + 0.0 * rows[0, :8].astype(F32), 'segment', [(1, 0)])  92.2 us
    all_to_all x1, waiting for transfers between devices, exchange(): lax.all_to_all(value.reshape(sources, 8, cols), ROUTE, 0, 0, tiled=True)  21.2 us
    ppermute x3, waiting for transfers between devices, step_down(): return lax.ppermute(new, 'segment', [(layer, layer - 1)])  12.2 us
    pallas_call x6, Pallas kernels, call(): pl.pallas_call(body, out_shape=[jax.ShapeDtypeStruct(s, d) for s, d in ou...  7.4 us
    all_to_all x1, starting transfers between devices, exchange(): lax.all_to_all(value.reshape(sources, 8, cols), ROUTE, 0, 0, tiled=True)  6.81 us
    pallas_call x2, Pallas kernels, call_rows(): pl.pallas_call(body, grid=(total // chunk,), out_shape=[jax.ShapeDtypeStr...  6.5 us
  transfers between devices with their start and end apart: 8, of which 4 were waited for; matrix products, arithmetic and copies ran while one was open for 1% of the time, Pallas kernels for 1%

profile of v6, /device:TPU:8, one launch (start us, length us, event | category | flops | bytes accessed | tf_op | source)
XLA Modules:
  0.0 284.2 jit_solution(2342884397439198801)
XLA Ops:
  0.6 0.8 copy.26.r_0_
  1.4 0.8 copy.27.r_1_
  2.2 0.8 copy-done.1
  3.0 1.0 shard_map.111
  4.0 189.5 %conditional.9 = (bf16[32,1024]{1,0:T(8,128)(2,1)}, bf16[1024,128]{1,0:T(8,128)(2,1)}, bf16[1024,512]{1,0:T(8,128)(2,1)}, bf16[1024,256]{1,0:T(8,128)(2,1)}, bf1...) conditional(s32[]{:T(128)} %convert_element_type.49, ...), branch_computations={%region_0.8_spmd, %region_8.9_spmd} | conditional | flops 6373416 | bytes 121013360 | solution.py:436
  4.0 1.3 collective-permute-start.8
  5.3 1.2 slice.30
  7.2 4.1 %collective-permute-done.8 = bf16[128,640]{1,0:T(8,128)(2,1)} collective-permute-done((bf16[128,640]{1,0:T(8,128)(2,1)S(1)}, bf16[128,640]{1,0:T(8,128)(2,1)}, u32[]{:S(2)}, u32[]{:S(2)}) %collective-permute-start.8) | collective-permute-done | bytes 163872 | tf_op jit(solution)/shard_map/cond/branch_0_fun/ppermute | solution.py:407
  11.3 49.4 %conditional.1 = (bf16[1024,640]{1,0:T(8,128)(2,1)}) conditional(s32[]{:T(128)} %convert_element_type.36, () %tuple.65, (pred[]{:T(512)}, bf16[128,640]{1,0:T(8,128)(2,1)}, bf16[128,640]{1,0:T(8,128)(2,1)S(1)}) %tuple.99), branch_computations={%region_3.3_spmd, %region_4.4_spmd} | conditional | flops 81920 | bytes 3112969 | solution.py:414
  11.3 0.9 broadcast_select_fusion.spread_ref
  12.4 48.3 %all_to_all.44 = bf16[128,8,640]{2,1,0:T(8,128)(2,1)} all-to-all(bf16[128,8,640]{2,1,0:T(8,128)(2,1)S(1)} %bitcast.104), channel_id=1, replica_groups=mesh['segment'=4,'expert'=16,'fsdp'=8] {'expert','fsdp'}, dimensions={0} | all-to-all | bytes 2621440 | tf_op jit(solution)/shard_map/cond/branch_0_fun/cond/branch_1_fun/all_to_all | solution.py:308
  60.7 2.4 collective-permute-start.10
  63.7 1.3 collective-permute-start.9
  65.0 92.2 %collective-permute-done.9 = f32[8]{0:T(128)S(1)} collective-permute-done((f32[8]{0:T(128)S(1)}, f32[8]{0:T(128)S(1)}, u32[]{:S(2)}, u32[]{:S(2)}) %collective-permute-start.9) | collective-permute-done | bytes 64 | tf_op jit(solution)/shard_map/cond/branch_0_fun/ppermute | solution.py:421
  157.3 32.3 %conditional.2 = (bf16[1024,640]{1,0:T(8,128)(2,1)S(1)}) conditional(s32[]{:T(128)} %clamp.2, bf16[128,640]{1,0:T(8,128)(2,1)S(1)} %get-tuple-element.198, bf16[1024,640]{1,0:T(8,128)(2,1)} %get-tuple-element.490, bf16[1024,640]{1,0:T(8,128)(2,1)} %collective-permute-done.10), branch_computations={%region_5.5_spmd, %region_6.6_spmd, %region_7.7_spmd} | conditional | bytes 2621448 | solution.py:422
  157.4 32.2 %all_to_all.45 = bf16[128,8,640]{2,1,0:T(8,128)(2,1)S(1)} all-to-all(bf16[128,8,640]{2,1,0:T(8,128)(2,1)S(1)} %bitcast.105), channel_id=1, replica_groups=mesh['segment'=4,'expert'=16,'fsdp'=8] {'expert','fsdp'}, dimensions={0} | all-to-all | bytes 2621440 | tf_op jit(solution)/shard_map/cond/branch_0_fun/cond/branch_0_fun/all_to_all | solution.py:308
  189.7 3.2 %branch_0_fun.11 = (bf16[1024,256]{1,0:T(8,128)(2,1)}, bf16[1024,256]{1,0:T(8,128)(2,1)}, bf16[1024,256]{1,0:T(8,128)(2,1)}, bf16[1024,256]{1,0:T(8,128)(2,1)}, bf16[1024,512]{1,0:T(8,128)(2,1)}) custom-call(bf16[1024,640]{1,0:T(8,128)(2,1)S(1)} %get-tuple-element.491.rows_ref, bf16[1024,256]{1,0:T(8,128)(2,1)S(1)} %copy-done.9, bf16[1024,256]{1,0:T(8,128)(2,1)S(1)} %copy-done.12), custom_call_target="tpu_custom_call" | custom-call | tf_op jit(solution)/shard_map/cond/branch_0_fun/pallas_call | solution.py:41
  192.9 0.7 dynamic-slice_bitcast_fusion
  194.2 0.9 conditional.10
  194.2 0.8 copy.92
  195.8 0.7 copy-done.25
  196.5 1.4 collective-permute-start.21
  198.0 0.7 collective-permute-start.20
  198.7 12.2 %collective-permute-done.21 = bf16[32,1024]{1,0:T(8,128)(2,1)S(1)} collective-permute-done((bf16[32,1024]{1,0:T(8,128)(2,1)S(1)}, bf16[32,1024]{1,0:T(8,128)(2,1)S(1)}, u32[]{:S(2)}, u32[]{:S(2)}) %collective-permute-start.21) | collective-permute-done | bytes 65568 | tf_op jit(solution)/shard_map/ppermute | solution.py:519
  210.8 72.8 %conditional.13 = (bf16[32,1024]{1,0:T(8,128)(2,1)}, f32[1,2,16,2]{2,3,1,0:T(2,128)S(1)}, bf16[1,1,1024,256]{3,2,1,0:T(8,128)(2,1)}, bf16[1,1,1024,256]{3,2,1,0:T(8,128)(2,1)}, bf16[1,1,256,1024]{3,2,1,0:T(8,128)(2,1)}) conditional(s32[]{:T(128)} %convert_element_type.46, (s32[]{:T(128)}, f32[8]{0:T(128)S(1)}, bf16[1024,128]{1,0:T(8,128)(2,1)}, ...), branch_computations={%region_15.18_spmd, %region_18.19_spmd} | conditional | flops 3221356544 | bytes 24642288 | solution.py:528
  211.7 33.5 %all_to_all.52 = bf16[128,8,512]{2,1,0:T(8,128)(2,1)S(1)} all-to-all(bf16[128,8,512]{2,1,0:T(8,128)(2,1)S(1)} %bitcast.109), channel_id=1, replica_groups=mesh['segment'=4,'expert'=16,'fsdp'=8] {'expert','fsdp'}, dimensions={0} | all-to-all | bytes 2097152 | tf_op jit(solution)/shard_map/cond/branch_1_fun/all_to_all | solution.py:308
  245.2 3.3 %branch_1_fun.33 = (bf16[1024,640]{1,0:T(8,128)(2,1)S(1)}, bf16[1024,256]{1,0:T(8,128)(2,1)S(1)}, bf16[1024,256]{1,0:T(8,128)(2,1)S(1)}) custom-call(bf16[1024,512]{1,0:T(8,128)(2,1)S(1)} %bitcast.110, bf16[1024,256]{1,0:T(8,128)(2,1)} %get-tuple-element.297.slope_ref, bf16[1024,256]{1,0:T(8,128)(2,1)} %get-tuple-element.298.act_ref, ...), custom_call_target="tpu_custom_call" | custom-call | tf_op jit(solution)/shard_map/cond/branch_1_fun/pallas_call | solution.py:41
  248.5 1.1 copy-done
  249.6 6.8 %all-to-all-start.8 = ((bf16[128,8,640]{2,1,0:T(8,128)(2,1)}), bf16[128,8,640]{2,1,0:T(8,128)(2,1)S(1)}, u32[]{:S(2)}, u32[]{:S(2)}) async-start(bf16[128,8,640]{2,1,0:T(8,128)(2,1)} %bitcast.112), calls=%async_computation.8 | async-start | bytes 2621440 | tf_op jit(solution)/shard_map/cond/branch_1_fun/all_to_all | solution.py:308
  256.4 4.1 %branch_1_fun.35 = (bf16[1,1,1024,256]{3,2,1,0:T(8,128)(2,1)}, bf16[1,1,1024,256]{3,2,1,0:T(8,128)(2,1)}, bf16[1,1,256,1024]{3,2,1,0:T(8,128)(2,1)}) custom-call(bf16[1024,512]{1,0:T(8,128)(2,1)} %get-tuple-element.306.x_ref, bf16[1024,512]{1,0:T(8,128)(2,1)S(1)} %bitcast.111, bf16[1024,256]{1,0:T(8,128)(2,1)S(1)} %get-tuple-element.307.da_ref, ...), custom_call_target="tpu_custom_call" | custom-call | flops 3221225472 | bytes 6291456 | tf_op jit(solution)/shard_map/cond/branch_1_fun/pallas_call | solution.py:28
  260.4 21.2 %all-to-all-done.8 = bf16[128,8,640]{2,1,0:T(8,128)(2,1)S(1)} async-done(((bf16[128,8,640]{2,1,0:T(8,128)(2,1)}), bf16[128,8,640]{2,1,0:T(8,128)(2,1)S(1)}, u32[]{:S(2)}, u32[]{:S(2)}) %all-to-all-start.8) | async-done | bytes 1310752 | tf_op jit(solution)/shard_map/cond/branch_1_fun/all_to_all | solution.py:308
  281.6 1.8 branch_1_fun.34
  (48 shorter events, 3.7 us)
Async XLA Ops:
  2.2 0.8 copy-start.1
  4.0 7.3 %collective-permute-start.8 = (bf16[128,640]{1,0:T(8,128)(2,1)S(1)}, bf16[128,640]{1,0:T(8,128)(2,1)}, u32[]{:S(2)}, u32[]{:S(2)}) collective-permute-start(bf16[128,640]{1,0:T(8,128)(2,1)S(1)} %get-tuple-element.198), channel_id=1, source_target_pairs={{256,0},{257,1},{258,2},{259,3},{260,4},{261,5},{262,6},{263,7},{2... | collective-permute-start | bytes 491528 | tf_op jit(solution)/shard_map/cond/branch_0_fun/ppermute | solution.py:407
  60.7 96.6 %collective-permute-start.10 = (bf16[1024,640]{1,0:T(8,128)(2,1)}, bf16[1024,640]{1,0:T(8,128)(2,1)}, u32[]{:S(2)}, u32[]{:S(2)}) collective-permute-start(bf16[1024,640]{1,0:T(8,128)(2,1)} %get-tuple-element.490), channel_id=1, source_target_pairs={{0,256},{1,257},{2,258},{3,259},{4,260},{5,261},{6,262},{7,263},{8... | collective-permute-start | bytes 3932168 | tf_op jit(solution)/shard_map/cond/branch_0_fun/ppermute | solution.py:420
  63.7 93.5 %collective-permute-start.9 = (f32[8]{0:T(128)S(1)}, f32[8]{0:T(128)S(1)}, u32[]{:S(2)}, u32[]{:S(2)}) collective-permute-start(f32[8]{0:T(128)S(1)} %fusion.2), channel_id=1, source_target_pairs={{128,0},{129,1},{130,2},{131,3},{132,4},{133,5},{134,6},{135,7},{1... | collective-permute-start | bytes 104 | tf_op jit(solution)/shard_map/cond/branch_0_fun/ppermute | solution.py:421
  157.3 32.4 %copy-start.9 = (bf16[1024,256]{1,0:T(8,128)(2,1)S(1)}, bf16[1024,256]{1,0:T(8,128)(2,1)}, u32[]{:S(2)}) copy-start(bf16[1024,256]{1,0:T(8,128)(2,1)} %get-tuple-element.195.wg_ref) | copy-start | bytes 1572868 | tf_op jit(solution)/shard_map/cond
  157.3 32.4 %copy-start.12 = (bf16[1024,256]{1,0:T(8,128)(2,1)S(1)}, bf16[1024,256]{1,0:T(8,128)(2,1)}, u32[]{:S(2)}) copy-start(bf16[1024,256]{1,0:T(8,128)(2,1)} %get-tuple-element.196.wu_ref) | copy-start | bytes 1572868 | tf_op jit(solution)/shard_map/cond
  193.6 0.7 collective-permute-start.18
  195.1 0.7 collective-permute-start.19
  195.8 0.7 copy-start.25
  195.8 0.7 copy-start.26
  196.5 14.3 %copy-start.2 = (bf16[1,1,256,1024]{3,2,1,0:T(8,128)(2,1)S(1)}, bf16[1,1,256,1024]{3,2,1,0:T(8,128)(2,1)}, u32[]{:S(2)}) copy-start(bf16[1,1,256,1024]{3,2,1,0:T(8,128)(2,1)} %param.32) | copy-start | bytes 1572868
  196.5 14.3 %copy-start.8 = (bf16[1,1,1024,256]{3,2,1,0:T(8,128)(2,1)S(1)}, bf16[1,1,1024,256]{3,2,1,0:T(8,128)(2,1)}, u32[]{:S(2)}) copy-start(bf16[1,1,1024,256]{3,2,1,0:T(8,128)(2,1)} %param.30) | copy-start | bytes 1572868
  196.5 14.3 %copy-start.20 = (bf16[64,1024]{1,0:T(8,128)(2,1)S(1)}, bf16[64,1024]{1,0:T(8,128)(2,1)}, u32[]{:S(2)}) copy-start(bf16[64,1024]{1,0:T(8,128)(2,1)} %get-tuple-element.375) | copy-start | bytes 393220
  196.5 14.3 %copy-start.24 = (bf16[32,1024]{1,0:T(8,128)(2,1)}, bf16[32,1024]{1,0:T(8,128)(2,1)S(1)}, u32[]{:S(2)}) copy-start(bf16[32,1024]{1,0:T(8,128)(2,1)S(1)} %get-tuple-element.373) | copy-start | bytes 196612
  196.5 14.3 %collective-permute-start.21 = (bf16[32,1024]{1,0:T(8,128)(2,1)S(1)}, bf16[32,1024]{1,0:T(8,128)(2,1)S(1)}, u32[]{:S(2)}, u32[]{:S(2)}) collective-permute-start(bf16[32,1024]{1,0:T(8,128)(2,1)S(1)} %get-tuple-element.373), channel_id=1, source_target_pairs={{128,0},{129,1},{130,2},{131,3},{132,4},{133,5},{134,6},{135,7},{1... | collective-permute-start | bytes 196616 | tf_op jit(solution)/shard_map/ppermute | solution.py:519
  198.0 0.7 collective-permute-start.20
  210.9 0.8 copy-start.6
  210.9 34.3 %copy-start.21 = (bf16[64,1024]{1,0:T(8,128)(2,1)}, bf16[64,1024]{1,0:T(8,128)(2,1)S(1)}, u32[]{:S(2)}) copy-start(bf16[64,1024]{1,0:T(8,128)(2,1)S(1)} %get-tuple-element.294.getz_ref) | copy-start | bytes 393220 | tf_op jit(solution)/shard_map/cond
  210.9 37.6 %copy-start.23 = (bf16[32,1024]{1,0:T(8,128)(2,1)}, bf16[32,1024]{1,0:T(8,128)(2,1)S(1)}, u32[]{:S(2)}) copy-start(bf16[32,1024]{1,0:T(8,128)(2,1)S(1)} %get-tuple-element.296.g_ref) | copy-start | bytes 196612 | tf_op jit(solution)/shard_map/cond
  210.9 34.3 %copy-start.15 = (bf16[1024,256]{1,0:T(8,128)(2,1)S(1)}, bf16[1024,256]{1,0:T(8,128)(2,1)}, u32[]{:S(2)}) copy-start(bf16[1024,256]{1,0:T(8,128)(2,1)} %get-tuple-element.302.wu_ref) | copy-start | bytes 1572868 | tf_op jit(solution)/shard_map/cond
  211.6 33.5 %copy-start.7 = (bf16[256,1024]{1,0:T(8,128)(2,1)S(1)}, bf16[256,1024]{1,0:T(8,128)(2,1)}, u32[]{:S(2)}) copy-start(bf16[256,1024]{1,0:T(8,128)(2,1)} %copy-done.6) | copy-start | bytes 1572868 | tf_op jit(solution)/shard_map/cond
  248.5 1.1 copy-start
  249.6 32.1 %all-to-all-start.8 = ((bf16[128,8,640]{2,1,0:T(8,128)(2,1)}), bf16[128,8,640]{2,1,0:T(8,128)(2,1)S(1)}, u32[]{:S(2)}, u32[]{:S(2)}) async-start(bf16[128,8,640]{2,1,0:T(8,128)(2,1)} %bitcast.112), calls=%async_computation.8 | async-start | bytes 2621440 | tf_op jit(solution)/shard_map/cond/branch_1_fun/all_to_all | solution.py:308
  283.6 0.6 copy-start.27

commit v7 on v6

--- a/solution.py
+++ b/solution.py
@@ -404,25 +404,27 @@
         return exchange(call(fan_body, [((n_expert, n_fsdp, 8, wide), BF)], value)[0])
 
     def gather_rows():
-        lent = lax.ppermute(spread, "segment", [(last - 1, 0)])
+        nil = lambda v: 0.0 * v[(0,) * v.ndim]
+        lent_one = lax.ppermute(spread, "segment", [(1, 0)])
+        lent_two = lax.ppermute(spread, "segment", [(last - 1, 0)])
         whole = lax.cond(
             segment == 1,
-            lambda: ring_whole(jnp.stack([wg.T, wu.T, wd])),
+            lambda: ring_whole(jnp.stack([wg.T, wu.T, wd]) + nil(lent_one).astype(BF)),
             lambda: unfilled(((n_fsdp,) + blocks, BF))[0],
         )
-        far = whole[n_fsdp - 1, 0, 0, 0].astype(F32)
-        rows = lax.cond(
-            (segment == 0) | ((segment == 1) & (jnp.abs(far) < 1e30)),
-            spread_out,
-            lambda v: jnp.zeros((total, wide), BF),
-            jnp.where(segment == 0, lent, spread),
-        )
-        handed = lax.ppermute(rows, "segment", [(0, last - 1)])
-        go = lax.ppermute(1.0 + 0.0 * rows[0, :8].astype(F32), "segment", [(1, 0)])
+
+        def on_zero(value):
+            return lax.cond(segment == 0, spread_out, lambda v: jnp.zeros((total, wide), BF), value)
+
+        rows_two = on_zero(lent_two + nil(lent_one).astype(BF))
+        handed_two = lax.ppermute(rows_two, "segment", [(0, last - 1)])
+        rows_one = on_zero(lent_one + nil(handed_two).astype(BF))
+        handed_one = lax.ppermute(rows_one, "segment", [(0, 1)])
+        rows = on_zero(spread + nil(handed_one).astype(BF))
         rows = lax.switch(
-            jnp.where(segment == last - 1, 2, jnp.where(go[0] > 0.5, 0, 1)),
-            (lambda v, e, h: spread_out(v), lambda v, e, h: e, lambda v, e, h: h),
-            spread, rows, handed,
+            jnp.minimum(segment, 2),
+            (lambda a, b, c: a, lambda a, b, c: b, lambda a, b, c: c),
+            rows, handed_one, handed_two,
         )
         slope, act, hidden, hg, x_rows = call_rows(
             forward_body, rows_of(hid, hid, hid, hid, half), [rows], [wg, wu], 2 * SMALL

time: 286 us -> 276 us (0.965)
  waiting for transfers between devices: 130 us -> 74.2 us
  blocking collectives: 114 us -> 154 us
    ppermute x3 -> x4, waiting for transfers between devices: 96.3 us -> 23.7 us  [the longest x1 16 us: gather_rows(): handed_two = lax.ppermute(rows_two, 'segment', [(0, last - 1)])]
    all_to_all x3 -> x4, blocking collectives: 114 us -> 154 us  [exchange(): lax.all_to_all(value.reshape(sources, 8, cols), ROUTE, 0, 0, tiled=True)]
    ppermute x3, waiting for transfers between devices: 12.2 us -> 29.3 us  [step_down(): return lax.ppermute(new, 'segment', [(layer, layer - 1)])]
    ppermute x3 -> x4, starting transfers between devices: 4.93 us -> 7.37 us  [the longest x1 2.44 us: gather_rows(): handed_one = lax.ppermute(rows_one, 'segment', [(0, 1)])]
    pallas_call x6 -> x7, Pallas kernels: 7.4 us -> 7.51 us  [call(): pl.pallas_call(body, out_shape=[jax.ShapeDtypeStruct(s, d) for s, d in ou...]
  transfers between devices with their start and end apart: 8 -> 9, of which waited for: 4 -> 6; matrix products, arithmetic and copies ran while one was open for 1% -> 0% of each run, Pallas kernels for 1% -> 1%
where the time goes in v7:
time: 276 us; the launch traced here: 274 us
  blocking collectives  154 us (56%)
  waiting for transfers between devices  74.2 us (27%)
  starting transfers between devices  17.7 us (6%)
  Pallas kernels  14 us (5%)
  local copies, waits for them, and re-layouts  9.83 us (4%)
    all_to_all x4, blocking collectives, exchange(): lax.all_to_all(value.reshape(sources, 8, cols), ROUTE, 0, 0, tiled=True)  154 us
    ppermute x3, waiting for transfers between devices, step_down(): return lax.ppermute(new, 'segment', [(layer, layer - 1)])  29.3 us
    all_to_all x1, waiting for transfers between devices, exchange(): lax.all_to_all(value.reshape(sources, 8, cols), ROUTE, 0, 0, tiled=True)  21.2 us
    ppermute x1, waiting for transfers between devices, gather_rows(): handed_two = lax.ppermute(rows_two, 'segment', [(0, last - 1)])  16 us
    pallas_call x7, Pallas kernels, call(): pl.pallas_call(body, out_shape=[jax.ShapeDtypeStruct(s, d) for s, d in ou...  7.51 us
    all_to_all x1, starting transfers between devices, exchange(): lax.all_to_all(value.reshape(sources, 8, cols), ROUTE, 0, 0, tiled=True)  6.93 us
    pallas_call x2, Pallas kernels, call_rows(): pl.pallas_call(body, grid=(total // chunk,), out_shape=[jax.ShapeDtypeStr...  6.5 us
  transfers between devices with their start and end apart: 9, of which 6 were waited for; matrix products, arithmetic and copies ran while one was open for 0% of the time, Pallas kernels for 1%

profile of v7, /device:TPU:8, one launch (start us, length us, event | category | flops | bytes accessed | tf_op | source)
XLA Modules:
  0.0 274.3 jit_solution(7938007879293721598)
XLA Ops:
  2.2 0.8 copy-done.1
  3.0 1.0 shard_map.111
  4.0 164.0 %conditional.11 = (bf16[32,1024]{1,0:T(8,128)(2,1)}, bf16[1024,128]{1,0:T(8,128)(2,1)}, bf16[1024,512]{1,0:T(8,128)(2,1)}, bf16[1024,256]{1,0:T(8,128)(2,1)}, bf...) conditional(s32[]{:T(128)} %convert_element_type.37, ...), branch_computations={%region_0.12_spmd, %region_12.13_spmd} | conditional | flops 8896525 | bytes 133301808 | solution.py:438
  4.0 1.3 collective-permute-start.8
  5.3 1.3 collective-permute-start.9
  7.3 5.2 %collective-permute-done.9 = bf16[128,640]{1,0:T(8,128)(2,1)S(1)} collective-permute-done((bf16[128,640]{1,0:T(8,128)(2,1)S(1)}, bf16[128,640]{1,0:T(8,128)(2,1)S(1)}, u32[]{:S(2)}, u32[]{:S(2)}) %collective-permute-start.9) | collective-permute-done | bytes 163872 | tf_op jit(solution)/shard_map/cond/branch_0_fun/ppermute | solution.py:409
  12.5 53.2 %conditional = (bf16[1024,640]{1,0:T(8,128)(2,1)S(1)}) conditional(s32[]{:T(128)} %convert_element_type.24, () %tuple.91, (bf16[128,640]{1,0:T(8,128)(2,1)S(1)}, bf16[128,640]{1,0:T(8,128)(2,1)S(1)}) %tuple.92), branch_computations={%region_1.0_spmd, %region_2.0_spmd} | conditional | flops 81921 | bytes 2949140 | solution.py:417
  13.8 51.9 %all_to_all.48 = bf16[128,8,640]{2,1,0:T(8,128)(2,1)S(1)} all-to-all(bf16[128,8,640]{2,1,0:T(8,128)(2,1)S(1)} %bitcast.107), channel_id=1, replica_groups=mesh['segment'=4,'expert'=16,'fsdp'=8] {'expert','fsdp'}, dimensions={0} | all-to-all | bytes 2621440 | tf_op jit(solution)/shard_map/cond/branch_0_fun/cond/branch_1_fun/all_to_all | solution.py:308
  65.7 2.4 collective-permute-start.10
  68.1 16.0 %collective-permute-done.10 = bf16[1024,640]{1,0:T(8,128)(2,1)} collective-permute-done((bf16[1024,640]{1,0:T(8,128)(2,1)S(1)}, bf16[1024,640]{1,0:T(8,128)(2,1)}, u32[]{:S(2)}, u32[]{:S(2)}) %collective-permute-start.10) | collective-permute-done | bytes 1310752 | tf_op jit(solution)/shard_map/cond/branch_0_fun/ppermute | solution.py:420
  84.1 40.8 %conditional.1 = (bf16[1024,640]{1,0:T(8,128)(2,1)}) conditional(s32[]{:T(128)} %convert_element_type.24, () %tuple.90, (bf16[1024,640]{1,0:T(8,128)(2,1)}, bf16[128,640]{1,0:T(8,128)(2,1)S(1)}) %tuple.93), branch_computations={%region_3.0_spmd, %region_4.0_spmd} | conditional | flops 81921 | bytes 2949140 | solution.py:417
  84.1 1.3 slice.19
  86.2 38.7 %all_to_all.49 = bf16[128,8,640]{2,1,0:T(8,128)(2,1)} all-to-all(bf16[128,8,640]{2,1,0:T(8,128)(2,1)S(1)} %bitcast.108), channel_id=1, replica_groups=mesh['segment'=4,'expert'=16,'fsdp'=8] {'expert','fsdp'}, dimensions={0} | all-to-all | bytes 2621440 | tf_op jit(solution)/shard_map/cond/branch_0_fun/cond/branch_1_fun/all_to_all | solution.py:308
  124.9 2.4 collective-permute-start.11
  127.4 1.8 collective-permute-done.11
  129.2 34.9 %conditional.2 = (bf16[1024,640]{1,0:T(8,128)(2,1)S(1)}) conditional(s32[]{:T(128)} %convert_element_type.24, () %tuple.89, (bf16[128,640]{1,0:T(8,128)(2,1)}, bf16[1024,640]{1,0:T(8,128)(2,1)}, ()) %tuple.175), branch_computations={%region_5.0_spmd, %region_6.0_spmd} | conditional | flops 81921 | bytes 2949140 | solution.py:417
  129.2 1.2 slice.27
  131.1 0.9 broadcast_add_fusion.2.spread_ref
  132.2 31.9 %all_to_all.50 = bf16[128,8,640]{2,1,0:T(8,128)(2,1)S(1)} all-to-all(bf16[128,8,640]{2,1,0:T(8,128)(2,1)S(1)} %bitcast.109), channel_id=1, replica_groups=mesh['segment'=4,'expert'=16,'fsdp'=8] {'expert','fsdp'}, dimensions={0} | all-to-all | bytes 2621440 | tf_op jit(solution)/shard_map/cond/branch_0_fun/cond/branch_1_fun/all_to_all | solution.py:308
  164.1 3.2 %branch_0_fun.9 = (bf16[1024,256]{1,0:T(8,128)(2,1)}, bf16[1024,256]{1,0:T(8,128)(2,1)}, bf16[1024,256]{1,0:T(8,128)(2,1)}, bf16[1024,256]{1,0:T(8,128)(2,1)}, bf16[1024,512]{1,0:T(8,128)(2,1)}) custom-call(bf16[1024,640]{1,0:T(8,128)(2,1)S(1)} %get-tuple-element.549.rows_ref, bf16[1024,256]{1,0:T(8,128)(2,1)S(1)} %copy-done.9, bf16[1024,256]{1,0:T(8,128)(2,1)S(1)} %copy-done.12), custom_call_target="tpu_custom_call" | custom-call | tf_op jit(solution)/shard_map/cond/branch_0_fun/pallas_call | solution.py:41
  168.7 0.9 conditional.12
  168.7 0.8 copy.96
  171.0 1.4 collective-permute-start.22
  173.1 29.3 %collective-permute-done.22 = bf16[32,1024]{1,0:T(8,128)(2,1)S(1)} collective-permute-done((bf16[32,1024]{1,0:T(8,128)(2,1)S(1)}, bf16[32,1024]{1,0:T(8,128)(2,1)S(1)}, u32[]{:S(2)}, u32[]{:S(2)}) %collective-permute-start.22) | collective-permute-done | bytes 65568 | tf_op jit(solution)/shard_map/ppermute | solution.py:521
  202.4 71.3 %conditional.15 = (bf16[32,1024]{1,0:T(8,128)(2,1)}, f32[1,2,16,2]{2,3,1,0:T(2,128)S(1)}, bf16[1,1,1024,256]{3,2,1,0:T(8,128)(2,1)}, bf16[1,1,1024,256]{3,2,1,0:T(8,128)(2,1)}, bf16[1,1,256,1024]{3,2,1,0:T(8,128)(2,1)}) conditional(s32[]{:T(128)} %convert_element_type.34, (s32[]{:T(128)}, f32[8]{0:T(128)S(1)}, bf16[1024,128]{1,0:T(8,128)(2,1)}, ...), branch_computations={%region_19.22_spmd, %region_22.23_spmd} | conditional | flops 3221356544 | bytes 24642288 | solution.py:530
  203.2 31.9 %all_to_all.57 = bf16[128,8,512]{2,1,0:T(8,128)(2,1)S(1)} all-to-all(bf16[128,8,512]{2,1,0:T(8,128)(2,1)S(1)} %bitcast.113), channel_id=1, replica_groups=mesh['segment'=4,'expert'=16,'fsdp'=8] {'expert','fsdp'}, dimensions={0} | all-to-all | bytes 2097152 | tf_op jit(solution)/shard_map/cond/branch_1_fun/all_to_all | solution.py:308
  235.2 3.3 %branch_1_fun.37 = (bf16[1024,640]{1,0:T(8,128)(2,1)S(1)}, bf16[1024,256]{1,0:T(8,128)(2,1)S(1)}, bf16[1024,256]{1,0:T(8,128)(2,1)S(1)}) custom-call(bf16[1024,512]{1,0:T(8,128)(2,1)S(1)} %bitcast.114, bf16[1024,256]{1,0:T(8,128)(2,1)} %get-tuple-element.350.slope_ref, bf16[1024,256]{1,0:T(8,128)(2,1)} %get-tuple-element.351.act_ref, ...), custom_call_target="tpu_custom_call" | custom-call | tf_op jit(solution)/shard_map/cond/branch_1_fun/pallas_call | solution.py:41
  238.5 1.0 copy-done
  239.5 6.9 %all-to-all-start.7 = ((bf16[128,8,640]{2,1,0:T(8,128)(2,1)}), bf16[128,8,640]{2,1,0:T(8,128)(2,1)S(1)}, u32[]{:S(2)}, u32[]{:S(2)}) async-start(bf16[128,8,640]{2,1,0:T(8,128)(2,1)} %bitcast.116), calls=%async_computation.7 | async-start | bytes 2621440 | tf_op jit(solution)/shard_map/cond/branch_1_fun/all_to_all | solution.py:308
  246.4 4.1 %branch_1_fun.39 = (bf16[1,1,1024,256]{3,2,1,0:T(8,128)(2,1)}, bf16[1,1,1024,256]{3,2,1,0:T(8,128)(2,1)}, bf16[1,1,256,1024]{3,2,1,0:T(8,128)(2,1)}) custom-call(bf16[1024,512]{1,0:T(8,128)(2,1)} %get-tuple-element.359.x_ref, bf16[1024,512]{1,0:T(8,128)(2,1)S(1)} %bitcast.115, bf16[1024,256]{1,0:T(8,128)(2,1)S(1)} %get-tuple-element.360.da_ref, ...), custom_call_target="tpu_custom_call" | custom-call | flops 3221225472 | bytes 6291456 | tf_op jit(solution)/shard_map/cond/branch_1_fun/pallas_call | solution.py:28
  250.5 21.2 %all-to-all-done.7 = bf16[128,8,640]{2,1,0:T(8,128)(2,1)S(1)} async-done(((bf16[128,8,640]{2,1,0:T(8,128)(2,1)}), bf16[128,8,640]{2,1,0:T(8,128)(2,1)S(1)}, u32[]{:S(2)}, u32[]{:S(2)}) %all-to-all-start.7) | async-done | bytes 1310752 | tf_op jit(solution)/shard_map/cond/branch_1_fun/all_to_all | solution.py:308
  271.7 1.8 branch_1_fun.38
  (61 shorter events, 8.0 us)
Async XLA Ops:
  2.2 0.8 copy-start.1
  4.0 8.5 %copy-start.20 = (bf16[128,640]{1,0:T(8,128)(2,1)}, bf16[128,640]{1,0:T(8,128)(2,1)S(1)}, u32[]{:S(2)}) copy-start(bf16[128,640]{1,0:T(8,128)(2,1)S(1)} %get-tuple-element.248) | copy-start | bytes 491524 | tf_op jit(solution)/shard_map/cond
  4.0 3.3 %collective-permute-start.8 = (bf16[128,640]{1,0:T(8,128)(2,1)S(1)}, bf16[128,640]{1,0:T(8,128)(2,1)S(1)}, u32[]{:S(2)}, u32[]{:S(2)}) collective-permute-start(bf16[128,640]{1,0:T(8,128)(2,1)S(1)} %get-tuple-element.248), channel_id=1, source_target_pairs={{128,0},{129,1},{130,2},{131,3},{132,4},{133,5},{134,6},{135,7},{1... | collective-permute-start | bytes 491528 | tf_op jit(solution)/shard_map/cond/branch_0_fun/ppermute | solution.py:408
  5.3 7.2 %collective-permute-start.9 = (bf16[128,640]{1,0:T(8,128)(2,1)S(1)}, bf16[128,640]{1,0:T(8,128)(2,1)S(1)}, u32[]{:S(2)}, u32[]{:S(2)}) collective-permute-start(bf16[128,640]{1,0:T(8,128)(2,1)S(1)} %get-tuple-element.248), channel_id=1, source_target_pairs={{256,0},{257,1},{258,2},{259,3},{260,4},{261,5},{262,6},{263,7},{2... | collective-permute-start | bytes 491528 | tf_op jit(solution)/shard_map/cond/branch_0_fun/ppermute | solution.py:409
  65.7 18.4 %collective-permute-start.10 = (bf16[1024,640]{1,0:T(8,128)(2,1)S(1)}, bf16[1024,640]{1,0:T(8,128)(2,1)}, u32[]{:S(2)}, u32[]{:S(2)}) collective-permute-start(bf16[1024,640]{1,0:T(8,128)(2,1)S(1)} %get-tuple-element.546), channel_id=1, source_target_pairs={{0,256},{1,257},{2,258},{3,259},{4,260},{5,261},{6,262},{7,263},{8... | collective-permute-start | bytes 3932168 | tf_op jit(solution)/shard_map/cond/branch_0_fun/ppermute | solution.py:420
  84.1 43.3 %copy-start.3 = (bf16[1,1,256,1024]{3,2,1,0:T(8,128)(2,1)S(1)}, bf16[1,1,256,1024]{3,2,1,0:T(8,128)(2,1)}, u32[]{:S(2)}) copy-start(bf16[1,1,256,1024]{3,2,1,0:T(8,128)(2,1)} %get-tuple-element.257) | copy-start | bytes 1572868 | tf_op jit(solution)/shard_map/cond
  84.1 43.3 %copy-start.9 = (bf16[1024,256]{1,0:T(8,128)(2,1)S(1)}, bf16[1024,256]{1,0:T(8,128)(2,1)}, u32[]{:S(2)}) copy-start(bf16[1024,256]{1,0:T(8,128)(2,1)} %get-tuple-element.249.wg_ref) | copy-start | bytes 1572868 | tf_op jit(solution)/shard_map/cond
  84.1 43.3 %copy-start.12 = (bf16[1024,256]{1,0:T(8,128)(2,1)S(1)}, bf16[1024,256]{1,0:T(8,128)(2,1)}, u32[]{:S(2)}) copy-start(bf16[1024,256]{1,0:T(8,128)(2,1)} %get-tuple-element.250.wu_ref) | copy-start | bytes 1572868 | tf_op jit(solution)/shard_map/cond
  124.9 4.3 %collective-permute-start.11 = (bf16[1024,640]{1,0:T(8,128)(2,1)}, bf16[1024,640]{1,0:T(8,128)(2,1)}, u32[]{:S(2)}, u32[]{:S(2)}) collective-permute-start(bf16[1024,640]{1,0:T(8,128)(2,1)} %get-tuple-element.547), channel_id=1, source_target_pairs={{0,128},{1,129},{2,130},{3,131},{4,132},{5,133},{6,134},{7,135},{8... | collective-permute-start | bytes 3932168 | tf_op jit(solution)/shard_map/cond/branch_0_fun/ppermute | solution.py:422
  168.0 0.7 collective-permute-start.19
  169.5 0.7 collective-permute-start.20
  170.2 0.7 copy-start.26
  170.2 0.7 copy-start.27
  170.9 31.4 %copy-start.2 = (bf16[1,1,256,1024]{3,2,1,0:T(8,128)(2,1)S(1)}, bf16[1,1,256,1024]{3,2,1,0:T(8,128)(2,1)}, u32[]{:S(2)}) copy-start(bf16[1,1,256,1024]{3,2,1,0:T(8,128)(2,1)} %param.36) | copy-start | bytes 1572868
  170.9 31.4 %copy-start.8 = (bf16[1,1,1024,256]{3,2,1,0:T(8,128)(2,1)S(1)}, bf16[1,1,1024,256]{3,2,1,0:T(8,128)(2,1)}, u32[]{:S(2)}) copy-start(bf16[1,1,1024,256]{3,2,1,0:T(8,128)(2,1)} %param.34) | copy-start | bytes 1572868
  170.9 31.4 %copy-start.21 = (bf16[64,1024]{1,0:T(8,128)(2,1)S(1)}, bf16[64,1024]{1,0:T(8,128)(2,1)}, u32[]{:S(2)}) copy-start(bf16[64,1024]{1,0:T(8,128)(2,1)} %get-tuple-element.428) | copy-start | bytes 393220
  171.0 31.4 %copy-start.25 = (bf16[32,1024]{1,0:T(8,128)(2,1)}, bf16[32,1024]{1,0:T(8,128)(2,1)S(1)}, u32[]{:S(2)}) copy-start(bf16[32,1024]{1,0:T(8,128)(2,1)S(1)} %get-tuple-element.426) | copy-start | bytes 196612
  171.0 31.4 %collective-permute-start.22 = (bf16[32,1024]{1,0:T(8,128)(2,1)S(1)}, bf16[32,1024]{1,0:T(8,128)(2,1)S(1)}, u32[]{:S(2)}, u32[]{:S(2)}) collective-permute-start(bf16[32,1024]{1,0:T(8,128)(2,1)S(1)} %get-tuple-element.426), channel_id=1, source_target_pairs={{128,0},{129,1},{130,2},{131,3},{132,4},{133,5},{134,6},{135,7},{1... | collective-permute-start | bytes 196616 | tf_op jit(solution)/shard_map/ppermute | solution.py:521
  172.4 0.7 collective-permute-start.21
  202.4 0.8 copy-start.6
  202.4 32.7 %copy-start.22 = (bf16[64,1024]{1,0:T(8,128)(2,1)}, bf16[64,1024]{1,0:T(8,128)(2,1)S(1)}, u32[]{:S(2)}) copy-start(bf16[64,1024]{1,0:T(8,128)(2,1)S(1)} %get-tuple-element.347.getz_ref) | copy-start | bytes 393220 | tf_op jit(solution)/shard_map/cond
  202.4 32.7 %copy-start.24 = (bf16[32,1024]{1,0:T(8,128)(2,1)}, bf16[32,1024]{1,0:T(8,128)(2,1)S(1)}, u32[]{:S(2)}) copy-start(bf16[32,1024]{1,0:T(8,128)(2,1)S(1)} %get-tuple-element.349.g_ref) | copy-start | bytes 196612 | tf_op jit(solution)/shard_map/cond
  202.4 32.7 %copy-start.15 = (bf16[1024,256]{1,0:T(8,128)(2,1)S(1)}, bf16[1024,256]{1,0:T(8,128)(2,1)}, u32[]{:S(2)}) copy-start(bf16[1024,256]{1,0:T(8,128)(2,1)} %get-tuple-element.355.wu_ref) | copy-start | bytes 1572868 | tf_op jit(solution)/shard_map/cond
  203.2 31.9 %copy-start.7 = (bf16[256,1024]{1,0:T(8,128)(2,1)S(1)}, bf16[256,1024]{1,0:T(8,128)(2,1)}, u32[]{:S(2)}) copy-start(bf16[256,1024]{1,0:T(8,128)(2,1)} %copy-done.6) | copy-start | bytes 1572868 | tf_op jit(solution)/shard_map/cond
  238.4 1.1 copy-start
  239.5 32.2 %all-to-all-start.7 = ((bf16[128,8,640]{2,1,0:T(8,128)(2,1)}), bf16[128,8,640]{2,1,0:T(8,128)(2,1)S(1)}, u32[]{:S(2)}, u32[]{:S(2)}) async-start(bf16[128,8,640]{2,1,0:T(8,128)(2,1)} %bitcast.116), calls=%async_computation.7 | async-start | bytes 2621440 | tf_op jit(solution)/shard_map/cond/branch_1_fun/all_to_all | solution.py:308
  273.7 0.6 copy-start.28
